TPU v7x, 128 devices: a whole 4x4x4 slice. The times are simulated.
128 devices in a mesh: segment: 8 (over x_hi, z), dp: 16 (over y, x_lo, core).
Axes of the slice: x: 4 (x_hi: 2, x_lo: 2; x = x_hi * 2 + x_lo), y: 4, z: 4, core: 2. Of those that a mesh axis runs over, the one named last changes fastest.
Arguments:
- images: bfloat16 [64, 16, 16, 256], P('dp'), may hold values from -6 to 6
- latent: float32 [64, 512], P('dp'), may hold values from -6 to 6
- weight: bfloat16 [8, 3, 3, 256, 256], P('segment'), may hold values from -0.125 to 0.125
- affine: float32 [8, 512, 256], P('segment'), may hold values from -0.25 to 0.25
- biases: float32 [8, 256], P('segment'), may hold values from -0.5 to 0.5
- cotangent: bfloat16 [64, 16, 16, 256], P('dp'), may hold values from -6 to 6
Outputs:
- grad_weight: float32 [8, 3, 3, 256, 256], P('segment')
- grad_affine: float32 [8, 512, 256], P('segment')
- grad_bias: float32 [8, 256], P('segment')
- grad_latent: float32 [64, 512], P('dp')
All inputs are finite; a program needn't handle non-finite values.
Results may differ from a plain program's by a relative error of at most 0.038.
Values may be sent and summed in bfloat16 or wider, within the bound.
No kernel may reach another device: no remote copies, remote signals or barrier semaphores. Data moves between devices by JAX's collectives and lax.ppermute only.
A program may use at most 64 MiB of HBM per device.

v0:
```python
import math

import jax
import jax.numpy as jnp
from jax import lax
from jax.sharding import PartitionSpec as P

MICRO = 1
MB = 4


GAIN = math.sqrt(2.0)


def from_behind(value, axis, steps):
    count = lax.axis_size(axis)
    leading, last = (max(0, -steps), min(count, count - steps))
    return lax.ppermute(value, axis, [(source, source + steps) for source in range(leading, last)])


def synth_layer(inputs, latent_rows, kernel, affine_map, offsets):
    styles = jnp.dot(latent_rows, affine_map, precision=lax.Precision.HIGHEST) + 1.0
    energy = jnp.sum(jnp.square(kernel.astype(jnp.float32)), axis=(0, 1))
    demodulate = lax.rsqrt(
        jnp.dot(styles * styles, energy, precision=lax.Precision.HIGHEST) + 1e-08
    )
    scaled = (inputs.astype(jnp.float32) * styles[:, None, None, :]).astype(jnp.bfloat16)
    convolved = lax.conv_general_dilated(
        scaled,
        kernel,
        (1, 1),
        "SAME",
        dimension_numbers=("NHWC", "HWIO", "NHWC"),
        preferred_element_type=jnp.float32,
    )
    hidden = convolved * demodulate[:, None, None, :] + offsets
    return (GAIN * hidden * (0.6 + 0.4 * jnp.tanh(hidden))).astype(jnp.bfloat16)


def body(images, latent, weight, affine, biases, cotangent):
    kernel = weight[0]
    affine_map = affine[0]
    offsets = biases[0]
    segments = lax.axis_size("segment")
    segment_index = lax.axis_index("segment")
    ticks = MB + segments - 1
    map_shape = (MICRO,) + images.shape[1:]

    def forward_tick(tick, carry):
        incoming, saved = carry
        slot = tick - segment_index
        is_valid = (slot >= 0) & (slot < MB)
        clipped = jnp.clip(slot, 0, MB - 1)
        first_input = lax.dynamic_slice_in_dim(images, clipped * MICRO, MICRO, 0)
        inputs = jnp.where(segment_index == 0, first_input, incoming)
        latent_rows = lax.dynamic_slice_in_dim(latent, clipped * MICRO, MICRO, 0)
        result = synth_layer(inputs, latent_rows, kernel, affine_map, offsets)
        previous = lax.dynamic_index_in_dim(saved, clipped, 0, keepdims=False)
        saved = lax.dynamic_update_index_in_dim(
            saved, jnp.where(is_valid, inputs, previous), clipped, 0
        )
        incoming = from_behind(result, "segment", 1)
        return (incoming, saved)

    saved_start = jnp.zeros((MB,) + map_shape, jnp.bfloat16)
    incoming_start = jnp.zeros(map_shape, jnp.bfloat16)
    unused, saved = lax.fori_loop(0, ticks, forward_tick, (incoming_start, saved_start))
    weight_start = jnp.zeros(kernel.shape, jnp.float32)

    def backward_tick(tick, carry):
        arriving, weight_acc, affine_acc, bias_acc, latent_acc = carry
        slot = tick - (segments - 1 - segment_index)
        is_valid = (slot >= 0) & (slot < MB)
        clipped = jnp.clip(slot, 0, MB - 1)
        last_input = lax.dynamic_slice_in_dim(cotangent, clipped * MICRO, MICRO, 0)
        upstream = jnp.where(segment_index == segments - 1, last_input, arriving)
        inputs = lax.dynamic_index_in_dim(saved, clipped, 0, keepdims=False)
        latent_rows = lax.dynamic_slice_in_dim(latent, clipped * MICRO, MICRO, 0)
        result, pull = jax.vjp(synth_layer, inputs, latent_rows, kernel, affine_map, offsets)
        grad_input, part_latent, part_weight, part_affine, part_bias = pull(upstream)
        weight_term = jnp.where(is_valid, part_weight.astype(jnp.float32), 0.0)
        weight_acc = weight_acc + weight_term
        affine_acc = affine_acc + jnp.where(is_valid, part_affine, 0.0)
        bias_acc = bias_acc + jnp.where(is_valid, part_bias, 0.0)
        latent_old = lax.dynamic_slice_in_dim(latent_acc, clipped * MICRO, MICRO, 0)
        latent_new = jnp.where(is_valid, latent_old + part_latent, latent_old)
        latent_acc = lax.dynamic_update_slice_in_dim(latent_acc, latent_new, clipped * MICRO, 0)
        arriving = from_behind(grad_input, "segment", -1)
        return (arriving, weight_acc, affine_acc, bias_acc, latent_acc)

    start = (
        jnp.zeros(map_shape, jnp.bfloat16),
        weight_start,
        jnp.zeros(affine_map.shape, jnp.float32),
        jnp.zeros(offsets.shape, jnp.float32),
        jnp.zeros(latent.shape, jnp.float32),
    )
    unused, weight_acc, affine_acc, bias_acc, latent_acc = lax.fori_loop(
        0, ticks, backward_tick, start
    )
    weight_total, affine_total, bias_total = lax.psum((weight_acc, affine_acc, bias_acc), "dp")
    latent_total = lax.psum(latent_acc, "segment")
    return (weight_total[None], affine_total[None], bias_total[None], latent_total)


def solution(mesh):
    placed = (
        P("dp", None, None, None),
        P("dp", None),
        P("segment", None, None, None, None),
        P("segment", None, None),
        P("segment", None),
        P("dp", None, None, None),
    )
    return jax.shard_map(
        body,
        mesh=mesh,
        in_specs=placed,
        out_specs=(
            P("segment", None, None, None, None),
            P("segment", None, None),
            P("segment", None),
            P("dp", None),
        ),
        check_vma=False,
    )
```

profile of v0, /device:TPU:1, one launch (start us, length us, event | category | flops | bytes accessed | tf_op | source)
XLA Modules:
  0.0 549.6 jit_solution(4825633269243587613)
XLA Ops:
  7.2 1.5 multiply_reduce_fusion
  8.8 128.5 %while.41 = (s32[]{:T(128)}, bf16[1,16,16,256]{3,1,2,0:T(8,128)(2,1)S(1)}, bf16[4,1,16,16,256]{4,2,3,1,0:T(8,128)(2,1)S(1)}, pred[]{:T(512)}, s32[]{:T(128)}, /*...) while((s32[]{:T(128)}, ...), condition=%wide.region_2.3_spmd, body=%wide.region_1.2_spmd.sunk | while | flops 438633216 | bytes 11044319 | solution.py:67
  8.9 1.4 fusion.119
  12.5 4.4 collective-permute-start
  17.0 2.0 collective-permute-done
  19.1 1.4 fusion.119
  22.7 4.1 collective-permute-start
  26.9 1.8 collective-permute-done
  28.8 1.4 fusion.119
  32.4 3.8 collective-permute-start
  36.3 1.8 collective-permute-done
  38.2 1.4 fusion.119
  41.8 3.8 collective-permute-start
  45.7 1.8 collective-permute-done
  47.6 1.4 fusion.119
  51.2 6.1 %collective-permute-start = (bf16[1,16,16,256]{3,1,2,0:T(8,128)(2,1)S(1)}, bf16[1,16,16,256]{3,1,2,0:T(8,128)(2,1)S(1)}, u32[]{:S(2)}, u32[]{:S(2)}) collective-permute-start(bf16[1,16,16,256]{3,1,2,0:T(8,128)(2,1)S(1)} %slice_bitcast_fusion.9), channel_id=1, source_target_pairs={{0,16},{16,32},{32,48},{48,64},{64,80},{80,96},{96,112},{1,17},{17... | collective-permute-start | bytes 393224 | tf_op jit(solution)/shard_map/while/body/eval_jaxpr/ppermute | solution.py:18
  57.5 1.8 collective-permute-done
  59.3 1.4 fusion.119
  62.9 7.4 %collective-permute-start = (bf16[1,16,16,256]{3,1,2,0:T(8,128)(2,1)S(1)}, bf16[1,16,16,256]{3,1,2,0:T(8,128)(2,1)S(1)}, u32[]{:S(2)}, u32[]{:S(2)}) collective-permute-start(bf16[1,16,16,256]{3,1,2,0:T(8,128)(2,1)S(1)} %slice_bitcast_fusion.9), channel_id=1, source_target_pairs={{0,16},{16,32},{32,48},{48,64},{64,80},{80,96},{96,112},{1,17},{17... | collective-permute-start | bytes 393224 | tf_op jit(solution)/shard_map/while/body/eval_jaxpr/ppermute | solution.py:18
  70.5 1.8 collective-permute-done
  72.3 1.4 fusion.119
  76.0 7.4 %collective-permute-start = (bf16[1,16,16,256]{3,1,2,0:T(8,128)(2,1)S(1)}, bf16[1,16,16,256]{3,1,2,0:T(8,128)(2,1)S(1)}, u32[]{:S(2)}, u32[]{:S(2)}) collective-permute-start(bf16[1,16,16,256]{3,1,2,0:T(8,128)(2,1)S(1)} %slice_bitcast_fusion.9), channel_id=1, source_target_pairs={{0,16},{16,32},{32,48},{48,64},{64,80},{80,96},{96,112},{1,17},{17... | collective-permute-start | bytes 393224 | tf_op jit(solution)/shard_map/while/body/eval_jaxpr/ppermute | solution.py:18
  83.5 1.8 collective-permute-done
  85.3 1.4 fusion.119
  88.9 7.4 %collective-permute-start = (bf16[1,16,16,256]{3,1,2,0:T(8,128)(2,1)S(1)}, bf16[1,16,16,256]{3,1,2,0:T(8,128)(2,1)S(1)}, u32[]{:S(2)}, u32[]{:S(2)}) collective-permute-start(bf16[1,16,16,256]{3,1,2,0:T(8,128)(2,1)S(1)} %slice_bitcast_fusion.9), channel_id=1, source_target_pairs={{0,16},{16,32},{32,48},{48,64},{64,80},{80,96},{96,112},{1,17},{17... | collective-permute-start | bytes 393224 | tf_op jit(solution)/shard_map/while/body/eval_jaxpr/ppermute | solution.py:18
  96.5 1.8 collective-permute-done
  98.4 1.4 fusion.119
  102.0 7.4 %collective-permute-start = (bf16[1,16,16,256]{3,1,2,0:T(8,128)(2,1)S(1)}, bf16[1,16,16,256]{3,1,2,0:T(8,128)(2,1)S(1)}, u32[]{:S(2)}, u32[]{:S(2)}) collective-permute-start(bf16[1,16,16,256]{3,1,2,0:T(8,128)(2,1)S(1)} %slice_bitcast_fusion.9), channel_id=1, source_target_pairs={{0,16},{16,32},{32,48},{48,64},{64,80},{80,96},{96,112},{1,17},{17... | collective-permute-start | bytes 393224 | tf_op jit(solution)/shard_map/while/body/eval_jaxpr/ppermute | solution.py:18
  109.5 1.8 collective-permute-done
  111.4 1.4 fusion.119
  115.0 7.4 %collective-permute-start = (bf16[1,16,16,256]{3,1,2,0:T(8,128)(2,1)S(1)}, bf16[1,16,16,256]{3,1,2,0:T(8,128)(2,1)S(1)}, u32[]{:S(2)}, u32[]{:S(2)}) collective-permute-start(bf16[1,16,16,256]{3,1,2,0:T(8,128)(2,1)S(1)} %slice_bitcast_fusion.9), channel_id=1, source_target_pairs={{0,16},{16,32},{32,48},{48,64},{64,80},{80,96},{96,112},{1,17},{17... | collective-permute-start | bytes 393224 | tf_op jit(solution)/shard_map/while/body/eval_jaxpr/ppermute | solution.py:18
  122.5 1.8 collective-permute-done
  124.4 1.4 fusion.119
  128.0 7.4 %collective-permute-start = (bf16[1,16,16,256]{3,1,2,0:T(8,128)(2,1)S(1)}, bf16[1,16,16,256]{3,1,2,0:T(8,128)(2,1)S(1)}, u32[]{:S(2)}, u32[]{:S(2)}) collective-permute-start(bf16[1,16,16,256]{3,1,2,0:T(8,128)(2,1)S(1)} %slice_bitcast_fusion.9), channel_id=1, source_target_pairs={{0,16},{16,32},{32,48},{48,64},{64,80},{80,96},{96,112},{1,17},{17... | collective-permute-start | bytes 393224 | tf_op jit(solution)/shard_map/while/body/eval_jaxpr/ppermute | solution.py:18
  135.5 1.8 collective-permute-done
  137.9 236.6 %while.42 = (s32[]{:T(128)}, bf16[1,16,16,256]{3,1,2,0:T(8,128)(2,1)S(1)}, f32[3,3,256,256]{3,2,1,0:T(8,128)}, f32[512,256]{1,0:T(8,128)S(1)}, f32[256]{0:T(256)...) while((s32[]{:T(128)}, ...), condition=%wide.region_8.9_spmd.clone, body=%wide.region_3.8_spmd.clone.sunk | while | flops 1162186496 | bytes 33856216 | solution.py:98
  143.9 1.4 multiply_convert_fusion.6
  152.2 1.3 dynamic_update_slice.24
  153.8 3.4 select_add_fusion.6
  163.6 1.4 multiply_convert_fusion.6
  172.0 1.3 dynamic_update_slice.24
  173.5 5.0 select_add_fusion.6
  185.0 1.4 multiply_convert_fusion.6
  194.9 5.0 select_add_fusion.6
  206.4 1.4 multiply_convert_fusion.6
  216.3 5.0 select_add_fusion.6
  227.8 1.4 multiply_convert_fusion.6
  237.7 5.0 select_add_fusion.6
  249.2 1.4 multiply_convert_fusion.6
  259.0 5.0 select_add_fusion.6
  270.6 1.4 multiply_convert_fusion.6
  280.4 5.0 select_add_fusion.6
  292.4 1.4 multiply_convert_fusion.6
  302.2 5.0 select_add_fusion.6
  314.4 1.4 multiply_convert_fusion.6
  324.3 5.0 select_add_fusion.6
  336.4 1.4 multiply_convert_fusion.6
  346.3 5.0 select_add_fusion.6
  358.4 1.4 multiply_convert_fusion.6
  368.3 5.0 select_add_fusion.6
  375.3 40.0 %psum.30 = f32[1,256]{1,0:T(1,128)} all-reduce(f32[1,256]{1,0:T(1,128)S(1)} %bitcast.237), channel_id=1, replica_groups=mesh['segment'=8,'dp'=16] {'dp'}, use_global_device_ids=true, to_apply=%region_11.12 | all-reduce | flops 256 | bytes 2048 | tf_op jit(solution)/shard_map/psum | solution.py:101
  415.4 43.1 %psum.31 = f32[4,512]{1,0:T(4,128)} all-reduce(f32[4,512]{1,0:T(4,128)S(1)} %copy-done.8), channel_id=1, replica_groups=mesh['segment'=8,'dp'=16] {'segment'}, use_global_device_ids=true, to_apply=%region_12.13 | all-reduce | flops 2048 | bytes 16384 | tf_op jit(solution)/shard_map/psum | solution.py:102
  458.5 80.2 %all-reduce.3.cloned.1.call-done = (f32[1,3,3,256,256]{4,3,2,1,0:T(8,128)}, f32[1,512,256]{2,1,0:T(8,128)}) async-done(((f32[1,3,3,256,256]{4,3,2,1,0:T(8,128)}, f32[1,512,256]{2,1,0:T(8,128)}), (f32[1,3,3,256,256]{4,3,2,1,0:T(8,128)}, f32[1,512,256]{2,1,0:T(8,128)})) %all-reduce.3.cloned.1.call-update) | async-done | bytes 2883600 | tf_op jit(solution)/shard_map/psum | solution.py:101
  538.7 3.3 copy.106
  (841 shorter events, 188.0 us)
Async XLA Ops:
  7.2 531.5 %all-reduce.3.cloned.1.call-start = ((), (), s32[]{:S(2)}) async-start(), calls=%async_computation | async-start | bytes 5767168 | tf_op jit(solution)/shard_map/psum | solution.py:101
  12.5 6.5 %collective-permute-start = (bf16[1,16,16,256]{3,1,2,0:T(8,128)(2,1)S(1)}, bf16[1,16,16,256]{3,1,2,0:T(8,128)(2,1)S(1)}, u32[]{:S(2)}, u32[]{:S(2)}) collective-permute-start(bf16[1,16,16,256]{3,1,2,0:T(8,128)(2,1)S(1)} %slice_bitcast_fusion.9), channel_id=1, source_target_pairs={{0,16},{16,32},{32,48},{48,64},{64,80},{80,96},{96,112},{1,17},{17... | collective-permute-start | bytes 393224 | tf_op jit(solution)/shard_map/while/body/eval_jaxpr/ppermute | solution.py:18
  22.7 6.0 %collective-permute-start = (bf16[1,16,16,256]{3,1,2,0:T(8,128)(2,1)S(1)}, bf16[1,16,16,256]{3,1,2,0:T(8,128)(2,1)S(1)}, u32[]{:S(2)}, u32[]{:S(2)}) collective-permute-start(bf16[1,16,16,256]{3,1,2,0:T(8,128)(2,1)S(1)} %slice_bitcast_fusion.9), channel_id=1, source_target_pairs={{0,16},{16,32},{32,48},{48,64},{64,80},{80,96},{96,112},{1,17},{17... | collective-permute-start | bytes 393224 | tf_op jit(solution)/shard_map/while/body/eval_jaxpr/ppermute | solution.py:18
  32.4 5.7 %collective-permute-start = (bf16[1,16,16,256]{3,1,2,0:T(8,128)(2,1)S(1)}, bf16[1,16,16,256]{3,1,2,0:T(8,128)(2,1)S(1)}, u32[]{:S(2)}, u32[]{:S(2)}) collective-permute-start(bf16[1,16,16,256]{3,1,2,0:T(8,128)(2,1)S(1)} %slice_bitcast_fusion.9), channel_id=1, source_target_pairs={{0,16},{16,32},{32,48},{48,64},{64,80},{80,96},{96,112},{1,17},{17... | collective-permute-start | bytes 393224 | tf_op jit(solution)/shard_map/while/body/eval_jaxpr/ppermute | solution.py:18
  41.8 5.7 %collective-permute-start = (bf16[1,16,16,256]{3,1,2,0:T(8,128)(2,1)S(1)}, bf16[1,16,16,256]{3,1,2,0:T(8,128)(2,1)S(1)}, u32[]{:S(2)}, u32[]{:S(2)}) collective-permute-start(bf16[1,16,16,256]{3,1,2,0:T(8,128)(2,1)S(1)} %slice_bitcast_fusion.9), channel_id=1, source_target_pairs={{0,16},{16,32},{32,48},{48,64},{64,80},{80,96},{96,112},{1,17},{17... | collective-permute-start | bytes 393224 | tf_op jit(solution)/shard_map/while/body/eval_jaxpr/ppermute | solution.py:18
  51.2 8.1 %collective-permute-start = (bf16[1,16,16,256]{3,1,2,0:T(8,128)(2,1)S(1)}, bf16[1,16,16,256]{3,1,2,0:T(8,128)(2,1)S(1)}, u32[]{:S(2)}, u32[]{:S(2)}) collective-permute-start(bf16[1,16,16,256]{3,1,2,0:T(8,128)(2,1)S(1)} %slice_bitcast_fusion.9), channel_id=1, source_target_pairs={{0,16},{16,32},{32,48},{48,64},{64,80},{80,96},{96,112},{1,17},{17... | collective-permute-start | bytes 393224 | tf_op jit(solution)/shard_map/while/body/eval_jaxpr/ppermute | solution.py:18
  62.9 9.3 %collective-permute-start = (bf16[1,16,16,256]{3,1,2,0:T(8,128)(2,1)S(1)}, bf16[1,16,16,256]{3,1,2,0:T(8,128)(2,1)S(1)}, u32[]{:S(2)}, u32[]{:S(2)}) collective-permute-start(bf16[1,16,16,256]{3,1,2,0:T(8,128)(2,1)S(1)} %slice_bitcast_fusion.9), channel_id=1, source_target_pairs={{0,16},{16,32},{32,48},{48,64},{64,80},{80,96},{96,112},{1,17},{17... | collective-permute-start | bytes 393224 | tf_op jit(solution)/shard_map/while/body/eval_jaxpr/ppermute | solution.py:18
  76.0 9.3 %collective-permute-start = (bf16[1,16,16,256]{3,1,2,0:T(8,128)(2,1)S(1)}, bf16[1,16,16,256]{3,1,2,0:T(8,128)(2,1)S(1)}, u32[]{:S(2)}, u32[]{:S(2)}) collective-permute-start(bf16[1,16,16,256]{3,1,2,0:T(8,128)(2,1)S(1)} %slice_bitcast_fusion.9), channel_id=1, source_target_pairs={{0,16},{16,32},{32,48},{48,64},{64,80},{80,96},{96,112},{1,17},{17... | collective-permute-start | bytes 393224 | tf_op jit(solution)/shard_map/while/body/eval_jaxpr/ppermute | solution.py:18
  88.9 9.3 %collective-permute-start = (bf16[1,16,16,256]{3,1,2,0:T(8,128)(2,1)S(1)}, bf16[1,16,16,256]{3,1,2,0:T(8,128)(2,1)S(1)}, u32[]{:S(2)}, u32[]{:S(2)}) collective-permute-start(bf16[1,16,16,256]{3,1,2,0:T(8,128)(2,1)S(1)} %slice_bitcast_fusion.9), channel_id=1, source_target_pairs={{0,16},{16,32},{32,48},{48,64},{64,80},{80,96},{96,112},{1,17},{17... | collective-permute-start | bytes 393224 | tf_op jit(solution)/shard_map/while/body/eval_jaxpr/ppermute | solution.py:18
  102.0 9.3 %collective-permute-start = (bf16[1,16,16,256]{3,1,2,0:T(8,128)(2,1)S(1)}, bf16[1,16,16,256]{3,1,2,0:T(8,128)(2,1)S(1)}, u32[]{:S(2)}, u32[]{:S(2)}) collective-permute-start(bf16[1,16,16,256]{3,1,2,0:T(8,128)(2,1)S(1)} %slice_bitcast_fusion.9), channel_id=1, source_target_pairs={{0,16},{16,32},{32,48},{48,64},{64,80},{80,96},{96,112},{1,17},{17... | collective-permute-start | bytes 393224 | tf_op jit(solution)/shard_map/while/body/eval_jaxpr/ppermute | solution.py:18
  115.0 9.3 %collective-permute-start = (bf16[1,16,16,256]{3,1,2,0:T(8,128)(2,1)S(1)}, bf16[1,16,16,256]{3,1,2,0:T(8,128)(2,1)S(1)}, u32[]{:S(2)}, u32[]{:S(2)}) collective-permute-start(bf16[1,16,16,256]{3,1,2,0:T(8,128)(2,1)S(1)} %slice_bitcast_fusion.9), channel_id=1, source_target_pairs={{0,16},{16,32},{32,48},{48,64},{64,80},{80,96},{96,112},{1,17},{17... | collective-permute-start | bytes 393224 | tf_op jit(solution)/shard_map/while/body/eval_jaxpr/ppermute | solution.py:18
  128.0 9.3 %collective-permute-start = (bf16[1,16,16,256]{3,1,2,0:T(8,128)(2,1)S(1)}, bf16[1,16,16,256]{3,1,2,0:T(8,128)(2,1)S(1)}, u32[]{:S(2)}, u32[]{:S(2)}) collective-permute-start(bf16[1,16,16,256]{3,1,2,0:T(8,128)(2,1)S(1)} %slice_bitcast_fusion.9), channel_id=1, source_target_pairs={{0,16},{16,32},{32,48},{48,64},{64,80},{80,96},{96,112},{1,17},{17... | collective-permute-start | bytes 393224 | tf_op jit(solution)/shard_map/while/body/eval_jaxpr/ppermute | solution.py:18
  143.9 7.1 %copy-start = (f32[512,256]{1,0:T(8,128)S(1)}, f32[512,256]{1,0:T(8,128)}, u32[]{:S(2)}) copy-start(f32[512,256]{1,0:T(8,128)} %get-tuple-element.981) | copy-start | bytes 1572868 | tf_op jit(solution)/shard_map/while
  146.0 11.1 %collective-permute-start.1 = (bf16[1,16,16,256]{3,1,2,0:T(8,128)(2,1)}, bf16[1,16,16,256]{3,1,2,0:T(8,128)(2,1)S(1)}, u32[]{:S(2)}, u32[]{:S(2)}) collective-permute-start(bf16[1,16,16,256]{3,1,2,0:T(8,128)(2,1)} %slice_bitcast_fusion.10), channel_id=1, source_target_pairs={{16,0},{32,16},{48,32},{64,48},{80,64},{96,80},{112,96},{17,1},{33... | collective-permute-start | bytes 393224 | tf_op jit(solution)/shard_map/while/body/eval_jaxpr/ppermute | solution.py:18
  149.0 4.7 copy-start.4
  163.6 7.1 %copy-start = (f32[512,256]{1,0:T(8,128)S(1)}, f32[512,256]{1,0:T(8,128)}, u32[]{:S(2)}) copy-start(f32[512,256]{1,0:T(8,128)} %get-tuple-element.981) | copy-start | bytes 1572868 | tf_op jit(solution)/shard_map/while
  165.7 12.8 %collective-permute-start.1 = (bf16[1,16,16,256]{3,1,2,0:T(8,128)(2,1)}, bf16[1,16,16,256]{3,1,2,0:T(8,128)(2,1)S(1)}, u32[]{:S(2)}, u32[]{:S(2)}) collective-permute-start(bf16[1,16,16,256]{3,1,2,0:T(8,128)(2,1)} %slice_bitcast_fusion.10), channel_id=1, source_target_pairs={{16,0},{32,16},{48,32},{64,48},{80,64},{96,80},{112,96},{17,1},{33... | collective-permute-start | bytes 393224 | tf_op jit(solution)/shard_map/while/body/eval_jaxpr/ppermute | solution.py:18
  168.8 4.7 copy-start.4
  173.5 5.0 copy-start.7
  173.5 5.0 copy-start.9
  185.0 7.1 %copy-start = (f32[512,256]{1,0:T(8,128)S(1)}, f32[512,256]{1,0:T(8,128)}, u32[]{:S(2)}) copy-start(f32[512,256]{1,0:T(8,128)} %get-tuple-element.981) | copy-start | bytes 1572868 | tf_op jit(solution)/shard_map/while
  187.1 12.8 %collective-permute-start.1 = (bf16[1,16,16,256]{3,1,2,0:T(8,128)(2,1)}, bf16[1,16,16,256]{3,1,2,0:T(8,128)(2,1)S(1)}, u32[]{:S(2)}, u32[]{:S(2)}) collective-permute-start(bf16[1,16,16,256]{3,1,2,0:T(8,128)(2,1)} %slice_bitcast_fusion.10), channel_id=1, source_target_pairs={{16,0},{32,16},{48,32},{64,48},{80,64},{96,80},{112,96},{17,1},{33... | collective-permute-start | bytes 393224 | tf_op jit(solution)/shard_map/while/body/eval_jaxpr/ppermute | solution.py:18
  190.2 4.7 copy-start.4
  194.9 5.0 copy-start.7
  194.9 5.0 copy-start.9
  206.4 7.1 %copy-start = (f32[512,256]{1,0:T(8,128)S(1)}, f32[512,256]{1,0:T(8,128)}, u32[]{:S(2)}) copy-start(f32[512,256]{1,0:T(8,128)} %get-tuple-element.981) | copy-start | bytes 1572868 | tf_op jit(solution)/shard_map/while
  208.5 12.8 %collective-permute-start.1 = (bf16[1,16,16,256]{3,1,2,0:T(8,128)(2,1)}, bf16[1,16,16,256]{3,1,2,0:T(8,128)(2,1)S(1)}, u32[]{:S(2)}, u32[]{:S(2)}) collective-permute-start(bf16[1,16,16,256]{3,1,2,0:T(8,128)(2,1)} %slice_bitcast_fusion.10), channel_id=1, source_target_pairs={{16,0},{32,16},{48,32},{64,48},{80,64},{96,80},{112,96},{17,1},{33... | collective-permute-start | bytes 393224 | tf_op jit(solution)/shard_map/while/body/eval_jaxpr/ppermute | solution.py:18
  211.5 4.7 copy-start.4
  216.2 5.0 copy-start.7
  216.3 5.0 copy-start.9
  227.8 7.1 %copy-start = (f32[512,256]{1,0:T(8,128)S(1)}, f32[512,256]{1,0:T(8,128)}, u32[]{:S(2)}) copy-start(f32[512,256]{1,0:T(8,128)} %get-tuple-element.981) | copy-start | bytes 1572868 | tf_op jit(solution)/shard_map/while
  229.9 12.8 %collective-permute-start.1 = (bf16[1,16,16,256]{3,1,2,0:T(8,128)(2,1)}, bf16[1,16,16,256]{3,1,2,0:T(8,128)(2,1)S(1)}, u32[]{:S(2)}, u32[]{:S(2)}) collective-permute-start(bf16[1,16,16,256]{3,1,2,0:T(8,128)(2,1)} %slice_bitcast_fusion.10), channel_id=1, source_target_pairs={{16,0},{32,16},{48,32},{64,48},{80,64},{96,80},{112,96},{17,1},{33... | collective-permute-start | bytes 393224 | tf_op jit(solution)/shard_map/while/body/eval_jaxpr/ppermute | solution.py:18
  232.9 4.7 copy-start.4
  237.6 5.0 copy-start.7
  237.6 5.0 copy-start.9
  249.2 7.1 %copy-start = (f32[512,256]{1,0:T(8,128)S(1)}, f32[512,256]{1,0:T(8,128)}, u32[]{:S(2)}) copy-start(f32[512,256]{1,0:T(8,128)} %get-tuple-element.981) | copy-start | bytes 1572868 | tf_op jit(solution)/shard_map/while
  251.3 13.1 %collective-permute-start.1 = (bf16[1,16,16,256]{3,1,2,0:T(8,128)(2,1)}, bf16[1,16,16,256]{3,1,2,0:T(8,128)(2,1)S(1)}, u32[]{:S(2)}, u32[]{:S(2)}) collective-permute-start(bf16[1,16,16,256]{3,1,2,0:T(8,128)(2,1)} %slice_bitcast_fusion.10), channel_id=1, source_target_pairs={{16,0},{32,16},{48,32},{64,48},{80,64},{96,80},{112,96},{17,1},{33... | collective-permute-start | bytes 393224 | tf_op jit(solution)/shard_map/while/body/eval_jaxpr/ppermute | solution.py:18
  254.3 4.7 copy-start.4
  259.0 5.0 copy-start.7
  259.0 5.0 copy-start.9
  270.5 7.1 %copy-start = (f32[512,256]{1,0:T(8,128)S(1)}, f32[512,256]{1,0:T(8,128)}, u32[]{:S(2)}) copy-start(f32[512,256]{1,0:T(8,128)} %get-tuple-element.981) | copy-start | bytes 1572868 | tf_op jit(solution)/shard_map/while
  272.7 13.8 %collective-permute-start.1 = (bf16[1,16,16,256]{3,1,2,0:T(8,128)(2,1)}, bf16[1,16,16,256]{3,1,2,0:T(8,128)(2,1)S(1)}, u32[]{:S(2)}, u32[]{:S(2)}) collective-permute-start(bf16[1,16,16,256]{3,1,2,0:T(8,128)(2,1)} %slice_bitcast_fusion.10), channel_id=1, source_target_pairs={{16,0},{32,16},{48,32},{64,48},{80,64},{96,80},{112,96},{17,1},{33... | collective-permute-start | bytes 393224 | tf_op jit(solution)/shard_map/while/body/eval_jaxpr/ppermute | solution.py:18
  275.7 4.7 copy-start.4
  280.4 5.0 copy-start.7
  280.4 5.0 copy-start.9
  292.4 7.1 %copy-start = (f32[512,256]{1,0:T(8,128)S(1)}, f32[512,256]{1,0:T(8,128)}, u32[]{:S(2)}) copy-start(f32[512,256]{1,0:T(8,128)} %get-tuple-element.981) | copy-start | bytes 1572868 | tf_op jit(solution)/shard_map/while
  294.5 14.0 %collective-permute-start.1 = (bf16[1,16,16,256]{3,1,2,0:T(8,128)(2,1)}, bf16[1,16,16,256]{3,1,2,0:T(8,128)(2,1)S(1)}, u32[]{:S(2)}, u32[]{:S(2)}) collective-permute-start(bf16[1,16,16,256]{3,1,2,0:T(8,128)(2,1)} %slice_bitcast_fusion.10), channel_id=1, source_target_pairs={{16,0},{32,16},{48,32},{64,48},{80,64},{96,80},{112,96},{17,1},{33... | collective-permute-start | bytes 393224 | tf_op jit(solution)/shard_map/while/body/eval_jaxpr/ppermute | solution.py:18
  297.5 4.7 copy-start.4
  302.2 5.0 copy-start.7
  302.2 5.0 copy-start.9
  314.4 7.1 %copy-start = (f32[512,256]{1,0:T(8,128)S(1)}, f32[512,256]{1,0:T(8,128)}, u32[]{:S(2)}) copy-start(f32[512,256]{1,0:T(8,128)} %get-tuple-element.981) | copy-start | bytes 1572868 | tf_op jit(solution)/shard_map/while
  316.5 14.0 %collective-permute-start.1 = (bf16[1,16,16,256]{3,1,2,0:T(8,128)(2,1)}, bf16[1,16,16,256]{3,1,2,0:T(8,128)(2,1)S(1)}, u32[]{:S(2)}, u32[]{:S(2)}) collective-permute-start(bf16[1,16,16,256]{3,1,2,0:T(8,128)(2,1)} %slice_bitcast_fusion.10), channel_id=1, source_target_pairs={{16,0},{32,16},{48,32},{64,48},{80,64},{96,80},{112,96},{17,1},{33... | collective-permute-start | bytes 393224 | tf_op jit(solution)/shard_map/while/body/eval_jaxpr/ppermute | solution.py:18
  324.2 5.0 copy-start.7
  324.2 5.0 copy-start.9
  336.4 7.1 %copy-start = (f32[512,256]{1,0:T(8,128)S(1)}, f32[512,256]{1,0:T(8,128)}, u32[]{:S(2)}) copy-start(f32[512,256]{1,0:T(8,128)} %get-tuple-element.981) | copy-start | bytes 1572868 | tf_op jit(solution)/shard_map/while
  338.5 14.0 %collective-permute-start.1 = (bf16[1,16,16,256]{3,1,2,0:T(8,128)(2,1)}, bf16[1,16,16,256]{3,1,2,0:T(8,128)(2,1)S(1)}, u32[]{:S(2)}, u32[]{:S(2)}) collective-permute-start(bf16[1,16,16,256]{3,1,2,0:T(8,128)(2,1)} %slice_bitcast_fusion.10), channel_id=1, source_target_pairs={{16,0},{32,16},{48,32},{64,48},{80,64},{96,80},{112,96},{17,1},{33... | collective-permute-start | bytes 393224 | tf_op jit(solution)/shard_map/while/body/eval_jaxpr/ppermute | solution.py:18
  341.6 4.7 copy-start.4
  346.3 5.0 copy-start.7
  346.3 5.0 copy-start.9
  358.4 7.1 %copy-start = (f32[512,256]{1,0:T(8,128)S(1)}, f32[512,256]{1,0:T(8,128)}, u32[]{:S(2)}) copy-start(f32[512,256]{1,0:T(8,128)} %get-tuple-element.981) | copy-start | bytes 1572868 | tf_op jit(solution)/shard_map/while
  360.5 14.0 %collective-permute-start.1 = (bf16[1,16,16,256]{3,1,2,0:T(8,128)(2,1)}, bf16[1,16,16,256]{3,1,2,0:T(8,128)(2,1)S(1)}, u32[]{:S(2)}, u32[]{:S(2)}) collective-permute-start(bf16[1,16,16,256]{3,1,2,0:T(8,128)(2,1)} %slice_bitcast_fusion.10), channel_id=1, source_target_pairs={{16,0},{32,16},{48,32},{64,48},{80,64},{96,80},{112,96},{17,1},{33... | collective-permute-start | bytes 393224 | tf_op jit(solution)/shard_map/while/body/eval_jaxpr/ppermute | solution.py:18
  368.3 5.0 copy-start.7
  368.3 5.0 copy-start.9
  374.5 40.9 %copy-start.8 = (f32[4,512]{1,0:T(4,128)S(1)}, f32[4,512]{1,0:T(4,128)}, u32[]{:S(2)}) copy-start(f32[4,512]{1,0:T(4,128)} %get-tuple-element.551) | copy-start | bytes 24580
  (95 other events, 284.5 us)
Sparse Core Ops, SparseCore 0:
  375.4 163.1 all-reduce.2
where the time goes:
time: 554 us; the launch traced here: 550 us
  matrix products  134 us (24%)
  waiting for transfers between devices  106 us (19%)
  local copies, waits for them, and re-layouts  84.1 us (15%)
  blocking collectives  83.1 us (15%)
  starting transfers between devices  80.7 us (15%)
  other arithmetic  41.8 us (8%)
  between operations  14.1 us (3%)
    conv_general_dilated x44, matrix products, synth_layer(): lax.conv_general_dilated(scaled, kernel, (1, 1), 'SAME', dimension_number...  83.8 us
    ppermute x22, starting transfers between devices, from_behind(): lax.ppermute(value, axis, [(source, source + steps) for source in range(l...  80.7 us
    psum x1, waiting for transfers between devices, body(): lax.psum((weight_acc, affine_acc, bias_acc), 'dp')  80.2 us
    dot_general x33, matrix products, synth_layer(): jnp.dot(latent_rows, affine_map, precision=lax.Precision.HIGHEST) + 1.0  43.4 us
    psum x1, blocking collectives, body(): latent_total = lax.psum(latent_acc, 'segment')  43.1 us
    psum x1, blocking collectives, body(): lax.psum((weight_acc, affine_acc, bias_acc), 'dp')  40 us
    ppermute x22, waiting for transfers between devices, from_behind(): lax.ppermute(value, axis, [(source, source + steps) for source in range(l...  26 us
    dynamic_update_slice x11, local copies, waits for them, and re-layouts, backward_tick(): lax.dynamic_update_slice_in_dim(latent_acc, latent_new, clipped * MICRO, 0)  14.7 us
  transfers between devices with their start and end apart: 23, of which 18 were waited for; matrix products, arithmetic and copies ran while one was open for 23% of the time, Pallas kernels for 0%

commit v1 on v0

v1 whole, which is shorter than its diff:
```python
import functools
import math

import jax
import jax.numpy as jnp
from jax import lax
from jax.experimental import pallas as pl
from jax.experimental.pallas import tpu as pltpu
from jax.sharding import PartitionSpec as P

GAIN = math.sqrt(2.0)
EPS = 1e-08
BF = jnp.bfloat16
F32 = jnp.float32
C = 256
PX = 256
TAPS = 9
ROWS = TAPS * C
HALF = ROWS // 2
STAT = 16
DEPTH = 4
ROW = 16
PAD = PX + 2 * ROW
HI = lax.Precision.HIGHEST


def any_spec():
    return pl.BlockSpec(memory_space=pl.ANY)


def vmem_spec():
    return pl.BlockSpec(memory_space=pltpu.VMEM)


def params():
    return pltpu.CompilerParams(vmem_limit_bytes=56 << 20)


def place():
    seg = lax.axis_index("segment")
    return seg // DEPTH, seg % DEPTH, lax.axis_index("dp") % 2


def split3(value):
    hi = value.astype(BF).astype(F32)
    rest = value - hi
    mid = rest.astype(BF).astype(F32)
    return hi, mid, rest - mid


def pack_rows(values):
    row = lax.broadcasted_iota(jnp.int32, (STAT, C), 0)
    out = jnp.zeros((STAT, C), F32)
    k = 0
    for value in values:
        for part in split3(value):
            out = jnp.where(row == k, jnp.broadcast_to(part, (STAT, C)), out)
            k += 1
    return out.astype(BF)


def unpack_rows(tile):
    t = tile.astype(F32)
    return [t[3 * k : 3 * k + 1] + t[3 * k + 1 : 3 * k + 2] + t[3 * k + 2 : 3 * k + 3] for k in range(3)]


def stack_rows(rows):
    index = lax.broadcasted_iota(jnp.int32, (8, C), 0)
    out = jnp.zeros((8, C), F32)
    for k, row in enumerate(rows):
        out = jnp.where(index == k, jnp.broadcast_to(row, (8, C)), out)
    return out


def prepare_kernel(latent_ref, affine_ref, w_ref, bias_ref, w_any, send_ref, styles_ref, demod_ref, energy_ref, tile_ref, sem):
    _, _, core = place()
    copies = [
        pltpu.make_async_copy(
            w_any.at[pl.ds(pl.multiple_of(core * HALF, HALF), HALF)], send_ref.at[k, pl.ds(0, HALF)], sem.at[k]
        )
        for k in range(DEPTH)
    ]
    for copy in copies:
        copy.start()
    styles = jnp.dot(latent_ref[...], affine_ref[...], precision=HI, preferred_element_type=F32) + 1.0
    energy = jnp.zeros((C, C), F32)
    for tap in range(TAPS):
        part = w_ref[tap * C : (tap + 1) * C, :].astype(F32)
        energy += part * part
    energy_ref[...] = energy
    demod = lax.rsqrt(jnp.dot(styles * styles, energy, precision=HI, preferred_element_type=F32) + EPS)
    styles_ref[...] = styles
    demod_ref[...] = demod
    for k in range(DEPTH):
        tile_ref[k] = pack_rows([styles[k : k + 1], demod[k : k + 1], bias_ref[...]])
    stats = [
        pltpu.make_async_copy(tile_ref.at[k], send_ref.at[k, pl.ds(HALF, STAT)], sem.at[DEPTH + k])
        for k in range(DEPTH)
    ]
    for copy in stats:
        copy.start()
    for copy in copies + stats:
        copy.wait()


def prepare(latent8, affine, w, bias):
    return pl.pallas_call(
        prepare_kernel,
        out_shape=(
            jax.ShapeDtypeStruct((DEPTH, HALF + STAT, C), BF),
            jax.ShapeDtypeStruct((8, C), F32),
            jax.ShapeDtypeStruct((8, C), F32),
            jax.ShapeDtypeStruct((C, C), F32),
        ),
        in_specs=[vmem_spec()] * 4 + [any_spec()],
        out_specs=(any_spec(), vmem_spec(), vmem_spec(), vmem_spec()),
        scratch_shapes=[pltpu.VMEM((DEPTH, STAT, C), BF), pltpu.SemaphoreType.DMA((2 * DEPTH,))],
        compiler_params=params(),
        name="prepare",
    )(latent8, affine, w, bias, w)


def weight_copies(a_any, b_any, w_buf, stat_buf, sem):
    _, _, core = place()
    mine = pl.ds(pl.multiple_of(core * HALF, HALF), HALF)
    other = pl.ds(pl.multiple_of((1 - core) * HALF, HALF), HALF)
    return [
        (
            pltpu.make_async_copy(a_any.at[l, pl.ds(HALF, STAT)], stat_buf.at[l], sem.at[0, l]),
            pltpu.make_async_copy(a_any.at[l, pl.ds(0, HALF)], w_buf.at[l, mine], sem.at[1, l]),
            pltpu.make_async_copy(b_any.at[l, pl.ds(0, HALF)], w_buf.at[l, other], sem.at[2, l]),
        )
        for l in range(DEPTH)
    ]


def clear_pads(pad_ref):
    for k in range(3):
        pad_ref[k, 0:ROW, :] = jnp.zeros((ROW, C), BF)
        pad_ref[k, ROW + PX : PAD, :] = jnp.zeros((ROW, C), BF)


def spread(pad_ref, value):
    column = lax.broadcasted_iota(jnp.int32, (PX, C), 0) % ROW
    pad_ref[1, ROW : ROW + PX, :] = value.astype(BF)
    pad_ref[0, ROW : ROW + PX, :] = jnp.where(column == 0, 0.0, pltpu.roll(value, 1, 0)).astype(BF)
    pad_ref[2, ROW : ROW + PX, :] = jnp.where(column == ROW - 1, 0.0, pltpu.roll(value, PX - 1, 0)).astype(BF)


def forward_layer(x, l, w_buf, stat, pad_ref):
    styles, demod, bias = stat
    scaled = (x.astype(F32) * styles).astype(BF).astype(F32)
    spread(pad_ref, scaled)
    conv = None
    for ky in range(3):
        lhs = jnp.concatenate([pad_ref[kx, ky * ROW : ky * ROW + PX, :] for kx in range(3)], axis=1)
        part = jnp.dot(lhs, w_buf[l, ky * 3 * C : (ky + 1) * 3 * C, :], preferred_element_type=F32)
        conv = part if conv is None else conv + part
    return conv


def activate(conv, stat):
    _, demod, bias = stat
    hidden = conv * demod + bias
    return (GAIN * hidden * (0.6 + 0.4 * jnp.tanh(hidden))).astype(BF)


def backward_layer(upstream, x, conv, l, w_buf, stat, pad_ref, send_ref):
    styles, demod, bias = stat
    hidden = conv * demod + bias
    t = jnp.tanh(hidden)
    dh = upstream.astype(F32) * (GAIN * (0.6 + 0.4 * t + 0.4 * hidden * (1.0 - t * t)))
    grad_bias = jnp.sum(dh, axis=0, keepdims=True)
    grad_demod = jnp.sum(dh * conv, axis=0, keepdims=True)
    grad_conv = (dh * demod).astype(BF).astype(F32)
    spread(pad_ref, grad_conv)
    send_ref[l, PX : 2 * PX, :] = pad_ref[1, ROW : ROW + PX, :]
    total = None
    for ky in range(3):
        for kx in range(3):
            lhs = pad_ref[2 - kx, (2 - ky) * ROW : (2 - ky) * ROW + PX, :]
            tap = ky * 3 + kx
            part = lax.dot_general(
                lhs, w_buf[l, tap * C : (tap + 1) * C, :], (((1,), (1,)), ((), ())), preferred_element_type=F32
            )
            total = part if total is None else total + part
    grad_scaled = total.astype(BF).astype(F32)
    xf = x.astype(F32)
    grad_styles = jnp.sum(grad_scaled * xf, axis=0, keepdims=True)
    send_ref[l, 0:PX, :] = (xf * styles).astype(BF)
    send_ref[l, 2 * PX : 2 * PX + STAT, :] = pack_rows([grad_styles, grad_demod, grad_bias])
    return (grad_scaled * styles).astype(BF)


def first_kernel(images_any, a_any, b_any, out_ref, w_buf, stat_buf, x_buf, pad_ref, sem, x_sem):
    _, z, _ = place()
    x_copy = pltpu.make_async_copy(images_any.at[z], x_buf, x_sem)
    x_copy.start()
    copies = weight_copies(a_any, b_any, w_buf, stat_buf, sem)
    for group in copies:
        for copy in group:
            copy.start()
    clear_pads(pad_ref)
    x_copy.wait()
    x = x_buf[...]
    for l in range(DEPTH):
        for copy in copies[l]:
            copy.wait()
        stat = unpack_rows(stat_buf[l])
        x = activate(forward_layer(x, l, w_buf, stat, pad_ref), stat)
    out_ref[...] = x


def middle_kernel(
    images_any, cot_any, recv_ref, a_any, b_any, dx_ref, xs_ref, conv_ref, send_ref,
    w_buf, stat_buf, x_buf, u_buf, pad_ref, sem, x_sem,
):
    half, z, _ = place()
    x_copy = pltpu.make_async_copy(images_any.at[z], x_buf, x_sem.at[0])
    u_copy = pltpu.make_async_copy(cot_any.at[z], u_buf, x_sem.at[1])
    x_copy.start()
    copies = weight_copies(a_any, b_any, w_buf, stat_buf, sem)
    for group in copies:
        for copy in group:
            copy.start()
    u_copy.start()
    clear_pads(pad_ref)
    x_copy.wait()
    x = jnp.where(half == 1, recv_ref[...], x_buf[...])
    stats = []
    for l in range(DEPTH):
        for copy in copies[l]:
            copy.wait()
        stats.append(unpack_rows(stat_buf[l]))
        xs_ref[l] = x
        conv = forward_layer(x, l, w_buf, stats[l], pad_ref)
        conv_ref[l] = conv
        if l < DEPTH - 1:
            x = activate(conv, stats[l])
    u_copy.wait()
    upstream = u_buf[...]
    for l in reversed(range(DEPTH)):
        upstream = backward_layer(upstream, xs_ref[l], conv_ref[l], l, w_buf, stats[l], pad_ref, send_ref)
    dx_ref[...] = upstream


def last_kernel(
    cot_any, recv_ref, xs_any, conv_any, a_any, b_any, send_ref,
    w_buf, stat_buf, xs_buf, conv_buf, u_buf, pad_ref, sem, s_sem, u_sem,
):
    half, z, _ = place()
    u_copy = pltpu.make_async_copy(cot_any.at[z], u_buf, u_sem)
    u_copy.start()
    copies = weight_copies(a_any, b_any, w_buf, stat_buf, sem)
    saves = [
        (
            pltpu.make_async_copy(xs_any.at[l], xs_buf.at[l], s_sem.at[0, l]),
            pltpu.make_async_copy(conv_any.at[l], conv_buf.at[l], s_sem.at[1, l]),
        )
        for l in range(DEPTH)
    ]
    for l in reversed(range(DEPTH)):
        for copy in saves[l] + copies[l]:
            copy.start()
    clear_pads(pad_ref)
    u_copy.wait()
    upstream = jnp.where(half == 1, u_buf[...], recv_ref[...])
    for l in reversed(range(DEPTH)):
        for copy in saves[l] + copies[l]:
            copy.wait()
        stat = unpack_rows(stat_buf[l])
        upstream = backward_layer(upstream, xs_buf[l], conv_buf[l], l, w_buf, stat, pad_ref, send_ref)


def weight_scratch():
    return [pltpu.VMEM((DEPTH, ROWS, C), BF), pltpu.VMEM((DEPTH, STAT, C), BF)]


MAP = jax.ShapeDtypeStruct((PX, C), BF)
SENT = jax.ShapeDtypeStruct((DEPTH, 2 * PX + STAT, C), BF)


def first(images, a, b):
    return pl.pallas_call(
        first_kernel,
        out_shape=MAP,
        in_specs=[any_spec()] * 3,
        out_specs=vmem_spec(),
        scratch_shapes=weight_scratch()
        + [
            pltpu.VMEM((PX, C), BF),
            pltpu.VMEM((3, PAD, C), BF),
            pltpu.SemaphoreType.DMA((3, DEPTH)),
            pltpu.SemaphoreType.DMA,
        ],
        compiler_params=params(),
        name="first",
    )(images, a, b)


def middle(images, cot, recv, a, b):
    return pl.pallas_call(
        middle_kernel,
        out_shape=(
            MAP,
            jax.ShapeDtypeStruct((DEPTH, PX, C), BF),
            jax.ShapeDtypeStruct((DEPTH, PX, C), F32),
            SENT,
        ),
        in_specs=[any_spec(), any_spec(), vmem_spec(), any_spec(), any_spec()],
        out_specs=(vmem_spec(),) * 4,
        scratch_shapes=weight_scratch()
        + [
            pltpu.VMEM((PX, C), BF),
            pltpu.VMEM((PX, C), BF),
            pltpu.VMEM((3, PAD, C), BF),
            pltpu.SemaphoreType.DMA((3, DEPTH)),
            pltpu.SemaphoreType.DMA((2,)),
        ],
        compiler_params=params(),
        name="middle",
    )(images, cot, recv, a, b)


def last(cot, recv, xs, conv, a, b):
    return pl.pallas_call(
        last_kernel,
        out_shape=SENT,
        in_specs=[any_spec(), vmem_spec(), any_spec(), any_spec(), any_spec(), any_spec()],
        out_specs=vmem_spec(),
        scratch_shapes=weight_scratch()
        + [
            pltpu.VMEM((DEPTH, PX, C), BF),
            pltpu.VMEM((DEPTH, PX, C), F32),
            pltpu.VMEM((PX, C), BF),
            pltpu.VMEM((3, PAD, C), BF),
            pltpu.SemaphoreType.DMA((3, DEPTH)),
            pltpu.SemaphoreType.DMA((2, DEPTH)),
            pltpu.SemaphoreType.DMA,
        ],
        compiler_params=params(),
        name="last",
    )(cot, recv, xs, conv, a, b)


def gradient_kernel(
    r_ref, w_ref, styles_ref, demod_ref, energy_ref, affine_ref,
    keep_ref, give_ref, rows_ref, latent_ref, flip_ref, pad_ref, total_ref,
):
    _, _, core = place()
    parts = [unpack_rows(r_ref[n, 2 * PX : 2 * PX + STAT, :]) for n in range(DEPTH)]
    styles = styles_ref[...]
    demod = demod_ref[...]
    grad_sum = stack_rows([p[1] for p in parts]) * (-0.5) * demod * demod * demod
    squares = styles * styles
    grad_squares = lax.dot_general(
        grad_sum, energy_ref[...], (((1,), (1,)), ((), ())), precision=HI, preferred_element_type=F32
    )
    grad_styles = stack_rows([p[0] for p in parts]) + 2.0 * styles * grad_squares
    index = lax.broadcasted_iota(jnp.int32, (8, C), 0)
    grad_bias = parts[0][2] + parts[1][2] + parts[2][2] + parts[3][2]
    rows_ref[...] = jnp.where(
        index < DEPTH, grad_styles, jnp.where(index == DEPTH, jnp.broadcast_to(grad_bias, (8, C)), 0.0)
    )
    latent_ref[...] = lax.dot_general(
        grad_styles, affine_ref[...], (((1,), (1,)), ((), ())), precision=HI, preferred_element_type=F32
    )
    grad_energy = 2.0 * lax.dot_general(
        squares, grad_sum, (((0,), (0,)), ((), ())), precision=HI, preferred_element_type=F32
    )
    for n in range(DEPTH):
        clear_pads(pad_ref.at[n])
        spread(pad_ref.at[n], r_ref[n, PX : 2 * PX, :].astype(F32))
        flip_ref[:, n * PX : (n + 1) * PX] = r_ref[n, 0:PX, :].astype(F32).T.astype(BF)
    for ky in range(3):
        for kx in range(3):
            tap = ky * 3 + kx
            rhs = jnp.concatenate(
                [pad_ref[n, 2 - kx, (2 - ky) * ROW : (2 - ky) * ROW + PX, :] for n in range(DEPTH)], axis=0
            )
            part = jnp.dot(flip_ref[...], rhs, preferred_element_type=F32)
            at = slice(tap * C, (tap + 1) * C)
            total_ref[at, :] = (part + w_ref[at, :].astype(F32) * grad_energy).astype(BF)
    keep_ref[...] = total_ref[pl.ds(pl.multiple_of(core * HALF, HALF), HALF), :]
    give_ref[...] = total_ref[pl.ds(pl.multiple_of((1 - core) * HALF, HALF), HALF), :]


def gradients(r, w, styles, demod, energy, affine):
    return pl.pallas_call(
        gradient_kernel,
        out_shape=(
            jax.ShapeDtypeStruct((HALF, C), BF),
            jax.ShapeDtypeStruct((HALF, C), BF),
            jax.ShapeDtypeStruct((8, C), F32),
            jax.ShapeDtypeStruct((8, affine.shape[0]), F32),
        ),
        in_specs=[vmem_spec()] * 6,
        out_specs=(vmem_spec(),) * 4,
        scratch_shapes=[
            pltpu.VMEM((C, DEPTH * PX), BF),
            pltpu.VMEM((DEPTH, 3, PAD, C), BF),
            pltpu.VMEM((ROWS, C), BF),
        ],
        compiler_params=params(),
        name="gradients",
    )(r, w, styles, demod, energy, affine)


def body(images, latent, weight, affine, biases, cotangent):
    width = latent.shape[1]
    replicas = lax.axis_size("dp")
    segments = lax.axis_size("segment")
    core = lax.axis_index("dp") % 2
    planes = [list(range(k, k + DEPTH)) for k in range(0, segments, DEPTH)]
    across = [(i, (i + DEPTH) % segments) for i in range(segments)]
    sibling = [(i, i ^ 1) for i in range(replicas)]
    cores = [list(range(k, replicas, 2)) for k in range(2)]
    peers = replicas // 2

    w = weight.reshape(ROWS, C)
    images = images.reshape(DEPTH, PX, C)
    cotangent = cotangent.reshape(DEPTH, PX, C)
    latent8 = jnp.pad(latent, ((0, 8 - DEPTH), (0, 0)))
    latent_all = lax.all_gather(latent, "dp", tiled=True)

    send, styles, demod, energy = prepare(latent8, affine[0], w, biases)
    a = lax.all_to_all(send, "segment", 0, 0, axis_index_groups=planes)
    b = lax.ppermute(a, "dp", sibling)

    act = first(images, a, b)
    arrived = lax.ppermute(act, "segment", across)
    dx, xs, conv, _ = middle(images, cotangent, arrived, a, b)
    returned = lax.ppermute(dx, "segment", across)
    sent = last(cotangent, returned, xs, conv, a, b)

    r = lax.all_to_all(sent, "segment", 0, 0, axis_index_groups=planes)
    keep, give, rows, latent_part = gradients(r, w, styles, demod, energy, affine[0])

    rows_all = lax.all_gather(rows, "dp")
    latent_parts = lax.all_gather(latent_part[:DEPTH], "segment")

    got = lax.ppermute(give, "dp", sibling)
    pair = (keep.astype(F32) + got.astype(F32)).astype(BF).reshape(peers, HALF // peers, C)
    shares = lax.all_to_all(pair, "dp", 0, 0, axis_index_groups=cores)
    share = jnp.sum(shares.astype(F32), axis=0).astype(BF)
    mine = lax.all_to_all(
        jnp.broadcast_to(share[None], (peers,) + share.shape), "dp", 0, 0, axis_index_groups=cores
    ).reshape(HALF, C)
    other = lax.ppermute(mine, "dp", sibling)
    low = jnp.where(core == 0, mine, other)
    high = jnp.where(core == 0, other, mine)
    grad_weight = jnp.concatenate([low, high], axis=0).astype(F32).reshape(weight.shape)

    grad_styles = rows_all[:, :DEPTH].reshape(replicas * DEPTH, C)
    grad_affine = lax.dot_general(latent_all, grad_styles, (((0,), (0,)), ((), ())), precision=HI)
    grad_bias = jnp.sum(rows_all[:, DEPTH], axis=0)
    grad_latent = jnp.sum(latent_parts, axis=0)
    return (grad_weight, grad_affine[None], grad_bias[None], grad_latent)


def solution(mesh):
    placed = (
        P("dp", None, None, None),
        P("dp", None),
        P("segment", None, None, None, None),
        P("segment", None, None),
        P("segment", None),
        P("dp", None, None, None),
    )
    return jax.shard_map(
        body,
        mesh=mesh,
        in_specs=placed,
        out_specs=(
            P("segment", None, None, None, None),
            P("segment", None, None),
            P("segment", None),
            P("dp", None),
        ),
        check_vma=False,
    )
```

time: 554 us -> 291 us (0.53)
  matrix products: 134 us -> 0.62 us
  Pallas kernels: 0 us -> 105 us
  waiting for transfers between devices: 106 us -> 21.6 us
  local copies, waits for them, and re-layouts: 84.1 us -> 5.96 us
  starting transfers between devices: 80.7 us -> 17.3 us
  blocking collectives: 83.1 us -> 129 us
  other arithmetic: 41.8 us -> 4.34 us
  between operations: 14.1 us -> 0.76 us
    pallas_call x0 -> x5, Pallas kernels: none -> 105 us  [the longest x1 74.8 us: prepare(): pl.pallas_call(prepare_kernel, out_shape=(jax.ShapeDtypeStruct((DEPTH, HA...]
    conv_general_dilated x44 -> x0, matrix products: 83.8 us -> none  [synth_layer(): lax.conv_general_dilated(scaled, kernel, (1, 1), 'SAME', dimension_number...]
    psum x2 -> x0, blocking collectives: 83.1 us -> none  [the longest x1 43.1 us: body(): latent_total = lax.psum(latent_acc, 'segment')]
    psum x1 -> x0, waiting for transfers between devices: 80.2 us -> none  [body(): lax.psum((weight_acc, affine_acc, bias_acc), 'dp')]
    ppermute x22 -> x5, starting transfers between devices: 80.7 us -> 13.8 us  [the longest x1 3.48 us: body(): got = lax.ppermute(give, 'dp', sibling)]
    all_to_all x0 -> x3, blocking collectives: none -> 66.6 us  [the longest x1 34.2 us: body(): a = lax.all_to_all(send, 'segment', 0, 0, axis_index_groups=planes)]
    all_gather x0 -> x3, blocking collectives: none -> 62.5 us  [the longest x1 27.8 us: body(): latent_parts = lax.all_gather(latent_part[:DEPTH], 'segment')]
    dot_general x66 -> x1, matrix products: 50.3 us -> 0.62 us  [body(): lax.dot_general(latent_all, grad_styles, (((0,), (0,)), ((), ())), precis...]
  transfers between devices with their start and end apart: 23 -> 6, of which waited for: 18 -> 5; matrix products, arithmetic and copies ran while one was open for 23% -> 1% of each run, Pallas kernels for 0% -> 0%
where the time goes in v1:
time: 291 us; the launch traced here: 285 us
  blocking collectives  129 us (44%)
  Pallas kernels  105 us (36%)
  waiting for transfers between devices  21.6 us (7%)
  starting transfers between devices  17.3 us (6%)
  local copies, waits for them, and re-layouts  5.96 us (2%)
  other arithmetic  4.34 us (1%)
    pallas_call x1, Pallas kernels, prepare(): pl.pallas_call(prepare_kernel, out_shape=(jax.ShapeDtypeStruct((DEPTH, HA...  74.8 us
    all_to_all x1, blocking collectives, body(): a = lax.all_to_all(send, 'segment', 0, 0, axis_index_groups=planes)  34.2 us
    all_gather x1, blocking collectives, body(): latent_parts = lax.all_gather(latent_part[:DEPTH], 'segment')  27.8 us
    all_gather x1, blocking collectives, body(): latent_all = lax.all_gather(latent, 'dp', tiled=True)  17.7 us
    all_to_all x1, blocking collectives, body(): r = lax.all_to_all(sent, 'segment', 0, 0, axis_index_groups=planes)  17.2 us
    all_gather x1, blocking collectives, body(): rows_all = lax.all_gather(rows, 'dp')  17 us
    all_to_all x1, blocking collectives, body(): shares = lax.all_to_all(pair, 'dp', 0, 0, axis_index_groups=cores)  15.1 us
    pallas_call x1, Pallas kernels, middle(): pl.pallas_call(middle_kernel, out_shape=(MAP, jax.ShapeDtypeStruct((DEPTH...  10.3 us
  transfers between devices with their start and end apart: 6, of which 5 were waited for; matrix products, arithmetic and copies ran while one was open for 1% of the time, Pallas kernels for 0%

profile of v1, /device:TPU:1, one launch (start us, length us, event | category | flops | bytes accessed | tf_op | source)
XLA Modules:
  0.0 284.9 jit_solution(16128018076632442242)
XLA Ops:
  0.6 1.3 pad.4.latent_ref
  1.9 74.8 %prepare.1 = (bf16[4,1168,256]{2,1,0:T(8,128)(2,1)}, f32[8,256]{1,0:T(8,128)}, f32[8,256]{1,0:T(8,128)}, f32[256,256]{1,0:T(8,128)}) custom-call(f32[8,512]{1,0:T(8,128)} %pad.4.latent_ref, f32[512,256]{1,0:T(8,128)} %bitcast.31, bf16[2304,256]{1,0:T(8,128)(2,1)} %bitcast.21, f32[1,256]{1,0:T(1,128)} %bias_ref.1, bf16[2304,256]{1,0:T(8,128)(2,1)} %bitcast.22), custom_call_target="tpu_custom_call" | custom-call | tf_op jit(solution)/shard_map/prepare/pallas_call | solution.py:107
  76.8 34.2 %all_to_all.20.a_any = bf16[4,1168,256]{2,1,0:T(8,128)(2,1)S(1)} all-to-all(bf16[4,1168,256]{2,1,0:T(8,128)(2,1)} %get-tuple-element.15), channel_id=1, replica_groups={{0,16,32,48},{64,80,96,112},{1,17,33,49},{65,81,97,113},{2,18,34,50},{6..., dimensions={0} | all-to-all | bytes 4784128 | tf_op jit(solution)/shard_map/all_to_all | solution.py:427
  111.0 0.0 copy-start
  111.0 2.1 collective-permute-start
  113.1 4.2 %collective-permute-done.b_any = bf16[4,1168,256]{2,1,0:T(8,128)(2,1)S(1)} collective-permute-done((bf16[4,1168,256]{2,1,0:T(8,128)(2,1)S(1)}, bf16[4,1168,256]{2,1,0:T(8,128)(2,1)S(1)}, u32[]{:S(2)}, u32[]{:S(2)}) %collective-permute-start) | collective-permute-done | bytes 2392096 | tf_op jit(solution)/shard_map/ppermute | solution.py:428
  117.3 0.0 copy-start.1
  117.3 0.0 copy-done
  117.3 1.4 copy-done.1
  118.7 6.2 %first.1 = bf16[256,256]{1,0:T(8,128)(2,1)} custom-call(bf16[4,256,256]{2,1,0:T(8,128)(2,1)} %bitcast.29, bf16[4,1168,256]{2,1,0:T(8,128)(2,1)} %copy-done, bf16[4,1168,256]{2,1,0:T(8,128)(2,1)} %copy-done.1), custom_call_target="tpu_custom_call" | custom-call | tf_op jit(solution)/shard_map/first/pallas_call | solution.py:284
  125.0 2.8 collective-permute-start.1
  127.8 3.7 %collective-permute-done.1.recv_ref = bf16[256,256]{1,0:T(8,128)(2,1)S(1)} collective-permute-done((bf16[256,256]{1,0:T(8,128)(2,1)}, bf16[256,256]{1,0:T(8,128)(2,1)S(1)}, u32[]{:S(2)}, u32[]{:S(2)}) %collective-permute-start.1) | collective-permute-done | bytes 131104 | tf_op jit(solution)/shard_map/ppermute | solution.py:431
  131.5 0.0 copy-start.3
  131.5 0.6 copy-done.3
  132.1 10.3 %middle.1 = (bf16[256,256]{1,0:T(8,128)(2,1)}, bf16[4,256,256]{2,1,0:T(8,128)(2,1)}, f32[4,256,256]{2,1,0:T(8,128)}, bf16[4,528,256]{2,1,0:T(8,128)(2,1)}) custom-call(bf16[4,256,256]{2,1,0:T(8,128)(2,1)} %bitcast.30, bf16[4,256,256]{2,1,0:T(8,128)(2,1)} %bitcast.27, bf16[256,256]{1,0:T(8,128)(2,1)} %copy-done.3, bf16[4,1168,256]{2,1,0:T(8,128)(2,1)} %copy-done, ...), custom_call_target="tpu_custom_call" | custom-call | tf_op jit(solution)/shard_map/middle/pallas_call | solution.py:302
  142.4 2.8 collective-permute-start.2
  145.2 2.8 collective-permute-done.2.recv_ref
  148.0 0.0 copy-start.2
  148.0 0.6 copy-done.2
  148.7 8.1 %last.1 = bf16[4,528,256]{2,1,0:T(8,128)(2,1)} custom-call(bf16[4,256,256]{2,1,0:T(8,128)(2,1)} %bitcast.28, bf16[256,256]{1,0:T(8,128)(2,1)} %copy-done.2, bf16[4,256,256]{2,1,0:T(8,128)(2,1)} %get-tuple-element.17.xs_any, f32[4,256,256]{2,1,0:T(8,128)} %get-tuple-element.18.conv_any, bf16[4,1168,256]{2,1,0:T(8,128)(2,1)} %copy-done, ...), custom_call_target="tpu_custom_call" | custom-call | tf_op jit(solution)/shard_map/last/pallas_call | solution.py:326
  156.7 17.2 %all_to_all.21.r_ref = bf16[4,528,256]{2,1,0:T(8,128)(2,1)} all-to-all(bf16[4,528,256]{2,1,0:T(8,128)(2,1)} %last.1), channel_id=1, replica_groups={{0,16,32,48},{64,80,96,112},{1,17,33,49},{65,81,97,113},{2,18,34,50},{6..., dimensions={0} | all-to-all | bytes 2162688 | tf_op jit(solution)/shard_map/all_to_all | solution.py:436
  174.0 5.8 %gradients.1 = (bf16[1152,256]{1,0:T(8,128)(2,1)}, bf16[1152,256]{1,0:T(8,128)(2,1)}, f32[8,256]{1,0:T(8,128)}, f32[8,512]{1,0:T(8,128)}) custom-call(bf16[4,528,256]{2,1,0:T(8,128)(2,1)} %all_to_all.21.r_ref, bf16[2304,256]{1,0:T(8,128)(2,1)} %bitcast.23, f32[8,256]{1,0:T(8,128)} %get-tuple-element.19.styles_ref, f32[8,256]{1,0:T(8,128)} %get-tuple-element.20.demod_ref, ...), custom_call_target="tpu_custom_call" | custom-call | tf_op jit(solution)/shard_map/gradients/pallas_call | solution.py:389
  179.8 3.5 %collective-permute-start.3 = (bf16[1152,256]{1,0:T(8,128)(2,1)}, bf16[1152,256]{1,0:T(8,128)(2,1)S(1)}, u32[]{:S(2)}, u32[]{:S(2)}) collective-permute-start(bf16[1152,256]{1,0:T(8,128)(2,1)} %get-tuple-element.23), channel_id=1, source_target_pairs={{0,1},{1,0},{2,3},{3,2},{4,5},{5,4},{6,7},{7,6},{8,9},{9,8},{10,11... | collective-permute-start | bytes 1769480 | tf_op jit(solution)/shard_map/ppermute | solution.py:442
  183.2 1.8 collective-permute-done.3
  185.1 1.2 add_convert_fusion
  186.3 15.1 %all_to_all.22 = bf16[8,144,256]{2,1,0:T(8,128)(2,1)S(1)} all-to-all(bf16[8,144,256]{2,1,0:T(8,128)(2,1)S(1)} %bitcast.26), channel_id=1, replica_groups={{0,2,4,6,8,10,12,14},{1,3,5,7,9,11,13,15},{16,18,20,22,24,26,28,30},{17..., dimensions={0} | all-to-all | bytes 1179648 | tf_op jit(solution)/shard_map/all_to_all | solution.py:444
  201.4 0.0 copy-start.4
  201.4 0.1 reduce_sum.30
  201.5 0.0 copy-start.5
  201.5 0.9 broadcast_in_dim.12
  202.4 3.5 %all-to-all-start.3 = ((bf16[8,144,256]{2,1,0:T(8,128)(2,1)}), bf16[8,144,256]{2,1,0:T(8,128)(2,1)S(1)}, u32[]{:S(2)}, u32[]{:S(2)}) async-start(bf16[8,144,256]{2,1,0:T(8,128)(2,1)} %broadcast_in_dim.12), calls=%async_computation.3 | async-start | bytes 1179648 | tf_op jit(solution)/shard_map/all_to_all | solution.py:446
  205.9 9.1 %all-to-all-done.3 = bf16[8,144,256]{2,1,0:T(8,128)(2,1)S(1)} async-done(((bf16[8,144,256]{2,1,0:T(8,128)(2,1)}), bf16[8,144,256]{2,1,0:T(8,128)(2,1)S(1)}, u32[]{:S(2)}, u32[]{:S(2)}) %all-to-all-start.3) | async-done | bytes 589856 | tf_op jit(solution)/shard_map/all_to_all | solution.py:446
  215.0 2.6 collective-permute-start.4
  217.6 0.0 copy-done.4
  217.6 17.7 %all-gather.2 = f32[16,4,512]{2,1,0:T(4,128)S(1)} all-gather(f32[1,4,512]{2,1,0:T(4,128)S(1)} %bitcast.35), channel_id=1, replica_groups=mesh['segment'=8,'dp'=16] {'dp'}, dimensions={0}, use_global_device_ids=true | all-gather | bytes 139264 | tf_op jit(solution)/shard_map/all_gather | solution.py:424
  235.3 0.0 copy-start.6
  235.3 0.0 copy-done.5
  235.3 17.0 %all-gather = f32[128,256]{1,0:T(8,128)S(1)} all-gather(f32[8,256]{1,0:T(8,128)S(1)} %copy-done.5), channel_id=2, replica_groups=mesh['segment'=8,'dp'=16] {'dp'}, dimensions={0}, use_global_device_ids=true | all-gather | bytes 139264 | tf_op jit(solution)/shard_map/all_gather | solution.py:439
  252.4 0.6 convolution_bitcast_fusion
  253.1 1.0 copy.11
  254.1 0.0 copy-done.6
  254.1 27.8 %all-gather.3 = f32[8,4,512]{2,1,0:T(4,128)S(1)} all-gather(f32[1,4,512]{2,1,0:T(4,128)S(1)} %slice_bitcast_fusion), channel_id=3, replica_groups=mesh['segment'=8,'dp'=16] {'segment'}, dimensions={0}, use_global_device_ids=true | all-gather | bytes 73728 | tf_op jit(solution)/shard_map/all_gather | solution.py:440
  281.9 0.6 reduce_sum.32
  282.5 0.6 slice_reduce_fusion
  283.1 0.0 collective-permute-done.4
  283.1 0.1 broadcast_select_fusion.1
  283.2 0.1 pad_maximum_fusion
  283.3 1.6 convert.2
  (4 shorter events, 0.1 us)
Async XLA Ops:
  111.0 6.3 %copy-start = (bf16[4,1168,256]{2,1,0:T(8,128)(2,1)}, bf16[4,1168,256]{2,1,0:T(8,128)(2,1)S(1)}, u32[]{:S(2)}) copy-start(bf16[4,1168,256]{2,1,0:T(8,128)(2,1)S(1)} %all_to_all.20.a_any) | copy-start | bytes 7176196
  111.0 6.3 %collective-permute-start = (bf16[4,1168,256]{2,1,0:T(8,128)(2,1)S(1)}, bf16[4,1168,256]{2,1,0:T(8,128)(2,1)S(1)}, u32[]{:S(2)}, u32[]{:S(2)}) collective-permute-start(bf16[4,1168,256]{2,1,0:T(8,128)(2,1)S(1)} %all_to_all.20.a_any), channel_id=1, source_target_pairs={{0,1},{1,0},{2,3},{3,2},{4,5},{5,4},{6,7},{7,6},{8,9},{9,8},{10,11... | collective-permute-start | bytes 7176200 | tf_op jit(solution)/shard_map/ppermute | solution.py:428
  117.3 1.4 copy-start.1
  125.0 6.5 %collective-permute-start.1 = (bf16[256,256]{1,0:T(8,128)(2,1)}, bf16[256,256]{1,0:T(8,128)(2,1)S(1)}, u32[]{:S(2)}, u32[]{:S(2)}) collective-permute-start(bf16[256,256]{1,0:T(8,128)(2,1)} %first.1), channel_id=1, source_target_pairs={{0,64},{16,80},{32,96},{48,112},{64,0},{80,16},{96,32},{112,48},{1... | collective-permute-start | bytes 393224 | tf_op jit(solution)/shard_map/ppermute | solution.py:431
  131.5 0.6 copy-start.3
  142.4 5.6 %collective-permute-start.2 = (bf16[256,256]{1,0:T(8,128)(2,1)}, bf16[256,256]{1,0:T(8,128)(2,1)S(1)}, u32[]{:S(2)}, u32[]{:S(2)}) collective-permute-start(bf16[256,256]{1,0:T(8,128)(2,1)} %get-tuple-element.16), channel_id=1, source_target_pairs={{0,64},{16,80},{32,96},{48,112},{64,0},{80,16},{96,32},{112,48},{1... | collective-permute-start | bytes 393224 | tf_op jit(solution)/shard_map/ppermute | solution.py:433
  148.0 0.6 copy-start.2
  179.8 5.3 %collective-permute-start.3 = (bf16[1152,256]{1,0:T(8,128)(2,1)}, bf16[1152,256]{1,0:T(8,128)(2,1)S(1)}, u32[]{:S(2)}, u32[]{:S(2)}) collective-permute-start(bf16[1152,256]{1,0:T(8,128)(2,1)} %get-tuple-element.23), channel_id=1, source_target_pairs={{0,1},{1,0},{2,3},{3,2},{4,5},{5,4},{6,7},{7,6},{8,9},{9,8},{10,11... | collective-permute-start | bytes 1769480 | tf_op jit(solution)/shard_map/ppermute | solution.py:442
  201.4 16.2 %copy-start.4 = (f32[4,512]{1,0:T(4,128)S(1)}, f32[4,512]{1,0:T(4,128)}, u32[]{:S(2)}) copy-start(f32[4,512]{1,0:T(4,128)} %param.7) | copy-start | bytes 24580
  201.5 33.8 %copy-start.5 = (f32[8,256]{1,0:T(8,128)S(1)}, f32[8,256]{1,0:T(8,128)}, u32[]{:S(2)}) copy-start(f32[8,256]{1,0:T(8,128)} %get-tuple-element.24) | copy-start | bytes 24580
  202.4 12.7 %all-to-all-start.3 = ((bf16[8,144,256]{2,1,0:T(8,128)(2,1)}), bf16[8,144,256]{2,1,0:T(8,128)(2,1)S(1)}, u32[]{:S(2)}, u32[]{:S(2)}) async-start(bf16[8,144,256]{2,1,0:T(8,128)(2,1)} %broadcast_in_dim.12), calls=%async_computation.3 | async-start | bytes 1179648 | tf_op jit(solution)/shard_map/all_to_all | solution.py:446
  215.0 68.0 %collective-permute-start.4 = (bf16[1152,256]{1,0:T(8,128)(2,1)S(1)}, bf16[1152,256]{1,0:T(8,128)(2,1)S(1)}, u32[]{:S(2)}, u32[]{:S(2)}) collective-permute-start(bf16[1152,256]{1,0:T(8,128)(2,1)S(1)} %bitcast.25), channel_id=1, source_target_pairs={{0,1},{1,0},{2,3},{3,2},{4,5},{5,4},{6,7},{7,6},{8,9},{9,8},{10,11... | collective-permute-start | bytes 1769480 | tf_op jit(solution)/shard_map/ppermute | solution.py:449
  235.3 18.8 %copy-start.6 = (f32[8,512]{1,0:T(8,128)S(1)}, f32[8,512]{1,0:T(8,128)}, u32[]{:S(2)}) copy-start(f32[8,512]{1,0:T(8,128)} %get-tuple-element.25) | copy-start | bytes 49156

commit v2 on v1

--- a/solution.py
+++ b/solution.py
@@ -19,6 +19,8 @@
 HALF = ROWS // 2
 STAT = 16
 DEPTH = 4
+PEERS = 8
+SHARE = HALF // PEERS
 ROW = 16
 PAD = PX + 2 * ROW
 HI = lax.Precision.HIGHEST
@@ -33,7 +35,11 @@
 
 
 def params():
-    return pltpu.CompilerParams(vmem_limit_bytes=56 << 20)
+    return pltpu.CompilerParams(vmem_limit_bytes=28 << 20)
+
+
+def near(value):
+    return pltpu.with_memory_space_constraint(value, pltpu.VMEM)
 
 
 def place():
@@ -72,17 +78,17 @@
     return out
 
 
-def prepare_kernel(latent_ref, affine_ref, w_ref, bias_ref, w_any, send_ref, styles_ref, demod_ref, energy_ref, tile_ref, sem):
+def prepare_kernel(latent_ref, affine_ref, w_ref, bias_ref, send_ref, styles_ref, demod_ref, energy_ref, rows_ref, tile_ref, sem):
     _, _, core = place()
+    mine = pl.ds(pl.multiple_of(core * HALF, HALF), HALF)
     copies = [
-        pltpu.make_async_copy(
-            w_any.at[pl.ds(pl.multiple_of(core * HALF, HALF), HALF)], send_ref.at[k, pl.ds(0, HALF)], sem.at[k]
-        )
-        for k in range(DEPTH)
+        pltpu.make_async_copy(w_ref.at[mine], send_ref.at[k, pl.ds(0, HALF)], sem.at[k]) for k in range(DEPTH)
     ]
     for copy in copies:
         copy.start()
-    styles = jnp.dot(latent_ref[...], affine_ref[...], precision=HI, preferred_element_type=F32) + 1.0
+    rows_ref[...] = jnp.zeros_like(rows_ref)
+    rows_ref[0:DEPTH, :] = latent_ref[...]
+    styles = jnp.dot(rows_ref[...], affine_ref[...], precision=HI, preferred_element_type=F32) + 1.0
     energy = jnp.zeros((C, C), F32)
     for tap in range(TAPS):
         part = w_ref[tap * C : (tap + 1) * C, :].astype(F32)
@@ -103,7 +109,7 @@
         copy.wait()
 
 
-def prepare(latent8, affine, w, bias):
+def prepare(latent, affine, w, bias):
     return pl.pallas_call(
         prepare_kernel,
         out_shape=(
@@ -112,12 +118,16 @@
             jax.ShapeDtypeStruct((8, C), F32),
             jax.ShapeDtypeStruct((C, C), F32),
         ),
-        in_specs=[vmem_spec()] * 4 + [any_spec()],
+        in_specs=[vmem_spec()] * 4,
         out_specs=(any_spec(), vmem_spec(), vmem_spec(), vmem_spec()),
-        scratch_shapes=[pltpu.VMEM((DEPTH, STAT, C), BF), pltpu.SemaphoreType.DMA((2 * DEPTH,))],
+        scratch_shapes=[
+            pltpu.VMEM((8, latent.shape[1]), F32),
+            pltpu.VMEM((DEPTH, STAT, C), BF),
+            pltpu.SemaphoreType.DMA((2 * DEPTH,)),
+        ],
         compiler_params=params(),
         name="prepare",
-    )(latent8, affine, w, bias, w)
+    )(latent, affine, w, bias)
 
 
 def weight_copies(a_any, b_any, w_buf, stat_buf, sem):
@@ -284,7 +294,7 @@
     return pl.pallas_call(
         first_kernel,
         out_shape=MAP,
-        in_specs=[any_spec()] * 3,
+        in_specs=[any_spec(), vmem_spec(), vmem_spec()],
         out_specs=vmem_spec(),
         scratch_shapes=weight_scratch()
         + [
@@ -307,7 +317,7 @@
             jax.ShapeDtypeStruct((DEPTH, PX, C), F32),
             SENT,
         ),
-        in_specs=[any_spec(), any_spec(), vmem_spec(), any_spec(), any_spec()],
+        in_specs=[any_spec(), any_spec(), vmem_spec(), vmem_spec(), vmem_spec()],
         out_specs=(vmem_spec(),) * 4,
         scratch_shapes=weight_scratch()
         + [
@@ -326,7 +336,7 @@
     return pl.pallas_call(
         last_kernel,
         out_shape=SENT,
-        in_specs=[any_spec(), vmem_spec(), any_spec(), any_spec(), any_spec(), any_spec()],
+        in_specs=[any_spec(), vmem_spec(), any_spec(), any_spec(), vmem_spec(), vmem_spec()],
         out_specs=vmem_spec(),
         scratch_shapes=weight_scratch()
         + [
@@ -344,8 +354,8 @@
 
 
 def gradient_kernel(
-    r_ref, w_ref, styles_ref, demod_ref, energy_ref, affine_ref,
-    keep_ref, give_ref, rows_ref, latent_ref, flip_ref, pad_ref, total_ref,
+    r_ref, w_ref, styles_ref, demod_ref, energy_ref, affine_ref, latent_ref,
+    keep_ref, give_ref, extra_ref, grad_latent_ref, flip_ref, pad_ref, total_ref, rows_ref,
 ):
     _, _, core = place()
     parts = [unpack_rows(r_ref[n, 2 * PX : 2 * PX + STAT, :]) for n in range(DEPTH)]
@@ -357,12 +367,16 @@
         grad_sum, energy_ref[...], (((1,), (1,)), ((), ())), precision=HI, preferred_element_type=F32
     )
     grad_styles = stack_rows([p[0] for p in parts]) + 2.0 * styles * grad_squares
-    index = lax.broadcasted_iota(jnp.int32, (8, C), 0)
     grad_bias = parts[0][2] + parts[1][2] + parts[2][2] + parts[3][2]
-    rows_ref[...] = jnp.where(
-        index < DEPTH, grad_styles, jnp.where(index == DEPTH, jnp.broadcast_to(grad_bias, (8, C)), 0.0)
-    )
-    latent_ref[...] = lax.dot_general(
+    rows_ref[...] = jnp.zeros_like(rows_ref)
+    rows_ref[0:DEPTH, :] = grad_styles[0:DEPTH]
+    rows_ref[DEPTH : DEPTH + 1, :] = grad_bias
+    rows_ref[8 : 8 + DEPTH, :] = latent_ref[:, 0:C]
+    rows_ref[8 + DEPTH : 8 + 2 * DEPTH, :] = latent_ref[:, C : 2 * C]
+    extra = rows_ref[...].astype(BF)
+    extra_ref[...] = extra
+    give_ref[HALF : HALF + STAT, :] = extra
+    grad_latent_ref[...] = lax.dot_general(
         grad_styles, affine_ref[...], (((1,), (1,)), ((), ())), precision=HI, preferred_element_type=F32
     )
     grad_energy = 2.0 * lax.dot_general(
@@ -382,28 +396,98 @@
             at = slice(tap * C, (tap + 1) * C)
             total_ref[at, :] = (part + w_ref[at, :].astype(F32) * grad_energy).astype(BF)
     keep_ref[...] = total_ref[pl.ds(pl.multiple_of(core * HALF, HALF), HALF), :]
-    give_ref[...] = total_ref[pl.ds(pl.multiple_of((1 - core) * HALF, HALF), HALF), :]
-
-
-def gradients(r, w, styles, demod, energy, affine):
+    give_ref[0:HALF, :] = total_ref[pl.ds(pl.multiple_of((1 - core) * HALF, HALF), HALF), :]
+
+
+def gradients(r, w, styles, demod, energy, affine, latent):
     return pl.pallas_call(
         gradient_kernel,
         out_shape=(
             jax.ShapeDtypeStruct((HALF, C), BF),
-            jax.ShapeDtypeStruct((HALF, C), BF),
-            jax.ShapeDtypeStruct((8, C), F32),
+            jax.ShapeDtypeStruct((HALF + STAT, C), BF),
+            jax.ShapeDtypeStruct((STAT, C), BF),
             jax.ShapeDtypeStruct((8, affine.shape[0]), F32),
         ),
-        in_specs=[vmem_spec()] * 6,
+        in_specs=[vmem_spec()] * 7,
         out_specs=(vmem_spec(),) * 4,
         scratch_shapes=[
             pltpu.VMEM((C, DEPTH * PX), BF),
             pltpu.VMEM((DEPTH, 3, PAD, C), BF),
             pltpu.VMEM((ROWS, C), BF),
+            pltpu.VMEM((STAT, C), F32),
         ],
         compiler_params=params(),
         name="gradients",
-    )(r, w, styles, demod, energy, affine)
+    )(r, w, styles, demod, energy, affine, latent)
+
+
+def pair_kernel(keep_ref, extra_ref, got_ref, out_ref):
+    for k in range(PEERS):
+        at = slice(k * SHARE, (k + 1) * SHARE)
+        out_ref[k, 0:SHARE, :] = (keep_ref[at, :].astype(F32) + got_ref[at, :].astype(F32)).astype(BF)
+        out_ref[k, SHARE : SHARE + STAT, :] = extra_ref[...]
+        out_ref[k, SHARE + STAT : SHARE + 2 * STAT, :] = got_ref[HALF : HALF + STAT, :]
+
+
+def pair(keep, extra, got):
+    return pl.pallas_call(
+        pair_kernel,
+        out_shape=jax.ShapeDtypeStruct((PEERS, SHARE + 2 * STAT, C), BF),
+        in_specs=[vmem_spec()] * 3,
+        out_specs=vmem_spec(),
+        compiler_params=params(),
+        name="pair",
+    )(keep, extra, got)
+
+
+def share_kernel(shares_ref, out_ref):
+    total = shares_ref[0, 0:SHARE, :].astype(F32)
+    for k in range(1, PEERS):
+        total += shares_ref[k, 0:SHARE, :].astype(F32)
+    total = total.astype(BF)
+    for k in range(PEERS):
+        out_ref[k] = total
+
+
+def share(shares):
+    return pl.pallas_call(
+        share_kernel,
+        out_shape=jax.ShapeDtypeStruct((PEERS, SHARE, C), BF),
+        in_specs=[vmem_spec()],
+        out_specs=vmem_spec(),
+        compiler_params=params(),
+        name="share",
+    )(shares)
+
+
+def affine_kernel(shares_ref, affine_ref, bias_ref, grads_ref, low_ref, high_ref):
+    row = lax.broadcasted_iota(jnp.int32, (STAT, C), 0)
+    bias = jnp.zeros((1, C), F32)
+    for k in range(2 * PEERS):
+        start = SHARE + (k % 2) * STAT
+        tile = shares_ref[k // 2, start : start + STAT, :].astype(F32)
+        bias += tile[DEPTH : DEPTH + 1]
+        at = slice(k * STAT, (k + 1) * STAT)
+        grads_ref[at, :] = jnp.where(row < DEPTH, tile, 0.0).astype(BF)
+        low_ref[at, :] = pltpu.roll(tile, 8, 0).astype(BF)
+        high_ref[at, :] = pltpu.roll(tile, 4, 0).astype(BF)
+    bias_ref[...] = bias
+    for k, ref in enumerate((low_ref, high_ref)):
+        affine_ref[k * C : (k + 1) * C, :] = lax.dot_general(
+            ref[...], grads_ref[...], (((0,), (0,)), ((), ())), preferred_element_type=F32
+        )
+
+
+def affine_gradient(shares, width):
+    return pl.pallas_call(
+        affine_kernel,
+        out_shape=(jax.ShapeDtypeStruct((width, C), F32), jax.ShapeDtypeStruct((1, C), F32)),
+        in_specs=[vmem_spec()],
+        out_specs=(vmem_spec(), vmem_spec()),
+        scratch_shapes=[pltpu.VMEM((2 * PEERS * STAT, C), BF)] * 3,
+        compiler_params=params(),
+        name="affine",
+    )(shares)
 
 
 def body(images, latent, weight, affine, biases, cotangent):
@@ -415,47 +499,42 @@
     across = [(i, (i + DEPTH) % segments) for i in range(segments)]
     sibling = [(i, i ^ 1) for i in range(replicas)]
     cores = [list(range(k, replicas, 2)) for k in range(2)]
-    peers = replicas // 2
 
     w = weight.reshape(ROWS, C)
     images = images.reshape(DEPTH, PX, C)
     cotangent = cotangent.reshape(DEPTH, PX, C)
-    latent8 = jnp.pad(latent, ((0, 8 - DEPTH), (0, 0)))
-    latent_all = lax.all_gather(latent, "dp", tiled=True)
-
-    send, styles, demod, energy = prepare(latent8, affine[0], w, biases)
+
+    send, styles, demod, energy = prepare(latent, affine[0], w, biases)
     a = lax.all_to_all(send, "segment", 0, 0, axis_index_groups=planes)
-    b = lax.ppermute(a, "dp", sibling)
+    b = near(lax.ppermute(a, "dp", sibling))
+    a = near(a)
 
     act = first(images, a, b)
-    arrived = lax.ppermute(act, "segment", across)
+    arrived = near(lax.ppermute(act, "segment", across))
     dx, xs, conv, _ = middle(images, cotangent, arrived, a, b)
-    returned = lax.ppermute(dx, "segment", across)
+    returned = near(lax.ppermute(dx, "segment", across))
     sent = last(cotangent, returned, xs, conv, a, b)
 
-    r = lax.all_to_all(sent, "segment", 0, 0, axis_index_groups=planes)
-    keep, give, rows, latent_part = gradients(r, w, styles, demod, energy, affine[0])
-
-    rows_all = lax.all_gather(rows, "dp")
-    latent_parts = lax.all_gather(latent_part[:DEPTH], "segment")
-
-    got = lax.ppermute(give, "dp", sibling)
-    pair = (keep.astype(F32) + got.astype(F32)).astype(BF).reshape(peers, HALF // peers, C)
-    shares = lax.all_to_all(pair, "dp", 0, 0, axis_index_groups=cores)
-    share = jnp.sum(shares.astype(F32), axis=0).astype(BF)
-    mine = lax.all_to_all(
-        jnp.broadcast_to(share[None], (peers,) + share.shape), "dp", 0, 0, axis_index_groups=cores
-    ).reshape(HALF, C)
+    r = near(lax.all_to_all(sent, "segment", 0, 0, axis_index_groups=planes))
+    keep, give, extra, latent_part = gradients(r, w, styles, demod, energy, affine[0], latent)
+
+    got = near(lax.ppermute(give, "dp", sibling))
+    part = latent_part[:DEPTH]
+    part = part + lax.ppermute(part, "segment", across)
+    shared = pair(keep, extra, got)
+    shared, part = lax.optimization_barrier((shared, part))
+    shares = near(lax.all_to_all(shared, "dp", 0, 0, axis_index_groups=cores))
+    part = part + lax.ppermute(part, "segment", [(i, i ^ 1) for i in range(segments)])
+    spread_share = share(shares)
+    spread_share, part = lax.optimization_barrier((spread_share, part))
+    mine = lax.all_to_all(spread_share, "dp", 0, 0, axis_index_groups=cores).reshape(HALF, C)
+    grad_latent = part + lax.ppermute(part, "segment", [(i, i ^ 2) for i in range(segments)])
+    grad_affine, grad_bias = affine_gradient(shares, width)
     other = lax.ppermute(mine, "dp", sibling)
     low = jnp.where(core == 0, mine, other)
     high = jnp.where(core == 0, other, mine)
     grad_weight = jnp.concatenate([low, high], axis=0).astype(F32).reshape(weight.shape)
-
-    grad_styles = rows_all[:, :DEPTH].reshape(replicas * DEPTH, C)
-    grad_affine = lax.dot_general(latent_all, grad_styles, (((0,), (0,)), ((), ())), precision=HI)
-    grad_bias = jnp.sum(rows_all[:, DEPTH], axis=0)
-    grad_latent = jnp.sum(latent_parts, axis=0)
-    return (grad_weight, grad_affine[None], grad_bias[None], grad_latent)
+    return (grad_weight, grad_affine[None], grad_bias, grad_latent)
 
 
 def solution(mesh):

time: 291 us -> 141 us (0.48); the launches traced: 285 us -> 140 us
  Pallas kernels: 105 us -> 25.1 us
  blocking collectives: 129 us -> 60.4 us
  starting transfers between devices: 17.3 us -> 23.8 us
    pallas_call x1, Pallas kernels: 74.8 us -> 1.39 us  [prepare(): pl.pallas_call(prepare_kernel, out_shape=(jax.ShapeDtypeStruct((DEPTH, HA...]
    all_gather x3 -> x0, blocking collectives: 62.5 us -> none  [the longest x1 27.8 us: body(): latent_parts = lax.all_gather(latent_part[:DEPTH], 'segment')]
    all_to_all x2, blocking collectives: 32.4 us -> 26.2 us  [the longest x1 15.4 us: body(): r = near(lax.all_to_all(sent, 'segment', 0, 0, axis_index_groups=planes))]
    ppermute x4 -> x7, starting transfers between devices: 11.2 us -> 15.1 us  [the longest x1 3.56 us: body(): got = near(lax.ppermute(give, 'dp', sibling))]
    ppermute x4 -> x7, waiting for transfers between devices: 12.5 us -> 15.9 us  [the longest x1 4.21 us: body(): b = near(lax.ppermute(a, 'dp', sibling))]
    pallas_call x1 -> x4, Pallas kernels: 6.24 us -> 6.52 us  [the longest x1 4.37 us: first(): pl.pallas_call(first_kernel, out_shape=MAP, in_specs=[any_spec(), vmem_sp...]
  transfers between devices with their start and end apart: 6 -> 9, of which waited for: 5 -> 7; matrix products, arithmetic and copies ran while one was open for 1% -> 0% of each run, Pallas kernels for 0% -> 1%
where the time goes in v2:
time: 141 us; the launch traced here: 140 us
  blocking collectives  60.4 us (43%)
  Pallas kernels  25.1 us (18%)
  waiting for transfers between devices  24.1 us (17%)
  starting transfers between devices  23.8 us (17%)
  local copies, waits for them, and re-layouts  3.7 us (3%)
  other arithmetic  2.44 us (2%)
    all_to_all x1, blocking collectives, body(): a = lax.all_to_all(send, 'segment', 0, 0, axis_index_groups=planes)  34.1 us
    all_to_all x1, blocking collectives, body(): r = near(lax.all_to_all(sent, 'segment', 0, 0, axis_index_groups=planes))  15.4 us
    all_to_all x1, blocking collectives, body(): lax.all_to_all(spread_share, 'dp', 0, 0, axis_index_groups=cores)  10.8 us
    pallas_call x1, Pallas kernels, middle(): pl.pallas_call(middle_kernel, out_shape=(MAP, jax.ShapeDtypeStruct((DEPTH...  8.7 us
    all_to_all x1, waiting for transfers between devices, body(): shares = near(lax.all_to_all(shared, 'dp', 0, 0, axis_index_groups=cores))  8.23 us
    pallas_call x1, Pallas kernels, last(): pl.pallas_call(last_kernel, out_shape=SENT, in_specs=[any_spec(), vmem_sp...  5.48 us
    all_to_all x1, starting transfers between devices, body(): shares = near(lax.all_to_all(shared, 'dp', 0, 0, axis_index_groups=cores))  5.12 us
    pallas_call x1, Pallas kernels, first(): pl.pallas_call(first_kernel, out_shape=MAP, in_specs=[any_spec(), vmem_sp...  4.37 us
  transfers between devices with their start and end apart: 9, of which 7 were waited for; matrix products, arithmetic and copies ran while one was open for 0% of the time, Pallas kernels for 1%

profile of v2, /device:TPU:1, one launch (start us, length us, event | category | flops | bytes accessed | tf_op | source)
XLA Modules:
  0.0 140.2 jit_solution(10144005435923748073)
XLA Ops:
  0.6 0.0 copy-start
  0.6 1.3 copy-done
  1.9 0.0 copy-start.2
  1.9 1.0 copy-done.2
  2.9 0.0 copy-start.5
  2.9 0.7 copy-done.5
  3.6 0.0 copy-start.7
  3.6 0.7 copy-done.7
  4.3 1.4 prepare.1
  5.7 0.0 copy-start.4
  5.7 34.1 %all_to_all.20.a_any = bf16[4,1168,256]{2,1,0:T(8,128)(2,1)S(1)} all-to-all(bf16[4,1168,256]{2,1,0:T(8,128)(2,1)S(1)} %get-tuple-element.21), channel_id=1, replica_groups={{0,16,32,48},{64,80,96,112},{1,17,33,49},{65,81,97,113},{2,18,34,50},{6..., dimensions={0} | all-to-all | bytes 4784128 | tf_op jit(solution)/shard_map/all_to_all | solution.py:508
  39.9 2.1 %collective-permute-start = (bf16[4,1168,256]{2,1,0:T(8,128)(2,1)S(1)}, bf16[4,1168,256]{2,1,0:T(8,128)(2,1)S(1)}, u32[]{:S(2)}, u32[]{:S(2)}) collective-permute-start(bf16[4,1168,256]{2,1,0:T(8,128)(2,1)S(1)} %all_to_all.20.a_any), channel_id=1, source_target_pairs={{0,1},{1,0},{2,3},{3,2},{4,5},{5,4},{6,7},{7,6},{8,9},{9,8},{10,11... | collective-permute-start | bytes 7176200 | tf_op jit(solution)/shard_map/ppermute | solution.py:509
  42.0 4.2 %collective-permute-done.b_any = bf16[4,1168,256]{2,1,0:T(8,128)(2,1)S(1)} collective-permute-done((bf16[4,1168,256]{2,1,0:T(8,128)(2,1)S(1)}, bf16[4,1168,256]{2,1,0:T(8,128)(2,1)S(1)}, u32[]{:S(2)}, u32[]{:S(2)}) %collective-permute-start) | collective-permute-done | bytes 2392096 | tf_op jit(solution)/shard_map/ppermute | solution.py:509
  46.2 0.0 copy-done.4
  46.2 0.0 copy-start.1
  46.2 4.4 %first.1 = bf16[256,256]{1,0:T(8,128)(2,1)S(1)} custom-call(bf16[4,256,256]{2,1,0:T(8,128)(2,1)S(1)} %bitcast.16, bf16[4,1168,256]{2,1,0:T(8,128)(2,1)S(1)} %all_to_all.20.a_any, bf16[4,1168,256]{2,1,0:T(8,128)(2,1)S(1)} %collective-permute-done.b_any), custom_call_target="tpu_custom_call" | custom-call | tf_op jit(solution)/shard_map/first/pallas_call | solution.py:294
  50.6 2.8 %collective-permute-start.1 = (bf16[256,256]{1,0:T(8,128)(2,1)S(1)}, bf16[256,256]{1,0:T(8,128)(2,1)S(1)}, u32[]{:S(2)}, u32[]{:S(2)}) collective-permute-start(bf16[256,256]{1,0:T(8,128)(2,1)S(1)} %first.1), channel_id=1, source_target_pairs={{0,64},{16,80},{32,96},{48,112},{64,0},{80,16},{96,32},{112,48},{1... | collective-permute-start | bytes 393224 | tf_op jit(solution)/shard_map/ppermute | solution.py:513
  53.4 3.5 %collective-permute-done.1.recv_ref = bf16[256,256]{1,0:T(8,128)(2,1)S(1)} collective-permute-done((bf16[256,256]{1,0:T(8,128)(2,1)S(1)}, bf16[256,256]{1,0:T(8,128)(2,1)S(1)}, u32[]{:S(2)}, u32[]{:S(2)}) %collective-permute-start.1) | collective-permute-done | bytes 131104 | tf_op jit(solution)/shard_map/ppermute | solution.py:513
  56.8 0.0 copy-done.1
  56.9 8.7 %middle.1 = (bf16[256,256]{1,0:T(8,128)(2,1)S(1)}, bf16[4,256,256]{2,1,0:T(8,128)(2,1)S(1)}, f32[4,256,256]{2,1,0:T(8,128)S(1)}, bf16[4,528,256]{2,1,0:T(8,128)(2,1)}) custom-call(bf16[4,256,256]{2,1,0:T(8,128)(2,1)S(1)} %bitcast.17, bf16[4,256,256]{2,1,0:T(8,128)(2,1)S(1)} %bitcast.12, bf16[256,256]{1,0:T(8,128)(2,1)S(1)} %collective-permute-done.1.recv_ref, ...), custom_call_target="tpu_custom_call" | custom-call | tf_op jit(solution)/shard_map/middle/pallas_call | solution.py:312
  65.6 2.8 %collective-permute-start.2 = (bf16[256,256]{1,0:T(8,128)(2,1)S(1)}, bf16[256,256]{1,0:T(8,128)(2,1)S(1)}, u32[]{:S(2)}, u32[]{:S(2)}) collective-permute-start(bf16[256,256]{1,0:T(8,128)(2,1)S(1)} %get-tuple-element.22), channel_id=1, source_target_pairs={{0,64},{16,80},{32,96},{48,112},{64,0},{80,16},{96,32},{112,48},{1... | collective-permute-start | bytes 393224 | tf_op jit(solution)/shard_map/ppermute | solution.py:515
  68.4 2.6 %collective-permute-done.2.recv_ref = bf16[256,256]{1,0:T(8,128)(2,1)S(1)} collective-permute-done((bf16[256,256]{1,0:T(8,128)(2,1)S(1)}, bf16[256,256]{1,0:T(8,128)(2,1)S(1)}, u32[]{:S(2)}, u32[]{:S(2)}) %collective-permute-start.2) | collective-permute-done | bytes 131104 | tf_op jit(solution)/shard_map/ppermute | solution.py:515
  71.0 5.5 %last.1 = bf16[4,528,256]{2,1,0:T(8,128)(2,1)S(1)} custom-call(bf16[4,256,256]{2,1,0:T(8,128)(2,1)S(1)} %bitcast.13, bf16[256,256]{1,0:T(8,128)(2,1)S(1)} %collective-permute-done.2.recv_ref, bf16[4,256,256]{2,1,0:T(8,128)(2,1)S(1)} %get-tuple-element.23.xs_any, f32[4,256,256]{2,1,0:T(8,128)S(1)} %get-tuple-element.24.conv_any, ...), custom_call_target="tpu_custom_call" | custom-call | tf_op jit(solution)/shard_map/last/pallas_call | solution.py:336
  76.5 0.0 copy-start.3
  76.5 0.0 copy-start.6
  76.5 15.4 %all_to_all.21.r_ref = bf16[4,528,256]{2,1,0:T(8,128)(2,1)S(1)} all-to-all(bf16[4,528,256]{2,1,0:T(8,128)(2,1)S(1)} %last.1), channel_id=1, replica_groups={{0,16,32,48},{64,80,96,112},{1,17,33,49},{65,81,97,113},{2,18,34,50},{6..., dimensions={0} | all-to-all | bytes 2162688 | tf_op jit(solution)/shard_map/all_to_all | solution.py:518
  91.9 0.0 copy-done.3
  91.9 0.0 copy-done.6
  91.9 3.0 %gradients.1 = (bf16[1152,256]{1,0:T(8,128)(2,1)S(1)}, bf16[1168,256]{1,0:T(8,128)(2,1)S(1)}, bf16[16,256]{1,0:T(8,128)(2,1)S(1)}, f32[8,512]{1,0:T(8,128)S(1)}) custom-call(bf16[4,528,256]{2,1,0:T(8,128)(2,1)S(1)} %all_to_all.21.r_ref, bf16[2304,256]{1,0:T(8,128)(2,1)S(1)} %bitcast.11, f32[8,256]{1,0:T(8,128)S(1)} %get-tuple-element.25.styles_ref, ...), custom_call_target="tpu_custom_call" | custom-call | tf_op jit(solution)/shard_map/gradients/pallas_call | solution.py:403
  94.9 3.6 %collective-permute-start.3 = (bf16[1168,256]{1,0:T(8,128)(2,1)S(1)}, bf16[1168,256]{1,0:T(8,128)(2,1)S(1)}, u32[]{:S(2)}, u32[]{:S(2)}) collective-permute-start(bf16[1168,256]{1,0:T(8,128)(2,1)S(1)} %get-tuple-element.30), channel_id=1, source_target_pairs={{0,1},{1,0},{2,3},{3,2},{4,5},{5,4},{6,7},{7,6},{8,9},{9,8},{10,11... | collective-permute-start | bytes 1794056 | tf_op jit(solution)/shard_map/ppermute | solution.py:521
  98.4 2.8 %collective-permute-start.4 = (f32[4,512]{1,0:T(4,128)S(1)}, f32[4,512]{1,0:T(4,128)S(1)}, u32[]{:S(2)}, u32[]{:S(2)}) collective-permute-start(f32[4,512]{1,0:T(4,128)S(1)} %slice.3), channel_id=1, source_target_pairs={{0,64},{16,80},{32,96},{48,112},{64,0},{80,16},{96,32},{112,48},{1... | collective-permute-start | bytes 24584 | tf_op jit(solution)/shard_map/ppermute | solution.py:523
  101.2 1.3 collective-permute-done.4
  102.5 0.0 collective-permute-done.3.got_ref
  102.5 1.0 pair.1
  103.5 5.1 %all-to-all-start.2 = ((bf16[8,176,256]{2,1,0:T(8,128)(2,1)}), bf16[8,176,256]{2,1,0:T(8,128)(2,1)S(1)}, u32[]{:S(2)}, u32[]{:S(2)}) async-start(bf16[8,176,256]{2,1,0:T(8,128)(2,1)} %pair.1), calls=%async_computation.2 | async-start | bytes 1441792 | tf_op jit(solution)/shard_map/all_to_all | solution.py:526
  108.6 0.3 collective-permute-start.5
  108.9 2.2 %collective-permute-done.5 = f32[4,512]{1,0:T(4,128)S(1)} collective-permute-done((f32[4,512]{1,0:T(4,128)S(1)}, f32[4,512]{1,0:T(4,128)S(1)}, u32[]{:S(2)}, u32[]{:S(2)}) %collective-permute-start.5) | collective-permute-done | bytes 8224 | tf_op jit(solution)/shard_map/ppermute | solution.py:527
  111.1 8.2 %all-to-all-done.2.shares_ref = bf16[8,176,256]{2,1,0:T(8,128)(2,1)S(1)} async-done(((bf16[8,176,256]{2,1,0:T(8,128)(2,1)}), bf16[8,176,256]{2,1,0:T(8,128)(2,1)S(1)}, u32[]{:S(2)}, u32[]{:S(2)}) %all-to-all-start.2) | async-done | bytes 720928 | tf_op jit(solution)/shard_map/all_to_all | solution.py:526
  119.3 0.1 share.1
  119.4 10.8 %all_to_all.22 = bf16[8,144,256]{2,1,0:T(8,128)(2,1)S(1)} all-to-all(bf16[8,144,256]{2,1,0:T(8,128)(2,1)S(1)} %share.1), channel_id=1, replica_groups={{0,2,4,6,8,10,12,14},{1,3,5,7,9,11,13,15},{16,18,20,22,24,26,28,30},{17..., dimensions={0} | all-to-all | bytes 1179648 | tf_op jit(solution)/shard_map/all_to_all | solution.py:530
  130.2 3.5 %collective-permute-start.6 = (bf16[1152,256]{1,0:T(8,128)(2,1)S(1)}, bf16[1152,256]{1,0:T(8,128)(2,1)S(1)}, u32[]{:S(2)}, u32[]{:S(2)}) collective-permute-start(bf16[1152,256]{1,0:T(8,128)(2,1)S(1)} %bitcast.19), channel_id=1, source_target_pairs={{0,1},{1,0},{2,3},{3,2},{4,5},{5,4},{6,7},{7,6},{8,9},{9,8},{10,11... | collective-permute-start | bytes 1769480 | tf_op jit(solution)/shard_map/ppermute | solution.py:533
  133.7 0.8 collective-permute-start.7
  134.5 1.1 affine.1
  135.6 2.1 %collective-permute-done.7 = f32[4,512]{1,0:T(4,128)S(1)} collective-permute-done((f32[4,512]{1,0:T(4,128)S(1)}, f32[4,512]{1,0:T(4,128)S(1)}, u32[]{:S(2)}, u32[]{:S(2)}) %collective-permute-start.7) | collective-permute-done | bytes 8224 | tf_op jit(solution)/shard_map/ppermute | solution.py:531
  137.7 0.6 add.16
  138.3 0.0 collective-permute-done.6
  138.3 0.1 broadcast_select_fusion.1
  138.5 0.1 pad_maximum_fusion
  138.6 1.6 %convert.1 = f32[1,3,3,256,256]{4,3,2,1,0:T(8,128)} convert(bf16[1,3,3,256,256]{4,3,2,1,0:T(8,128)(2,1)S(1)} %bitcast.18) | non-fusion elementwise | flops 589824 | bytes 3538944 | tf_op jit(solution)/shard_map/convert_element_type | solution.py:536
  (3 shorter events, 0.0 us)
Async XLA Ops:
  0.6 1.3 copy-start
  1.9 1.0 copy-start.2
  2.9 0.7 copy-start.5
  3.6 0.7 copy-start.7
  5.7 40.5 %copy-start.4 = (bf16[4,16,16,256]{3,2,1,0:T(8,128)(2,1)S(1)}, bf16[4,16,16,256]{3,2,1,0:T(8,128)(2,1)}, u32[]{:S(2)}) copy-start(bf16[4,16,16,256]{3,2,1,0:T(8,128)(2,1)} %param.6) | copy-start | bytes 1572868
  39.9 6.3 %collective-permute-start = (bf16[4,1168,256]{2,1,0:T(8,128)(2,1)S(1)}, bf16[4,1168,256]{2,1,0:T(8,128)(2,1)S(1)}, u32[]{:S(2)}, u32[]{:S(2)}) collective-permute-start(bf16[4,1168,256]{2,1,0:T(8,128)(2,1)S(1)} %all_to_all.20.a_any), channel_id=1, source_target_pairs={{0,1},{1,0},{2,3},{3,2},{4,5},{5,4},{6,7},{7,6},{8,9},{9,8},{10,11... | collective-permute-start | bytes 7176200 | tf_op jit(solution)/shard_map/ppermute | solution.py:509
  46.2 10.7 %copy-start.1 = (bf16[4,16,16,256]{3,2,1,0:T(8,128)(2,1)S(1)}, bf16[4,16,16,256]{3,2,1,0:T(8,128)(2,1)}, u32[]{:S(2)}) copy-start(bf16[4,16,16,256]{3,2,1,0:T(8,128)(2,1)} %param.11) | copy-start | bytes 1572868
  50.6 6.3 %collective-permute-start.1 = (bf16[256,256]{1,0:T(8,128)(2,1)S(1)}, bf16[256,256]{1,0:T(8,128)(2,1)S(1)}, u32[]{:S(2)}, u32[]{:S(2)}) collective-permute-start(bf16[256,256]{1,0:T(8,128)(2,1)S(1)} %first.1), channel_id=1, source_target_pairs={{0,64},{16,80},{32,96},{48,112},{64,0},{80,16},{96,32},{112,48},{1... | collective-permute-start | bytes 393224 | tf_op jit(solution)/shard_map/ppermute | solution.py:513
  65.6 5.4 %collective-permute-start.2 = (bf16[256,256]{1,0:T(8,128)(2,1)S(1)}, bf16[256,256]{1,0:T(8,128)(2,1)S(1)}, u32[]{:S(2)}, u32[]{:S(2)}) collective-permute-start(bf16[256,256]{1,0:T(8,128)(2,1)S(1)} %get-tuple-element.22), channel_id=1, source_target_pairs={{0,64},{16,80},{32,96},{48,112},{64,0},{80,16},{96,32},{112,48},{1... | collective-permute-start | bytes 393224 | tf_op jit(solution)/shard_map/ppermute | solution.py:515
  76.5 15.5 %copy-start.3 = (f32[1,512,256]{2,1,0:T(8,128)S(1)}, f32[1,512,256]{2,1,0:T(8,128)}, u32[]{:S(2)}) copy-start(f32[1,512,256]{2,1,0:T(8,128)} %param.9) | copy-start | bytes 1572868
  76.5 15.5 %copy-start.6 = (f32[4,512]{1,0:T(4,128)S(1)}, f32[4,512]{1,0:T(4,128)}, u32[]{:S(2)}) copy-start(f32[4,512]{1,0:T(4,128)} %latent_ref.3) | copy-start | bytes 24580
  94.9 7.6 %collective-permute-start.3 = (bf16[1168,256]{1,0:T(8,128)(2,1)S(1)}, bf16[1168,256]{1,0:T(8,128)(2,1)S(1)}, u32[]{:S(2)}, u32[]{:S(2)}) collective-permute-start(bf16[1168,256]{1,0:T(8,128)(2,1)S(1)} %get-tuple-element.30), channel_id=1, source_target_pairs={{0,1},{1,0},{2,3},{3,2},{4,5},{5,4},{6,7},{7,6},{8,9},{9,8},{10,11... | collective-permute-start | bytes 1794056 | tf_op jit(solution)/shard_map/ppermute | solution.py:521
  98.4 4.0 %collective-permute-start.4 = (f32[4,512]{1,0:T(4,128)S(1)}, f32[4,512]{1,0:T(4,128)S(1)}, u32[]{:S(2)}, u32[]{:S(2)}) collective-permute-start(f32[4,512]{1,0:T(4,128)S(1)} %slice.3), channel_id=1, source_target_pairs={{0,64},{16,80},{32,96},{48,112},{64,0},{80,16},{96,32},{112,48},{1... | collective-permute-start | bytes 24584 | tf_op jit(solution)/shard_map/ppermute | solution.py:523
  103.5 15.9 %all-to-all-start.2 = ((bf16[8,176,256]{2,1,0:T(8,128)(2,1)}), bf16[8,176,256]{2,1,0:T(8,128)(2,1)S(1)}, u32[]{:S(2)}, u32[]{:S(2)}) async-start(bf16[8,176,256]{2,1,0:T(8,128)(2,1)} %pair.1), calls=%async_computation.2 | async-start | bytes 1441792 | tf_op jit(solution)/shard_map/all_to_all | solution.py:526
  108.6 2.5 %collective-permute-start.5 = (f32[4,512]{1,0:T(4,128)S(1)}, f32[4,512]{1,0:T(4,128)S(1)}, u32[]{:S(2)}, u32[]{:S(2)}) collective-permute-start(f32[4,512]{1,0:T(4,128)S(1)} %slice_add_fusion), channel_id=1, source_target_pairs={{0,16},{16,0},{32,48},{48,32},{64,80},{80,64},{96,112},{112,96},{1... | collective-permute-start | bytes 24584 | tf_op jit(solution)/shard_map/ppermute | solution.py:527
  130.2 8.1 %collective-permute-start.6 = (bf16[1152,256]{1,0:T(8,128)(2,1)S(1)}, bf16[1152,256]{1,0:T(8,128)(2,1)S(1)}, u32[]{:S(2)}, u32[]{:S(2)}) collective-permute-start(bf16[1152,256]{1,0:T(8,128)(2,1)S(1)} %bitcast.19), channel_id=1, source_target_pairs={{0,1},{1,0},{2,3},{3,2},{4,5},{5,4},{6,7},{7,6},{8,9},{9,8},{10,11... | collective-permute-start | bytes 1769480 | tf_op jit(solution)/shard_map/ppermute | solution.py:533
  133.7 4.0 %collective-permute-start.7 = (f32[4,512]{1,0:T(4,128)S(1)}, f32[4,512]{1,0:T(4,128)S(1)}, u32[]{:S(2)}, u32[]{:S(2)}) collective-permute-start(f32[4,512]{1,0:T(4,128)S(1)} %add.15), channel_id=1, source_target_pairs={{0,32},{16,48},{32,0},{48,16},{64,96},{80,112},{96,64},{112,80},{1... | collective-permute-start | bytes 24584 | tf_op jit(solution)/shard_map/ppermute | solution.py:531

commit v3 on v2

--- a/solution.py
+++ b/solution.py
@@ -78,19 +78,34 @@
     return out
 
 
-def prepare_kernel(latent_ref, affine_ref, w_ref, bias_ref, send_ref, styles_ref, demod_ref, energy_ref, rows_ref, tile_ref, sem):
+def prepare_kernel(
+    latent_hbm, affine_hbm, w_hbm, bias_hbm, send_ref, styles_ref, demod_ref, energy_ref,
+    rows_ref, affine_ref, w_ref, bias_ref, sem,
+):
     _, _, core = place()
     mine = pl.ds(pl.multiple_of(core * HALF, HALF), HALF)
-    copies = [
-        pltpu.make_async_copy(w_ref.at[mine], send_ref.at[k, pl.ds(0, HALF)], sem.at[k]) for k in range(DEPTH)
+    rows_ref[...] = jnp.zeros_like(rows_ref)
+    third = ROWS // 3
+    loads = [
+        pltpu.make_async_copy(affine_hbm, affine_ref, sem.at[0]),
+        pltpu.make_async_copy(latent_hbm, rows_ref.at[pl.ds(0, DEPTH)], sem.at[1]),
+        pltpu.make_async_copy(bias_hbm, bias_ref, sem.at[2]),
+    ] + [
+        pltpu.make_async_copy(w_hbm.at[pl.ds(k * third, third)], w_ref.at[pl.ds(k * third, third)], sem.at[3 + k])
+        for k in range(3)
     ]
-    for copy in copies:
+    sends = [
+        pltpu.make_async_copy(w_hbm.at[mine], send_ref.at[k, pl.ds(0, HALF)], sem.at[6 + k]) for k in range(DEPTH)
+    ]
+    for copy in loads + sends:
         copy.start()
-    rows_ref[...] = jnp.zeros_like(rows_ref)
-    rows_ref[0:DEPTH, :] = latent_ref[...]
+    for copy in loads[:3]:
+        copy.wait()
     styles = jnp.dot(rows_ref[...], affine_ref[...], precision=HI, preferred_element_type=F32) + 1.0
     energy = jnp.zeros((C, C), F32)
     for tap in range(TAPS):
+        if tap % 3 == 0:
+            loads[3 + tap // 3].wait()
         part = w_ref[tap * C : (tap + 1) * C, :].astype(F32)
         energy += part * part
     energy_ref[...] = energy
@@ -98,18 +113,13 @@
     styles_ref[...] = styles
     demod_ref[...] = demod
     for k in range(DEPTH):
-        tile_ref[k] = pack_rows([styles[k : k + 1], demod[k : k + 1], bias_ref[...]])
-    stats = [
-        pltpu.make_async_copy(tile_ref.at[k], send_ref.at[k, pl.ds(HALF, STAT)], sem.at[DEPTH + k])
-        for k in range(DEPTH)
-    ]
-    for copy in stats:
-        copy.start()
-    for copy in copies + stats:
+        send_ref[k, HALF : HALF + STAT, :] = pack_rows([styles[k : k + 1], demod[k : k + 1], bias_ref[...]])
+    for copy in sends:
         copy.wait()
 
 
 def prepare(latent, affine, w, bias):
+    far = [pltpu.with_memory_space_constraint(value, pltpu.HBM) for value in (latent, affine, w, bias)]
     return pl.pallas_call(
         prepare_kernel,
         out_shape=(
@@ -118,16 +128,18 @@
             jax.ShapeDtypeStruct((8, C), F32),
             jax.ShapeDtypeStruct((C, C), F32),
         ),
-        in_specs=[vmem_spec()] * 4,
-        out_specs=(any_spec(), vmem_spec(), vmem_spec(), vmem_spec()),
+        in_specs=[pl.BlockSpec(memory_space=pltpu.HBM)] * 4,
+        out_specs=(vmem_spec(),) * 4,
         scratch_shapes=[
             pltpu.VMEM((8, latent.shape[1]), F32),
-            pltpu.VMEM((DEPTH, STAT, C), BF),
-            pltpu.SemaphoreType.DMA((2 * DEPTH,)),
+            pltpu.VMEM(affine.shape, F32),
+            pltpu.VMEM((ROWS, C), BF),
+            pltpu.VMEM((1, C), F32),
+            pltpu.SemaphoreType.DMA((6 + DEPTH,)),
         ],
         compiler_params=params(),
         name="prepare",
-    )(latent, affine, w, bias)
+    )(*far)
 
 
 def weight_copies(a_any, b_any, w_buf, stat_buf, sem):
@@ -157,16 +169,13 @@
     pad_ref[2, ROW : ROW + PX, :] = jnp.where(column == ROW - 1, 0.0, pltpu.roll(value, PX - 1, 0)).astype(BF)
 
 
-def forward_layer(x, l, w_buf, stat, pad_ref):
+def forward_layer(x, l, w_ref, stat, pad_ref):
     styles, demod, bias = stat
-    scaled = (x.astype(F32) * styles).astype(BF).astype(F32)
-    spread(pad_ref, scaled)
-    conv = None
-    for ky in range(3):
-        lhs = jnp.concatenate([pad_ref[kx, ky * ROW : ky * ROW + PX, :] for kx in range(3)], axis=1)
-        part = jnp.dot(lhs, w_buf[l, ky * 3 * C : (ky + 1) * 3 * C, :], preferred_element_type=F32)
-        conv = part if conv is None else conv + part
-    return conv
+    spread(pad_ref, (x.astype(F32) * styles).astype(BF).astype(F32))
+    lhs = jnp.concatenate(
+        [pad_ref[kx, ky * ROW : ky * ROW + PX, :] for ky in range(3) for kx in range(3)], axis=1
+    )
+    return jnp.dot(lhs, w_ref[l], preferred_element_type=F32)
 
 
 def activate(conv, stat):
@@ -175,7 +184,7 @@
     return (GAIN * hidden * (0.6 + 0.4 * jnp.tanh(hidden))).astype(BF)
 
 
-def backward_layer(upstream, x, conv, l, w_buf, stat, pad_ref, send_ref):
+def backward_layer(upstream, x, conv, l, flip_ref, stat, pad_ref, send_ref):
     styles, demod, bias = stat
     hidden = conv * demod + bias
     t = jnp.tanh(hidden)
@@ -185,15 +194,10 @@
     grad_conv = (dh * demod).astype(BF).astype(F32)
     spread(pad_ref, grad_conv)
     send_ref[l, PX : 2 * PX, :] = pad_ref[1, ROW : ROW + PX, :]
-    total = None
-    for ky in range(3):
-        for kx in range(3):
-            lhs = pad_ref[2 - kx, (2 - ky) * ROW : (2 - ky) * ROW + PX, :]
-            tap = ky * 3 + kx
-            part = lax.dot_general(
-                lhs, w_buf[l, tap * C : (tap + 1) * C, :], (((1,), (1,)), ((), ())), preferred_element_type=F32
-            )
-            total = part if total is None else total + part
+    lhs = jnp.concatenate(
+        [pad_ref[2 - kx, (2 - ky) * ROW : (2 - ky) * ROW + PX, :] for ky in range(3) for kx in range(3)], axis=1
+    )
+    total = jnp.dot(lhs, flip_ref[l], preferred_element_type=F32)
     grad_scaled = total.astype(BF).astype(F32)
     xf = x.astype(F32)
     grad_styles = jnp.sum(grad_scaled * xf, axis=0, keepdims=True)
@@ -202,11 +206,11 @@
     return (grad_scaled * styles).astype(BF)
 
 
-def first_kernel(images_any, a_any, b_any, out_ref, w_buf, stat_buf, x_buf, pad_ref, sem, x_sem):
+def first_kernel(images_any, a_ref, b_ref, out_ref, w_ref, stat_ref, x_buf, pad_ref, sem, x_sem):
     _, z, _ = place()
     x_copy = pltpu.make_async_copy(images_any.at[z], x_buf, x_sem)
     x_copy.start()
-    copies = weight_copies(a_any, b_any, w_buf, stat_buf, sem)
+    copies = weight_copies(a_ref, b_ref, w_ref, stat_ref, sem)
     for group in copies:
         for copy in group:
             copy.start()
@@ -216,88 +220,69 @@
     for l in range(DEPTH):
         for copy in copies[l]:
             copy.wait()
-        stat = unpack_rows(stat_buf[l])
-        x = activate(forward_layer(x, l, w_buf, stat, pad_ref), stat)
+        stat = unpack_rows(stat_ref[l])
+        x = activate(forward_layer(x, l, w_ref, stat, pad_ref), stat)
     out_ref[...] = x
 
 
+def flip_kernel(w_ref, flip_ref):
+    for l in range(DEPTH):
+        for tap in range(TAPS):
+            at = slice(tap * C, (tap + 1) * C)
+            flip_ref[l, at, :] = w_ref[l, at, :].T
+
+
 def middle_kernel(
-    images_any, cot_any, recv_ref, a_any, b_any, dx_ref, xs_ref, conv_ref, send_ref,
-    w_buf, stat_buf, x_buf, u_buf, pad_ref, sem, x_sem,
+    images_any, cot_any, recv_ref, w_ref, flip_ref, stat_ref, dx_ref, xs_ref, conv_ref, send_ref,
+    x_buf, u_buf, pad_ref, x_sem,
 ):
     half, z, _ = place()
     x_copy = pltpu.make_async_copy(images_any.at[z], x_buf, x_sem.at[0])
     u_copy = pltpu.make_async_copy(cot_any.at[z], u_buf, x_sem.at[1])
     x_copy.start()
-    copies = weight_copies(a_any, b_any, w_buf, stat_buf, sem)
-    for group in copies:
-        for copy in group:
-            copy.start()
     u_copy.start()
     clear_pads(pad_ref)
     x_copy.wait()
     x = jnp.where(half == 1, recv_ref[...], x_buf[...])
     stats = []
     for l in range(DEPTH):
-        for copy in copies[l]:
-            copy.wait()
-        stats.append(unpack_rows(stat_buf[l]))
+        stats.append(unpack_rows(stat_ref[l]))
         xs_ref[l] = x
-        conv = forward_layer(x, l, w_buf, stats[l], pad_ref)
+        conv = forward_layer(x, l, w_ref, stats[l], pad_ref)
         conv_ref[l] = conv
         if l < DEPTH - 1:
             x = activate(conv, stats[l])
     u_copy.wait()
     upstream = u_buf[...]
     for l in reversed(range(DEPTH)):
-        upstream = backward_layer(upstream, xs_ref[l], conv_ref[l], l, w_buf, stats[l], pad_ref, send_ref)
+        upstream = backward_layer(upstream, xs_ref[l], conv_ref[l], l, flip_ref, stats[l], pad_ref, send_ref)
     dx_ref[...] = upstream
 
 
-def last_kernel(
-    cot_any, recv_ref, xs_any, conv_any, a_any, b_any, send_ref,
-    w_buf, stat_buf, xs_buf, conv_buf, u_buf, pad_ref, sem, s_sem, u_sem,
-):
+def last_kernel(cot_any, recv_ref, xs_ref, conv_ref, flip_ref, stat_ref, send_ref, u_buf, pad_ref, u_sem):
     half, z, _ = place()
     u_copy = pltpu.make_async_copy(cot_any.at[z], u_buf, u_sem)
     u_copy.start()
-    copies = weight_copies(a_any, b_any, w_buf, stat_buf, sem)
-    saves = [
-        (
-            pltpu.make_async_copy(xs_any.at[l], xs_buf.at[l], s_sem.at[0, l]),
-            pltpu.make_async_copy(conv_any.at[l], conv_buf.at[l], s_sem.at[1, l]),
-        )
-        for l in range(DEPTH)
-    ]
-    for l in reversed(range(DEPTH)):
-        for copy in saves[l] + copies[l]:
-            copy.start()
     clear_pads(pad_ref)
     u_copy.wait()
     upstream = jnp.where(half == 1, u_buf[...], recv_ref[...])
     for l in reversed(range(DEPTH)):
-        for copy in saves[l] + copies[l]:
-            copy.wait()
-        stat = unpack_rows(stat_buf[l])
-        upstream = backward_layer(upstream, xs_buf[l], conv_buf[l], l, w_buf, stat, pad_ref, send_ref)
-
-
-def weight_scratch():
-    return [pltpu.VMEM((DEPTH, ROWS, C), BF), pltpu.VMEM((DEPTH, STAT, C), BF)]
+        stat = unpack_rows(stat_ref[l])
+        upstream = backward_layer(upstream, xs_ref[l], conv_ref[l], l, flip_ref, stat, pad_ref, send_ref)
 
 
 MAP = jax.ShapeDtypeStruct((PX, C), BF)
+KERNELS = jax.ShapeDtypeStruct((DEPTH, ROWS, C), BF)
 SENT = jax.ShapeDtypeStruct((DEPTH, 2 * PX + STAT, C), BF)
 
 
 def first(images, a, b):
     return pl.pallas_call(
         first_kernel,
-        out_shape=MAP,
+        out_shape=(MAP, KERNELS, jax.ShapeDtypeStruct((DEPTH, STAT, C), BF)),
         in_specs=[any_spec(), vmem_spec(), vmem_spec()],
-        out_specs=vmem_spec(),
-        scratch_shapes=weight_scratch()
-        + [
+        out_specs=(vmem_spec(),) * 3,
+        scratch_shapes=[
             pltpu.VMEM((PX, C), BF),
             pltpu.VMEM((3, PAD, C), BF),
             pltpu.SemaphoreType.DMA((3, DEPTH)),
@@ -308,7 +293,18 @@
     )(images, a, b)
 
 
-def middle(images, cot, recv, a, b):
+def flip(w):
+    return pl.pallas_call(
+        flip_kernel,
+        out_shape=KERNELS,
+        in_specs=[vmem_spec()],
+        out_specs=vmem_spec(),
+        compiler_params=params(),
+        name="flip",
+    )(w)
+
+
+def middle(images, cot, recv, w, flipped, stat):
     return pl.pallas_call(
         middle_kernel,
         out_shape=(
@@ -317,40 +313,33 @@
             jax.ShapeDtypeStruct((DEPTH, PX, C), F32),
             SENT,
         ),
-        in_specs=[any_spec(), any_spec(), vmem_spec(), vmem_spec(), vmem_spec()],
+        in_specs=[any_spec(), any_spec()] + [vmem_spec()] * 4,
         out_specs=(vmem_spec(),) * 4,
-        scratch_shapes=weight_scratch()
-        + [
+        scratch_shapes=[
             pltpu.VMEM((PX, C), BF),
             pltpu.VMEM((PX, C), BF),
             pltpu.VMEM((3, PAD, C), BF),
-            pltpu.SemaphoreType.DMA((3, DEPTH)),
             pltpu.SemaphoreType.DMA((2,)),
         ],
         compiler_params=params(),
         name="middle",
-    )(images, cot, recv, a, b)
-
-
-def last(cot, recv, xs, conv, a, b):
+    )(images, cot, recv, w, flipped, stat)
+
+
+def last(cot, recv, xs, conv, flipped, stat):
     return pl.pallas_call(
         last_kernel,
         out_shape=SENT,
-        in_specs=[any_spec(), vmem_spec(), any_spec(), any_spec(), vmem_spec(), vmem_spec()],
+        in_specs=[any_spec()] + [vmem_spec()] * 5,
         out_specs=vmem_spec(),
-        scratch_shapes=weight_scratch()
-        + [
-            pltpu.VMEM((DEPTH, PX, C), BF),
-            pltpu.VMEM((DEPTH, PX, C), F32),
+        scratch_shapes=[
             pltpu.VMEM((PX, C), BF),
             pltpu.VMEM((3, PAD, C), BF),
-            pltpu.SemaphoreType.DMA((3, DEPTH)),
-            pltpu.SemaphoreType.DMA((2, DEPTH)),
             pltpu.SemaphoreType.DMA,
         ],
         compiler_params=params(),
         name="last",
-    )(cot, recv, xs, conv, a, b)
+    )(cot, recv, xs, conv, flipped, stat)
 
 
 def gradient_kernel(
@@ -490,11 +479,39 @@
     )(shares)
 
 
+def own_kernel(mine_ref, out_any, wide_ref, sem):
+    _, _, core = place()
+    wide_ref[...] = mine_ref[...].astype(F32)
+    copy = pltpu.make_async_copy(wide_ref, out_any.at[pl.ds(pl.multiple_of(core * HALF, HALF), HALF)], sem)
+    copy.start()
+    copy.wait()
+
+
+def rest_kernel(other_ref, _, out_any, wide_ref, sem):
+    _, _, core = place()
+    wide_ref[...] = other_ref[...].astype(F32)
+    copy = pltpu.make_async_copy(wide_ref, out_any.at[pl.ds(pl.multiple_of((1 - core) * HALF, HALF), HALF)], sem)
+    copy.start()
+    copy.wait()
+
+
+def widen(kernel, name, *args):
+    return pl.pallas_call(
+        kernel,
+        out_shape=jax.ShapeDtypeStruct((ROWS, C), F32),
+        in_specs=[vmem_spec(), pl.BlockSpec(memory_space=pltpu.HBM)][: len(args)],
+        out_specs=pl.BlockSpec(memory_space=pltpu.HBM),
+        input_output_aliases={1: 0} if len(args) == 2 else {},
+        scratch_shapes=[pltpu.VMEM((HALF, C), F32), pltpu.SemaphoreType.DMA],
+        compiler_params=params(),
+        name=name,
+    )(*args)
+
+
 def body(images, latent, weight, affine, biases, cotangent):
     width = latent.shape[1]
     replicas = lax.axis_size("dp")
     segments = lax.axis_size("segment")
-    core = lax.axis_index("dp") % 2
     planes = [list(range(k, k + DEPTH)) for k in range(0, segments, DEPTH)]
     across = [(i, (i + DEPTH) % segments) for i in range(segments)]
     sibling = [(i, i ^ 1) for i in range(replicas)]
@@ -509,31 +526,28 @@
     b = near(lax.ppermute(a, "dp", sibling))
     a = near(a)
 
-    act = first(images, a, b)
+    act, kernels, stat = first(images, a, b)
+    flipped = flip(kernels)
     arrived = near(lax.ppermute(act, "segment", across))
-    dx, xs, conv, _ = middle(images, cotangent, arrived, a, b)
+    dx, xs, conv, _ = middle(images, cotangent, arrived, kernels, flipped, stat)
     returned = near(lax.ppermute(dx, "segment", across))
-    sent = last(cotangent, returned, xs, conv, a, b)
+    sent = last(cotangent, returned, xs, conv, flipped, stat)
 
     r = near(lax.all_to_all(sent, "segment", 0, 0, axis_index_groups=planes))
     keep, give, extra, latent_part = gradients(r, w, styles, demod, energy, affine[0], latent)
 
     got = near(lax.ppermute(give, "dp", sibling))
-    part = latent_part[:DEPTH]
+    shared, part = lax.optimization_barrier((pair(keep, extra, got), latent_part[:DEPTH]))
+    shares = near(lax.all_to_all(shared, "dp", 0, 0, axis_index_groups=cores))
     part = part + lax.ppermute(part, "segment", across)
-    shared = pair(keep, extra, got)
-    shared, part = lax.optimization_barrier((shared, part))
-    shares = near(lax.all_to_all(shared, "dp", 0, 0, axis_index_groups=cores))
     part = part + lax.ppermute(part, "segment", [(i, i ^ 1) for i in range(segments)])
-    spread_share = share(shares)
-    spread_share, part = lax.optimization_barrier((spread_share, part))
+    spread_share, part = lax.optimization_barrier((share(shares), part))
     mine = lax.all_to_all(spread_share, "dp", 0, 0, axis_index_groups=cores).reshape(HALF, C)
     grad_latent = part + lax.ppermute(part, "segment", [(i, i ^ 2) for i in range(segments)])
+    mine, grad_latent = lax.optimization_barrier((mine, grad_latent))
+    other = near(lax.ppermute(mine, "dp", sibling))
     grad_affine, grad_bias = affine_gradient(shares, width)
-    other = lax.ppermute(mine, "dp", sibling)
-    low = jnp.where(core == 0, mine, other)
-    high = jnp.where(core == 0, other, mine)
-    grad_weight = jnp.concatenate([low, high], axis=0).astype(F32).reshape(weight.shape)
+    grad_weight = widen(rest_kernel, "rest", other, widen(own_kernel, "own", near(mine))).reshape(weight.shape)
     return (grad_weight, grad_affine[None], grad_bias, grad_latent)
 
 

time: 141 us -> 135 us (0.957)
  blocking collectives: 60.4 us -> 49.6 us
  starting transfers between devices: 23.8 us -> 28.4 us
  local copies, waits for them, and re-layouts: 3.7 us -> 0.03 us
  waiting for transfers between devices: 24.1 us -> 27.7 us
  Pallas kernels: 25.1 us -> 27.2 us
  other arithmetic: 2.44 us -> 0.61 us
    all_to_all x1 -> x0, blocking collectives: 10.8 us -> none  [body(): lax.all_to_all(spread_share, 'dp', 0, 0, axis_index_groups=cores)]
    all_to_all x1, waiting for transfers between devices: 8.23 us -> 0.01 us  [body(): shares = near(lax.all_to_all(shared, 'dp', 0, 0, axis_index_groups=cores))]
    ppermute x1, waiting for transfers between devices: 1.26 us -> 8.29 us  [body(): part = part + lax.ppermute(part, 'segment', across)]
    all_to_all x0 -> x1, starting transfers between devices: none -> 4.17 us  [body(): lax.all_to_all(spread_share, 'dp', 0, 0, axis_index_groups=cores)]
    unnamed x16 -> x10, local copies, waits for them, and re-layouts: 3.7 us -> 0.03 us
    all_to_all x0 -> x1, waiting for transfers between devices: none -> 3.4 us  [body(): lax.all_to_all(spread_share, 'dp', 0, 0, axis_index_groups=cores)]
    ppermute x1, waiting for transfers between devices: 0.01 us -> 1.64 us  [body(): got = near(lax.ppermute(give, 'dp', sibling))]
    convert_element_type x1 -> x0, other arithmetic: 1.63 us -> none  [body(): jnp.concatenate([low, high], axis=0).astype(F32).reshape(weight.shape)]
  transfers between devices with their start and end apart: 9 -> 10, of which waited for: 7 -> 8; matrix products, arithmetic and copies ran while one was open for 0% -> 0% of each run, Pallas kernels for 1% -> 3%
where the time goes in v3:
time: 135 us; the launch traced here: 134 us
  blocking collectives  49.6 us (37%)
  starting transfers between devices  28.4 us (21%)
  waiting for transfers between devices  27.7 us (21%)
  Pallas kernels  27.2 us (20%)
    all_to_all x1, blocking collectives, body(): a = lax.all_to_all(send, 'segment', 0, 0, axis_index_groups=planes)  34.2 us
    all_to_all x1, blocking collectives, body(): r = near(lax.all_to_all(sent, 'segment', 0, 0, axis_index_groups=planes))  15.4 us
    ppermute x1, waiting for transfers between devices, body(): part = part + lax.ppermute(part, 'segment', across)  8.29 us
    pallas_call x1, Pallas kernels, middle(): pl.pallas_call(middle_kernel, out_shape=(MAP, jax.ShapeDtypeStruct((DEPTH...  7.61 us
    all_to_all x1, starting transfers between devices, body(): shares = near(lax.all_to_all(shared, 'dp', 0, 0, axis_index_groups=cores))  5.12 us
    pallas_call x1, Pallas kernels, first(): pl.pallas_call(first_kernel, out_shape=(MAP, KERNELS, jax.ShapeDtypeStruc...  4.37 us
    ppermute x1, starting transfers between devices, body(): other = near(lax.ppermute(mine, 'dp', sibling))  4.28 us
    ppermute x1, waiting for transfers between devices, body(): b = near(lax.ppermute(a, 'dp', sibling))  4.21 us
  transfers between devices with their start and end apart: 10, of which 8 were waited for; matrix products, arithmetic and copies ran while one was open for 0% of the time, Pallas kernels for 3%

profile of v3, /device:TPU:1, one launch (start us, length us, event | category | flops | bytes accessed | tf_op | source)
XLA Modules:
  0.0 134.5 jit_solution(3389546170642382354)
XLA Ops:
  0.6 2.5 %prepare.1 = (bf16[4,1168,256]{2,1,0:T(8,128)(2,1)S(1)}, f32[8,256]{1,0:T(8,128)S(1)}, f32[8,256]{1,0:T(8,128)S(1)}, f32[256,256]{1,0:T(8,128)S(1)}) custom-call(f32[4,512]{1,0:T(4,128)} %latent_ref.1, f32[512,256]{1,0:T(8,128)} %bitcast.11, bf16[2304,256]{1,0:T(8,128)(2,1)} %bitcast.7, f32[1,256]{1,0:T(1,128)} %bias_hbm.1), custom_call_target="tpu_custom_call" | custom-call | tf_op jit(solution)/shard_map/prepare/pallas_call | solution.py:123
  3.1 0.0 copy-start.2
  3.1 34.2 %all_to_all.20.a_ref = bf16[4,1168,256]{2,1,0:T(8,128)(2,1)S(1)} all-to-all(bf16[4,1168,256]{2,1,0:T(8,128)(2,1)S(1)} %get-tuple-element.26), channel_id=1, replica_groups={{0,16,32,48},{64,80,96,112},{1,17,33,49},{65,81,97,113},{2,18,34,50},{6..., dimensions={0} | all-to-all | bytes 4784128 | tf_op jit(solution)/shard_map/all_to_all | solution.py:525
  37.3 2.1 %collective-permute-start = (bf16[4,1168,256]{2,1,0:T(8,128)(2,1)S(1)}, bf16[4,1168,256]{2,1,0:T(8,128)(2,1)S(1)}, u32[]{:S(2)}, u32[]{:S(2)}) collective-permute-start(bf16[4,1168,256]{2,1,0:T(8,128)(2,1)S(1)} %all_to_all.20.a_ref), channel_id=1, source_target_pairs={{0,1},{1,0},{2,3},{3,2},{4,5},{5,4},{6,7},{7,6},{8,9},{9,8},{10,11... | collective-permute-start | bytes 7176200 | tf_op jit(solution)/shard_map/ppermute | solution.py:526
  39.3 4.2 %collective-permute-done.b_ref = bf16[4,1168,256]{2,1,0:T(8,128)(2,1)S(1)} collective-permute-done((bf16[4,1168,256]{2,1,0:T(8,128)(2,1)S(1)}, bf16[4,1168,256]{2,1,0:T(8,128)(2,1)S(1)}, u32[]{:S(2)}, u32[]{:S(2)}) %collective-permute-start) | collective-permute-done | bytes 2392096 | tf_op jit(solution)/shard_map/ppermute | solution.py:526
  43.5 0.0 copy-done.2
  43.6 4.4 %first.1 = (bf16[256,256]{1,0:T(8,128)(2,1)S(1)}, bf16[4,2304,256]{2,1,0:T(8,128)(2,1)S(1)}, bf16[4,16,256]{2,1,0:T(8,128)(2,1)S(1)}) custom-call(bf16[4,256,256]{2,1,0:T(8,128)(2,1)S(1)} %bitcast.13, bf16[4,1168,256]{2,1,0:T(8,128)(2,1)S(1)} %all_to_all.20.a_ref, bf16[4,1168,256]{2,1,0:T(8,128)(2,1)S(1)} %collective-permute-done.b_ref), custom_call_target="tpu_custom_call" | custom-call | tf_op jit(solution)/shard_map/first/pallas_call | solution.py:280
  47.9 2.8 %collective-permute-start.1 = (bf16[256,256]{1,0:T(8,128)(2,1)S(1)}, bf16[256,256]{1,0:T(8,128)(2,1)S(1)}, u32[]{:S(2)}, u32[]{:S(2)}) collective-permute-start(bf16[256,256]{1,0:T(8,128)(2,1)S(1)} %get-tuple-element.27), channel_id=1, source_target_pairs={{0,64},{16,80},{32,96},{48,112},{64,0},{80,16},{96,32},{112,48},{1... | collective-permute-start | bytes 393224 | tf_op jit(solution)/shard_map/ppermute | solution.py:531
  50.8 0.0 copy-start.3
  50.8 1.3 flip.1.flip_ref
  52.0 2.2 %collective-permute-done.1.recv_ref = bf16[256,256]{1,0:T(8,128)(2,1)S(1)} collective-permute-done((bf16[256,256]{1,0:T(8,128)(2,1)S(1)}, bf16[256,256]{1,0:T(8,128)(2,1)S(1)}, u32[]{:S(2)}, u32[]{:S(2)}) %collective-permute-start.1) | collective-permute-done | bytes 131104 | tf_op jit(solution)/shard_map/ppermute | solution.py:531
  54.2 0.0 copy-done.3
  54.2 7.6 %middle.1 = (bf16[256,256]{1,0:T(8,128)(2,1)S(1)}, bf16[4,256,256]{2,1,0:T(8,128)(2,1)S(1)}, f32[4,256,256]{2,1,0:T(8,128)S(1)}, bf16[4,528,256]{2,1,0:T(8,128)(2,1)}) custom-call(bf16[4,256,256]{2,1,0:T(8,128)(2,1)S(1)} %bitcast.14, bf16[4,256,256]{2,1,0:T(8,128)(2,1)S(1)} %bitcast.15, bf16[256,256]{1,0:T(8,128)(2,1)S(1)} %collective-permute-done.1.recv_ref, ...), custom_call_target="tpu_custom_call" | custom-call | tf_op jit(solution)/shard_map/middle/pallas_call | solution.py:308
  61.8 2.8 %collective-permute-start.2 = (bf16[256,256]{1,0:T(8,128)(2,1)S(1)}, bf16[256,256]{1,0:T(8,128)(2,1)S(1)}, u32[]{:S(2)}, u32[]{:S(2)}) collective-permute-start(bf16[256,256]{1,0:T(8,128)(2,1)S(1)} %get-tuple-element.30), channel_id=1, source_target_pairs={{0,64},{16,80},{32,96},{48,112},{64,0},{80,16},{96,32},{112,48},{1... | collective-permute-start | bytes 393224 | tf_op jit(solution)/shard_map/ppermute | solution.py:533
  64.7 2.6 %collective-permute-done.2.recv_ref = bf16[256,256]{1,0:T(8,128)(2,1)S(1)} collective-permute-done((bf16[256,256]{1,0:T(8,128)(2,1)S(1)}, bf16[256,256]{1,0:T(8,128)(2,1)S(1)}, u32[]{:S(2)}, u32[]{:S(2)}) %collective-permute-start.2) | collective-permute-done | bytes 131104 | tf_op jit(solution)/shard_map/ppermute | solution.py:533
  67.2 0.0 copy-start.4
  67.2 3.4 %last.1 = bf16[4,528,256]{2,1,0:T(8,128)(2,1)S(1)} custom-call(bf16[4,256,256]{2,1,0:T(8,128)(2,1)S(1)} %bitcast.16, bf16[256,256]{1,0:T(8,128)(2,1)S(1)} %collective-permute-done.2.recv_ref, bf16[4,256,256]{2,1,0:T(8,128)(2,1)S(1)} %get-tuple-element.31.xs_ref, f32[4,256,256]{2,1,0:T(8,128)S(1)} %get-tuple-element.32.conv_ref, ...), custom_call_target="tpu_custom_call" | custom-call | tf_op jit(solution)/shard_map/last/pallas_call | solution.py:330
  70.7 0.0 copy-start
  70.7 0.0 copy-start.1
  70.7 15.4 %all_to_all.21.r_ref = bf16[4,528,256]{2,1,0:T(8,128)(2,1)S(1)} all-to-all(bf16[4,528,256]{2,1,0:T(8,128)(2,1)S(1)} %last.1), channel_id=1, replica_groups={{0,16,32,48},{64,80,96,112},{1,17,33,49},{65,81,97,113},{2,18,34,50},{6..., dimensions={0} | all-to-all | bytes 2162688 | tf_op jit(solution)/shard_map/all_to_all | solution.py:536
  86.1 0.0 copy-done.4
  86.1 0.0 copy-done
  86.1 0.0 copy-done.1
  86.2 3.0 %gradients.1 = (bf16[1152,256]{1,0:T(8,128)(2,1)S(1)}, bf16[1168,256]{1,0:T(8,128)(2,1)S(1)}, bf16[16,256]{1,0:T(8,128)(2,1)S(1)}, f32[8,512]{1,0:T(8,128)S(1)}) custom-call(bf16[4,528,256]{2,1,0:T(8,128)(2,1)S(1)} %all_to_all.21.r_ref, bf16[2304,256]{1,0:T(8,128)(2,1)S(1)} %bitcast.8, f32[8,256]{1,0:T(8,128)S(1)} %get-tuple-element.33.styles_ref, ...), custom_call_target="tpu_custom_call" | custom-call | tf_op jit(solution)/shard_map/gradients/pallas_call | solution.py:392
  89.1 3.6 %collective-permute-start.3 = (bf16[1168,256]{1,0:T(8,128)(2,1)S(1)}, bf16[1168,256]{1,0:T(8,128)(2,1)S(1)}, u32[]{:S(2)}, u32[]{:S(2)}) collective-permute-start(bf16[1168,256]{1,0:T(8,128)(2,1)S(1)} %get-tuple-element.38), channel_id=1, source_target_pairs={{0,1},{1,0},{2,3},{3,2},{4,5},{5,4},{6,7},{7,6},{8,9},{9,8},{10,11... | collective-permute-start | bytes 1794056 | tf_op jit(solution)/shard_map/ppermute | solution.py:539
  92.7 1.6 %collective-permute-done.3.got_ref = bf16[1168,256]{1,0:T(8,128)(2,1)S(1)} collective-permute-done((bf16[1168,256]{1,0:T(8,128)(2,1)S(1)}, bf16[1168,256]{1,0:T(8,128)(2,1)S(1)}, u32[]{:S(2)}, u32[]{:S(2)}) %collective-permute-start.3) | collective-permute-done | bytes 598048 | tf_op jit(solution)/shard_map/ppermute | solution.py:539
  94.3 1.0 pair.1
  95.3 5.1 %all-to-all-start.2 = ((bf16[8,176,256]{2,1,0:T(8,128)(2,1)}), bf16[8,176,256]{2,1,0:T(8,128)(2,1)S(1)}, u32[]{:S(2)}, u32[]{:S(2)}) async-start(bf16[8,176,256]{2,1,0:T(8,128)(2,1)} %pair.1), calls=%async_computation.2 | async-start | bytes 1441792 | tf_op jit(solution)/shard_map/all_to_all | solution.py:541
  100.4 2.4 %collective-permute-start.4 = (f32[4,512]{1,0:T(4,128)S(1)}, f32[4,512]{1,0:T(4,128)S(1)}, u32[]{:S(2)}, u32[]{:S(2)}) collective-permute-start(f32[4,512]{1,0:T(4,128)S(1)} %slice.3), channel_id=1, source_target_pairs={{0,64},{16,80},{32,96},{48,112},{64,0},{80,16},{96,32},{112,48},{1... | collective-permute-start | bytes 24584 | tf_op jit(solution)/shard_map/ppermute | solution.py:542
  102.9 8.3 %collective-permute-done.4 = f32[4,512]{1,0:T(4,128)S(1)} collective-permute-done((f32[4,512]{1,0:T(4,128)S(1)}, f32[4,512]{1,0:T(4,128)S(1)}, u32[]{:S(2)}, u32[]{:S(2)}) %collective-permute-start.4) | collective-permute-done | bytes 8224 | tf_op jit(solution)/shard_map/ppermute | solution.py:542
  111.2 0.3 collective-permute-start.5
  111.5 2.2 %collective-permute-done.5 = f32[4,512]{1,0:T(4,128)S(1)} collective-permute-done((f32[4,512]{1,0:T(4,128)S(1)}, f32[4,512]{1,0:T(4,128)S(1)}, u32[]{:S(2)}, u32[]{:S(2)}) %collective-permute-start.5) | collective-permute-done | bytes 8224 | tf_op jit(solution)/shard_map/ppermute | solution.py:543
  113.7 0.0 all-to-all-done.2.shares_ref
  113.7 0.9 share.1
  114.6 4.2 %all-to-all-start.3 = ((bf16[8,144,256]{2,1,0:T(8,128)(2,1)}), bf16[8,144,256]{2,1,0:T(8,128)(2,1)S(1)}, u32[]{:S(2)}, u32[]{:S(2)}) async-start(bf16[8,144,256]{2,1,0:T(8,128)(2,1)} %share.1), calls=%async_computation.3 | async-start | bytes 1179648 | tf_op jit(solution)/shard_map/all_to_all | solution.py:545
  118.8 0.8 collective-permute-start.6
  119.6 3.2 %collective-permute-done.6 = f32[4,512]{1,0:T(4,128)S(1)} collective-permute-done((f32[4,512]{1,0:T(4,128)S(1)}, f32[4,512]{1,0:T(4,128)S(1)}, u32[]{:S(2)}, u32[]{:S(2)}) %collective-permute-start.6) | collective-permute-done | bytes 8224 | tf_op jit(solution)/shard_map/ppermute | solution.py:546
  122.8 0.6 add.11
  123.4 3.4 %all-to-all-done.3 = bf16[8,144,256]{2,1,0:T(8,128)(2,1)S(1)} async-done(((bf16[8,144,256]{2,1,0:T(8,128)(2,1)}), bf16[8,144,256]{2,1,0:T(8,128)(2,1)S(1)}, u32[]{:S(2)}, u32[]{:S(2)}) %all-to-all-start.3) | async-done | bytes 589856 | tf_op jit(solution)/shard_map/all_to_all | solution.py:545
  126.8 4.3 %collective-permute-start.7 = (bf16[1152,256]{1,0:T(8,128)(2,1)S(1)}, bf16[1152,256]{1,0:T(8,128)(2,1)S(1)}, u32[]{:S(2)}, u32[]{:S(2)}) collective-permute-start(bf16[1152,256]{1,0:T(8,128)(2,1)S(1)} %bitcast.9), channel_id=1, source_target_pairs={{0,1},{1,0},{2,3},{3,2},{4,5},{5,4},{6,7},{7,6},{8,9},{9,8},{10,11... | collective-permute-start | bytes 1769480 | tf_op jit(solution)/shard_map/ppermute | solution.py:548
  131.0 1.1 affine.1
  132.1 1.1 own.1._
  133.2 0.0 collective-permute-done.7.other_ref
  133.2 1.1 rest.1
  (3 shorter events, 0.0 us)
Async XLA Ops:
  3.1 40.5 %copy-start.2 = (bf16[4,16,16,256]{3,2,1,0:T(8,128)(2,1)S(1)}, bf16[4,16,16,256]{3,2,1,0:T(8,128)(2,1)}, u32[]{:S(2)}) copy-start(bf16[4,16,16,256]{3,2,1,0:T(8,128)(2,1)} %param.6) | copy-start | bytes 1572868
  37.3 6.3 %collective-permute-start = (bf16[4,1168,256]{2,1,0:T(8,128)(2,1)S(1)}, bf16[4,1168,256]{2,1,0:T(8,128)(2,1)S(1)}, u32[]{:S(2)}, u32[]{:S(2)}) collective-permute-start(bf16[4,1168,256]{2,1,0:T(8,128)(2,1)S(1)} %all_to_all.20.a_ref), channel_id=1, source_target_pairs={{0,1},{1,0},{2,3},{3,2},{4,5},{5,4},{6,7},{7,6},{8,9},{9,8},{10,11... | collective-permute-start | bytes 7176200 | tf_op jit(solution)/shard_map/ppermute | solution.py:526
  47.9 6.3 %collective-permute-start.1 = (bf16[256,256]{1,0:T(8,128)(2,1)S(1)}, bf16[256,256]{1,0:T(8,128)(2,1)S(1)}, u32[]{:S(2)}, u32[]{:S(2)}) collective-permute-start(bf16[256,256]{1,0:T(8,128)(2,1)S(1)} %get-tuple-element.27), channel_id=1, source_target_pairs={{0,64},{16,80},{32,96},{48,112},{64,0},{80,16},{96,32},{112,48},{1... | collective-permute-start | bytes 393224 | tf_op jit(solution)/shard_map/ppermute | solution.py:531
  50.8 3.5 %copy-start.3 = (bf16[4,16,16,256]{3,2,1,0:T(8,128)(2,1)S(1)}, bf16[4,16,16,256]{3,2,1,0:T(8,128)(2,1)}, u32[]{:S(2)}) copy-start(bf16[4,16,16,256]{3,2,1,0:T(8,128)(2,1)} %param.11) | copy-start | bytes 1572868
  61.8 5.4 %collective-permute-start.2 = (bf16[256,256]{1,0:T(8,128)(2,1)S(1)}, bf16[256,256]{1,0:T(8,128)(2,1)S(1)}, u32[]{:S(2)}, u32[]{:S(2)}) collective-permute-start(bf16[256,256]{1,0:T(8,128)(2,1)S(1)} %get-tuple-element.30), channel_id=1, source_target_pairs={{0,64},{16,80},{32,96},{48,112},{64,0},{80,16},{96,32},{112,48},{1... | collective-permute-start | bytes 393224 | tf_op jit(solution)/shard_map/ppermute | solution.py:533
  67.2 18.9 %copy-start.4 = (f32[4,512]{1,0:T(4,128)S(1)}, f32[4,512]{1,0:T(4,128)}, u32[]{:S(2)}) copy-start(f32[4,512]{1,0:T(4,128)} %latent_ref.1) | copy-start | bytes 24580
  70.7 15.5 %copy-start = (bf16[1,3,3,256,256]{4,3,2,1,0:T(8,128)(2,1)S(1)}, bf16[1,3,3,256,256]{4,3,2,1,0:T(8,128)(2,1)}, u32[]{:S(2)}) copy-start(bf16[1,3,3,256,256]{4,3,2,1,0:T(8,128)(2,1)} %param.8) | copy-start | bytes 3538948
  70.7 15.5 %copy-start.1 = (f32[1,512,256]{2,1,0:T(8,128)S(1)}, f32[1,512,256]{2,1,0:T(8,128)}, u32[]{:S(2)}) copy-start(f32[1,512,256]{2,1,0:T(8,128)} %param.9) | copy-start | bytes 1572868
  89.1 5.2 %collective-permute-start.3 = (bf16[1168,256]{1,0:T(8,128)(2,1)S(1)}, bf16[1168,256]{1,0:T(8,128)(2,1)S(1)}, u32[]{:S(2)}, u32[]{:S(2)}) collective-permute-start(bf16[1168,256]{1,0:T(8,128)(2,1)S(1)} %get-tuple-element.38), channel_id=1, source_target_pairs={{0,1},{1,0},{2,3},{3,2},{4,5},{5,4},{6,7},{7,6},{8,9},{9,8},{10,11... | collective-permute-start | bytes 1794056 | tf_op jit(solution)/shard_map/ppermute | solution.py:539
  95.3 18.4 %all-to-all-start.2 = ((bf16[8,176,256]{2,1,0:T(8,128)(2,1)}), bf16[8,176,256]{2,1,0:T(8,128)(2,1)S(1)}, u32[]{:S(2)}, u32[]{:S(2)}) async-start(bf16[8,176,256]{2,1,0:T(8,128)(2,1)} %pair.1), calls=%async_computation.2 | async-start | bytes 1441792 | tf_op jit(solution)/shard_map/all_to_all | solution.py:541
  100.4 10.7 %collective-permute-start.4 = (f32[4,512]{1,0:T(4,128)S(1)}, f32[4,512]{1,0:T(4,128)S(1)}, u32[]{:S(2)}, u32[]{:S(2)}) collective-permute-start(f32[4,512]{1,0:T(4,128)S(1)} %slice.3), channel_id=1, source_target_pairs={{0,64},{16,80},{32,96},{48,112},{64,0},{80,16},{96,32},{112,48},{1... | collective-permute-start | bytes 24584 | tf_op jit(solution)/shard_map/ppermute | solution.py:542
  111.2 2.5 %collective-permute-start.5 = (f32[4,512]{1,0:T(4,128)S(1)}, f32[4,512]{1,0:T(4,128)S(1)}, u32[]{:S(2)}, u32[]{:S(2)}) collective-permute-start(f32[4,512]{1,0:T(4,128)S(1)} %add.9), channel_id=1, source_target_pairs={{0,16},{16,0},{32,48},{48,32},{64,80},{80,64},{96,112},{112,96},{1... | collective-permute-start | bytes 24584 | tf_op jit(solution)/shard_map/ppermute | solution.py:543
  114.6 12.2 %all-to-all-start.3 = ((bf16[8,144,256]{2,1,0:T(8,128)(2,1)}), bf16[8,144,256]{2,1,0:T(8,128)(2,1)S(1)}, u32[]{:S(2)}, u32[]{:S(2)}) async-start(bf16[8,144,256]{2,1,0:T(8,128)(2,1)} %share.1), calls=%async_computation.3 | async-start | bytes 1179648 | tf_op jit(solution)/shard_map/all_to_all | solution.py:545
  118.8 4.0 %collective-permute-start.6 = (f32[4,512]{1,0:T(4,128)S(1)}, f32[4,512]{1,0:T(4,128)S(1)}, u32[]{:S(2)}, u32[]{:S(2)}) collective-permute-start(f32[4,512]{1,0:T(4,128)S(1)} %add.10), channel_id=1, source_target_pairs={{0,32},{16,48},{32,0},{48,16},{64,96},{80,112},{96,64},{112,80},{1... | collective-permute-start | bytes 24584 | tf_op jit(solution)/shard_map/ppermute | solution.py:546
  126.8 6.5 %collective-permute-start.7 = (bf16[1152,256]{1,0:T(8,128)(2,1)S(1)}, bf16[1152,256]{1,0:T(8,128)(2,1)S(1)}, u32[]{:S(2)}, u32[]{:S(2)}) collective-permute-start(bf16[1152,256]{1,0:T(8,128)(2,1)S(1)} %bitcast.9), channel_id=1, source_target_pairs={{0,1},{1,0},{2,3},{3,2},{4,5},{5,4},{6,7},{7,6},{8,9},{9,8},{10,11... | collective-permute-start | bytes 1769480 | tf_op jit(solution)/shard_map/ppermute | solution.py:548

commit v4 on v3

--- a/solution.py
+++ b/solution.py
@@ -22,6 +22,7 @@
 PEERS = 8
 SHARE = HALF // PEERS
 ROW = 16
+BLOCK = 128
 PAD = PX + 2 * ROW
 HI = lax.Precision.HIGHEST
 
@@ -169,13 +170,23 @@
     pad_ref[2, ROW : ROW + PX, :] = jnp.where(column == ROW - 1, 0.0, pltpu.roll(value, PX - 1, 0)).astype(BF)
 
 
+def taps_matmul(pad_ref, w, mirrored):
+    out = []
+    for start in range(0, PX, BLOCK):
+        pieces = []
+        for ky in range(3):
+            for kx in range(3):
+                plane, shift = (2 - kx, 2 - ky) if mirrored else (kx, ky)
+                first_row = start + shift * ROW
+                pieces.append(pad_ref[plane, first_row : first_row + BLOCK, :])
+        out.append(jnp.dot(jnp.concatenate(pieces, axis=1), w, preferred_element_type=F32))
+    return jnp.concatenate(out, axis=0)
+
+
 def forward_layer(x, l, w_ref, stat, pad_ref):
     styles, demod, bias = stat
     spread(pad_ref, (x.astype(F32) * styles).astype(BF).astype(F32))
-    lhs = jnp.concatenate(
-        [pad_ref[kx, ky * ROW : ky * ROW + PX, :] for ky in range(3) for kx in range(3)], axis=1
-    )
-    return jnp.dot(lhs, w_ref[l], preferred_element_type=F32)
+    return taps_matmul(pad_ref, w_ref[l], False)
 
 
 def activate(conv, stat):
@@ -194,10 +205,7 @@
     grad_conv = (dh * demod).astype(BF).astype(F32)
     spread(pad_ref, grad_conv)
     send_ref[l, PX : 2 * PX, :] = pad_ref[1, ROW : ROW + PX, :]
-    lhs = jnp.concatenate(
-        [pad_ref[2 - kx, (2 - ky) * ROW : (2 - ky) * ROW + PX, :] for ky in range(3) for kx in range(3)], axis=1
-    )
-    total = jnp.dot(lhs, flip_ref[l], preferred_element_type=F32)
+    total = taps_matmul(pad_ref, flip_ref[l], True)
     grad_scaled = total.astype(BF).astype(F32)
     xf = x.astype(F32)
     grad_styles = jnp.sum(grad_scaled * xf, axis=0, keepdims=True)
@@ -211,15 +219,17 @@
     x_copy = pltpu.make_async_copy(images_any.at[z], x_buf, x_sem)
     x_copy.start()
     copies = weight_copies(a_ref, b_ref, w_ref, stat_ref, sem)
-    for group in copies:
-        for copy in group:
-            copy.start()
+    for copy in copies[0]:
+        copy.start()
     clear_pads(pad_ref)
     x_copy.wait()
     x = x_buf[...]
     for l in range(DEPTH):
         for copy in copies[l]:
             copy.wait()
+        if l < DEPTH - 1:
+            for copy in copies[l + 1]:
+                copy.start()
         stat = unpack_rows(stat_ref[l])
         x = activate(forward_layer(x, l, w_ref, stat, pad_ref), stat)
     out_ref[...] = x
@@ -342,9 +352,24 @@
     )(cot, recv, xs, conv, flipped, stat)
 
 
-def gradient_kernel(
+def half_gradient(flip_ref, pad_ref, w_ref, grad_energy_ref, half, out_ref):
+    first_row = pl.multiple_of(half * BLOCK, BLOCK)
+    lhs = flip_ref[pl.ds(first_row, BLOCK), :]
+    grad_energy = grad_energy_ref[pl.ds(first_row, BLOCK), :]
+    for ky in range(3):
+        for kx in range(3):
+            tap = ky * 3 + kx
+            rhs = jnp.concatenate(
+                [pad_ref[n, 2 - kx, (2 - ky) * ROW : (2 - ky) * ROW + PX, :] for n in range(DEPTH)], axis=0
+            )
+            part = jnp.dot(lhs, rhs, preferred_element_type=F32)
+            w = w_ref[pl.ds(pl.multiple_of(tap * C + half * BLOCK, BLOCK), BLOCK), :].astype(F32)
+            out_ref[tap * BLOCK : (tap + 1) * BLOCK, :] = (part + w * grad_energy).astype(BF)
+
+
+def give_kernel(
     r_ref, w_ref, styles_ref, demod_ref, energy_ref, affine_ref, latent_ref,
-    keep_ref, give_ref, extra_ref, grad_latent_ref, flip_ref, pad_ref, total_ref, rows_ref,
+    give_ref, extra_ref, grad_latent_ref, flip_ref, pad_ref, grad_energy_ref, rows_ref,
 ):
     _, _, core = place()
     parts = [unpack_rows(r_ref[n, 2 * PX : 2 * PX + STAT, :]) for n in range(DEPTH)]
@@ -365,49 +390,53 @@
     extra = rows_ref[...].astype(BF)
     extra_ref[...] = extra
     give_ref[HALF : HALF + STAT, :] = extra
-    grad_latent_ref[...] = lax.dot_general(
+    grad_latent = lax.dot_general(
         grad_styles, affine_ref[...], (((1,), (1,)), ((), ())), precision=HI, preferred_element_type=F32
     )
-    grad_energy = 2.0 * lax.dot_general(
+    grad_latent_ref[...] = grad_latent[0:DEPTH]
+    grad_energy_ref[...] = 2.0 * lax.dot_general(
         squares, grad_sum, (((0,), (0,)), ((), ())), precision=HI, preferred_element_type=F32
     )
     for n in range(DEPTH):
         clear_pads(pad_ref.at[n])
         spread(pad_ref.at[n], r_ref[n, PX : 2 * PX, :].astype(F32))
         flip_ref[:, n * PX : (n + 1) * PX] = r_ref[n, 0:PX, :].astype(F32).T.astype(BF)
-    for ky in range(3):
-        for kx in range(3):
-            tap = ky * 3 + kx
-            rhs = jnp.concatenate(
-                [pad_ref[n, 2 - kx, (2 - ky) * ROW : (2 - ky) * ROW + PX, :] for n in range(DEPTH)], axis=0
-            )
-            part = jnp.dot(flip_ref[...], rhs, preferred_element_type=F32)
-            at = slice(tap * C, (tap + 1) * C)
-            total_ref[at, :] = (part + w_ref[at, :].astype(F32) * grad_energy).astype(BF)
-    keep_ref[...] = total_ref[pl.ds(pl.multiple_of(core * HALF, HALF), HALF), :]
-    give_ref[0:HALF, :] = total_ref[pl.ds(pl.multiple_of((1 - core) * HALF, HALF), HALF), :]
-
-
-def gradients(r, w, styles, demod, energy, affine, latent):
-    return pl.pallas_call(
-        gradient_kernel,
+    half_gradient(flip_ref, pad_ref, w_ref, grad_energy_ref, 1 - core, give_ref)
+
+
+def give_half(r, w, styles, demod, energy, affine, latent):
+    return pl.pallas_call(
+        give_kernel,
         out_shape=(
-            jax.ShapeDtypeStruct((HALF, C), BF),
             jax.ShapeDtypeStruct((HALF + STAT, C), BF),
             jax.ShapeDtypeStruct((STAT, C), BF),
-            jax.ShapeDtypeStruct((8, affine.shape[0]), F32),
+            jax.ShapeDtypeStruct((DEPTH, affine.shape[0]), F32),
+            jax.ShapeDtypeStruct((C, DEPTH * PX), BF),
+            jax.ShapeDtypeStruct((DEPTH, 3, PAD, C), BF),
+            jax.ShapeDtypeStruct((C, C), F32),
         ),
         in_specs=[vmem_spec()] * 7,
-        out_specs=(vmem_spec(),) * 4,
-        scratch_shapes=[
-            pltpu.VMEM((C, DEPTH * PX), BF),
-            pltpu.VMEM((DEPTH, 3, PAD, C), BF),
-            pltpu.VMEM((ROWS, C), BF),
-            pltpu.VMEM((STAT, C), F32),
-        ],
-        compiler_params=params(),
-        name="gradients",
+        out_specs=(vmem_spec(),) * 6,
+        scratch_shapes=[pltpu.VMEM((STAT, C), F32)],
+        compiler_params=params(),
+        name="give",
     )(r, w, styles, demod, energy, affine, latent)
+
+
+def keep_kernel(flip_ref, pad_ref, w_ref, grad_energy_ref, keep_ref):
+    _, _, core = place()
+    half_gradient(flip_ref, pad_ref, w_ref, grad_energy_ref, core, keep_ref)
+
+
+def keep_half(flipped, padded, w, grad_energy):
+    return pl.pallas_call(
+        keep_kernel,
+        out_shape=jax.ShapeDtypeStruct((HALF, C), BF),
+        in_specs=[vmem_spec()] * 4,
+        out_specs=vmem_spec(),
+        compiler_params=params(),
+        name="keep",
+    )(flipped, padded, w, grad_energy)
 
 
 def pair_kernel(keep_ref, extra_ref, got_ref, out_ref):
@@ -479,32 +508,28 @@
     )(shares)
 
 
-def own_kernel(mine_ref, out_any, wide_ref, sem):
+def widen_kernel(own, value_ref, *refs):
+    out_any, wide_ref, sem = refs[-3:]
     _, _, core = place()
-    wide_ref[...] = mine_ref[...].astype(F32)
-    copy = pltpu.make_async_copy(wide_ref, out_any.at[pl.ds(pl.multiple_of(core * HALF, HALF), HALF)], sem)
+    half = core if own else 1 - core
+    wide_ref[...] = value_ref[...].reshape(TAPS, BLOCK, C).astype(F32)
+    copy = pltpu.make_async_copy(wide_ref, out_any.at[:, pl.ds(pl.multiple_of(half * BLOCK, BLOCK), BLOCK)], sem)
     copy.start()
     copy.wait()
 
 
-def rest_kernel(other_ref, _, out_any, wide_ref, sem):
-    _, _, core = place()
-    wide_ref[...] = other_ref[...].astype(F32)
-    copy = pltpu.make_async_copy(wide_ref, out_any.at[pl.ds(pl.multiple_of((1 - core) * HALF, HALF), HALF)], sem)
-    copy.start()
-    copy.wait()
-
-
-def widen(kernel, name, *args):
-    return pl.pallas_call(
-        kernel,
-        out_shape=jax.ShapeDtypeStruct((ROWS, C), F32),
-        in_specs=[vmem_spec(), pl.BlockSpec(memory_space=pltpu.HBM)][: len(args)],
-        out_specs=pl.BlockSpec(memory_space=pltpu.HBM),
+def widen(value, target=None):
+    hbm = pl.BlockSpec(memory_space=pltpu.HBM)
+    args = (value,) if target is None else (value, target)
+    return pl.pallas_call(
+        functools.partial(widen_kernel, target is None),
+        out_shape=jax.ShapeDtypeStruct((TAPS, C, C), F32),
+        in_specs=[vmem_spec(), hbm][: len(args)],
+        out_specs=hbm,
         input_output_aliases={1: 0} if len(args) == 2 else {},
-        scratch_shapes=[pltpu.VMEM((HALF, C), F32), pltpu.SemaphoreType.DMA],
-        compiler_params=params(),
-        name=name,
+        scratch_shapes=[pltpu.VMEM((TAPS, BLOCK, C), F32), pltpu.SemaphoreType.DMA],
+        compiler_params=params(),
+        name="own" if target is None else "rest",
     )(*args)
 
 
@@ -534,20 +559,22 @@
     sent = last(cotangent, returned, xs, conv, flipped, stat)
 
     r = near(lax.all_to_all(sent, "segment", 0, 0, axis_index_groups=planes))
-    keep, give, extra, latent_part = gradients(r, w, styles, demod, energy, affine[0], latent)
-
+    give, extra, part, flipped_maps, padded, grad_energy = give_half(
+        r, w, styles, demod, energy, affine[0], latent
+    )
     got = near(lax.ppermute(give, "dp", sibling))
-    shared, part = lax.optimization_barrier((pair(keep, extra, got), latent_part[:DEPTH]))
-    shares = near(lax.all_to_all(shared, "dp", 0, 0, axis_index_groups=cores))
     part = part + lax.ppermute(part, "segment", across)
+    keep = keep_half(flipped_maps, padded, w, grad_energy)
+    shared, part = lax.optimization_barrier((pair(keep, extra, got), part))
+    shares = near(lax.all_to_all(near(shared), "dp", 0, 0, axis_index_groups=cores))
     part = part + lax.ppermute(part, "segment", [(i, i ^ 1) for i in range(segments)])
-    spread_share, part = lax.optimization_barrier((share(shares), part))
-    mine = lax.all_to_all(spread_share, "dp", 0, 0, axis_index_groups=cores).reshape(HALF, C)
     grad_latent = part + lax.ppermute(part, "segment", [(i, i ^ 2) for i in range(segments)])
-    mine, grad_latent = lax.optimization_barrier((mine, grad_latent))
+    spread_share, grad_latent = lax.optimization_barrier((share(shares), grad_latent))
+    mine = lax.all_to_all(near(spread_share), "dp", 0, 0, axis_index_groups=cores)
+    grad_affine, grad_bias = affine_gradient(shares, width)
+    mine, grad_affine, grad_bias = lax.optimization_barrier((mine, grad_affine, grad_bias))
     other = near(lax.ppermute(mine, "dp", sibling))
-    grad_affine, grad_bias = affine_gradient(shares, width)
-    grad_weight = widen(rest_kernel, "rest", other, widen(own_kernel, "own", near(mine))).reshape(weight.shape)
+    grad_weight = widen(other, widen(near(mine))).reshape(weight.shape)
     return (grad_weight, grad_affine[None], grad_bias, grad_latent)
 
 

time: 135 us -> 129 us (0.956)
  Pallas kernels: 27.2 us -> 23.7 us
  waiting for transfers between devices: 27.7 us -> 26.1 us
    ppermute x1, waiting for transfers between devices: 8.29 us -> 0.49 us  [body(): part = part + lax.ppermute(part, 'segment', across)]
    all_to_all x2, waiting for transfers between devices: 3.4 us -> 10.6 us  [the longest x1 6.97 us: body(): lax.all_to_all(near(spread_share), 'dp', 0, 0, axis_index_groups=cores)]
    pallas_call x1, Pallas kernels: 7.61 us -> 5.75 us  [middle(): pl.pallas_call(middle_kernel, out_shape=(MAP, jax.ShapeDtypeStruct((DEPTH...]
    ppermute x1, waiting for transfers between devices: 1.64 us -> 0.01 us  [body(): got = near(lax.ppermute(give, 'dp', sibling))]
    pallas_call x3 -> x4, Pallas kernels: 5.16 us -> 5.25 us  [the longest x1 2.26 us: give_half(): pl.pallas_call(give_kernel, out_shape=(jax.ShapeDtypeStruct((HALF + STAT,...]
  transfers between devices with their start and end apart: 10 -> 10, of which waited for: 8 -> 9; matrix products, arithmetic and copies ran while one was open for 0% -> 0% of each run, Pallas kernels for 3% -> 3%
where the time goes in v4:
time: 129 us; the launch traced here: 128 us
  blocking collectives  49.6 us (38%)
  starting transfers between devices  27.3 us (21%)
  waiting for transfers between devices  26.1 us (20%)
  Pallas kernels  23.7 us (18%)
    all_to_all x1, blocking collectives, body(): a = lax.all_to_all(send, 'segment', 0, 0, axis_index_groups=planes)  34.2 us
    all_to_all x1, blocking collectives, body(): r = near(lax.all_to_all(sent, 'segment', 0, 0, axis_index_groups=planes))  15.4 us
    all_to_all x1, waiting for transfers between devices, body(): lax.all_to_all(near(spread_share), 'dp', 0, 0, axis_index_groups=cores)  6.97 us
    pallas_call x1, Pallas kernels, middle(): pl.pallas_call(middle_kernel, out_shape=(MAP, jax.ShapeDtypeStruct((DEPTH...  5.75 us
    all_to_all x1, starting transfers between devices, body(): lax.all_to_all(near(shared), 'dp', 0, 0, axis_index_groups=cores)  5.12 us
    ppermute x1, waiting for transfers between devices, body(): b = near(lax.ppermute(a, 'dp', sibling))  4.21 us
    ppermute x1, starting transfers between devices, body(): other = near(lax.ppermute(mine, 'dp', sibling))  3.63 us
    all_to_all x1, waiting for transfers between devices, body(): lax.all_to_all(near(shared), 'dp', 0, 0, axis_index_groups=cores)  3.62 us
  transfers between devices with their start and end apart: 10, of which 9 were waited for; matrix products, arithmetic and copies ran while one was open for 0% of the time, Pallas kernels for 3%

profile of v4, /device:TPU:1, one launch (start us, length us, event | category | flops | bytes accessed | tf_op | source)
XLA Modules:
  0.0 128.2 jit_solution(3885874375093882053)
XLA Ops:
  0.6 2.5 %prepare.1 = (bf16[4,1168,256]{2,1,0:T(8,128)(2,1)S(1)}, f32[8,256]{1,0:T(8,128)S(1)}, f32[8,256]{1,0:T(8,128)S(1)}, f32[256,256]{1,0:T(8,128)S(1)}) custom-call(f32[4,512]{1,0:T(4,128)} %latent_ref.1, f32[512,256]{1,0:T(8,128)} %bitcast.9, bf16[2304,256]{1,0:T(8,128)(2,1)} %bitcast.6, f32[1,256]{1,0:T(1,128)} %bias_hbm.1), custom_call_target="tpu_custom_call" | custom-call | tf_op jit(solution)/shard_map/prepare/pallas_call | solution.py:124
  3.1 0.0 copy-start.2
  3.1 34.2 %all_to_all.20.a_ref = bf16[4,1168,256]{2,1,0:T(8,128)(2,1)S(1)} all-to-all(bf16[4,1168,256]{2,1,0:T(8,128)(2,1)S(1)} %get-tuple-element.29), channel_id=1, replica_groups={{0,16,32,48},{64,80,96,112},{1,17,33,49},{65,81,97,113},{2,18,34,50},{6..., dimensions={0} | all-to-all | bytes 4784128 | tf_op jit(solution)/shard_map/all_to_all | solution.py:550
  37.3 2.1 %collective-permute-start = (bf16[4,1168,256]{2,1,0:T(8,128)(2,1)S(1)}, bf16[4,1168,256]{2,1,0:T(8,128)(2,1)S(1)}, u32[]{:S(2)}, u32[]{:S(2)}) collective-permute-start(bf16[4,1168,256]{2,1,0:T(8,128)(2,1)S(1)} %all_to_all.20.a_ref), channel_id=1, source_target_pairs={{0,1},{1,0},{2,3},{3,2},{4,5},{5,4},{6,7},{7,6},{8,9},{9,8},{10,11... | collective-permute-start | bytes 7176200 | tf_op jit(solution)/shard_map/ppermute | solution.py:551
  39.3 4.2 %collective-permute-done.b_ref = bf16[4,1168,256]{2,1,0:T(8,128)(2,1)S(1)} collective-permute-done((bf16[4,1168,256]{2,1,0:T(8,128)(2,1)S(1)}, bf16[4,1168,256]{2,1,0:T(8,128)(2,1)S(1)}, u32[]{:S(2)}, u32[]{:S(2)}) %collective-permute-start) | collective-permute-done | bytes 2392096 | tf_op jit(solution)/shard_map/ppermute | solution.py:551
  43.5 0.0 copy-done.2
  43.6 3.4 %first.1 = (bf16[256,256]{1,0:T(8,128)(2,1)S(1)}, bf16[4,2304,256]{2,1,0:T(8,128)(2,1)S(1)}, bf16[4,16,256]{2,1,0:T(8,128)(2,1)S(1)}) custom-call(bf16[4,256,256]{2,1,0:T(8,128)(2,1)S(1)} %bitcast.11, bf16[4,1168,256]{2,1,0:T(8,128)(2,1)S(1)} %all_to_all.20.a_ref, bf16[4,1168,256]{2,1,0:T(8,128)(2,1)S(1)} %collective-permute-done.b_ref), custom_call_target="tpu_custom_call" | custom-call | tf_op jit(solution)/shard_map/first/pallas_call | solution.py:290
  47.0 2.8 %collective-permute-start.1 = (bf16[256,256]{1,0:T(8,128)(2,1)S(1)}, bf16[256,256]{1,0:T(8,128)(2,1)S(1)}, u32[]{:S(2)}, u32[]{:S(2)}) collective-permute-start(bf16[256,256]{1,0:T(8,128)(2,1)S(1)} %get-tuple-element.30), channel_id=1, source_target_pairs={{0,64},{16,80},{32,96},{48,112},{64,0},{80,16},{96,32},{112,48},{1... | collective-permute-start | bytes 393224 | tf_op jit(solution)/shard_map/ppermute | solution.py:556
  49.8 0.0 copy-start.3
  49.8 1.3 flip.1.flip_ref
  51.1 2.2 %collective-permute-done.1.recv_ref = bf16[256,256]{1,0:T(8,128)(2,1)S(1)} collective-permute-done((bf16[256,256]{1,0:T(8,128)(2,1)S(1)}, bf16[256,256]{1,0:T(8,128)(2,1)S(1)}, u32[]{:S(2)}, u32[]{:S(2)}) %collective-permute-start.1) | collective-permute-done | bytes 131104 | tf_op jit(solution)/shard_map/ppermute | solution.py:556
  53.3 0.0 copy-done.3
  53.3 5.8 %middle.1 = (bf16[256,256]{1,0:T(8,128)(2,1)S(1)}, bf16[4,256,256]{2,1,0:T(8,128)(2,1)S(1)}, f32[4,256,256]{2,1,0:T(8,128)S(1)}, bf16[4,528,256]{2,1,0:T(8,128)(2,1)}) custom-call(bf16[4,256,256]{2,1,0:T(8,128)(2,1)S(1)} %bitcast.12, bf16[4,256,256]{2,1,0:T(8,128)(2,1)S(1)} %bitcast.13, bf16[256,256]{1,0:T(8,128)(2,1)S(1)} %collective-permute-done.1.recv_ref, ...), custom_call_target="tpu_custom_call" | custom-call | tf_op jit(solution)/shard_map/middle/pallas_call | solution.py:318
  59.0 2.8 %collective-permute-start.2 = (bf16[256,256]{1,0:T(8,128)(2,1)S(1)}, bf16[256,256]{1,0:T(8,128)(2,1)S(1)}, u32[]{:S(2)}, u32[]{:S(2)}) collective-permute-start(bf16[256,256]{1,0:T(8,128)(2,1)S(1)} %get-tuple-element.33), channel_id=1, source_target_pairs={{0,64},{16,80},{32,96},{48,112},{64,0},{80,16},{96,32},{112,48},{1... | collective-permute-start | bytes 393224 | tf_op jit(solution)/shard_map/ppermute | solution.py:558
  61.8 2.6 %collective-permute-done.2.recv_ref = bf16[256,256]{1,0:T(8,128)(2,1)S(1)} collective-permute-done((bf16[256,256]{1,0:T(8,128)(2,1)S(1)}, bf16[256,256]{1,0:T(8,128)(2,1)S(1)}, u32[]{:S(2)}, u32[]{:S(2)}) %collective-permute-start.2) | collective-permute-done | bytes 131104 | tf_op jit(solution)/shard_map/ppermute | solution.py:558
  64.4 0.0 copy-start.4
  64.4 2.6 %last.1 = bf16[4,528,256]{2,1,0:T(8,128)(2,1)S(1)} custom-call(bf16[4,256,256]{2,1,0:T(8,128)(2,1)S(1)} %bitcast.14, bf16[256,256]{1,0:T(8,128)(2,1)S(1)} %collective-permute-done.2.recv_ref, bf16[4,256,256]{2,1,0:T(8,128)(2,1)S(1)} %get-tuple-element.34.xs_ref, f32[4,256,256]{2,1,0:T(8,128)S(1)} %get-tuple-element.35.conv_ref, ...), custom_call_target="tpu_custom_call" | custom-call | tf_op jit(solution)/shard_map/last/pallas_call | solution.py:340
  67.0 0.0 copy-start
  67.0 0.0 copy-start.1
  67.1 15.4 %all_to_all.21.r_ref = bf16[4,528,256]{2,1,0:T(8,128)(2,1)S(1)} all-to-all(bf16[4,528,256]{2,1,0:T(8,128)(2,1)S(1)} %last.1), channel_id=1, replica_groups={{0,16,32,48},{64,80,96,112},{1,17,33,49},{65,81,97,113},{2,18,34,50},{6..., dimensions={0} | all-to-all | bytes 2162688 | tf_op jit(solution)/shard_map/all_to_all | solution.py:561
  82.5 0.0 copy-done.4
  82.5 0.0 copy-done
  82.5 0.0 copy-done.1
  82.5 2.3 %give.1 = (bf16[1168,256]{1,0:T(8,128)(2,1)S(1)}, bf16[16,256]{1,0:T(8,128)(2,1)S(1)}, f32[4,512]{1,0:T(4,128)S(1)}, bf16[256,1024]{1,0:T(8,128)(2,1)S(1)}, bf16...) custom-call(bf16[4,528,256]{2,1,0:T(8,128)(2,1)S(1)} %all_to_all.21.r_ref, bf16[2304,256]{1,0:T(8,128)(2,1)S(1)} %bitcast.7, ...), custom_call_target="tpu_custom_call" | custom-call | tf_op jit(solution)/shard_map/give/pallas_call | solution.py:408
  84.8 3.6 %collective-permute-start.3 = (bf16[1168,256]{1,0:T(8,128)(2,1)S(1)}, bf16[1168,256]{1,0:T(8,128)(2,1)S(1)}, u32[]{:S(2)}, u32[]{:S(2)}) collective-permute-start(bf16[1168,256]{1,0:T(8,128)(2,1)S(1)} %get-tuple-element.43), channel_id=1, source_target_pairs={{0,1},{1,0},{2,3},{3,2},{4,5},{5,4},{6,7},{7,6},{8,9},{9,8},{10,11... | collective-permute-start | bytes 1794056 | tf_op jit(solution)/shard_map/ppermute | solution.py:565
  88.3 2.7 %collective-permute-start.4 = (f32[4,512]{1,0:T(4,128)S(1)}, f32[4,512]{1,0:T(4,128)S(1)}, u32[]{:S(2)}, u32[]{:S(2)}) collective-permute-start(f32[4,512]{1,0:T(4,128)S(1)} %get-tuple-element.44), channel_id=1, source_target_pairs={{0,64},{16,80},{32,96},{48,112},{64,0},{80,16},{96,32},{112,48},{1... | collective-permute-start | bytes 24584 | tf_op jit(solution)/shard_map/ppermute | solution.py:566
  91.1 0.8 keep.1.keep_ref
  91.9 0.5 collective-permute-done.4
  92.4 0.0 collective-permute-done.3.got_ref
  92.4 1.0 pair.1
  93.4 5.1 %all-to-all-start.2 = ((bf16[8,176,256]{2,1,0:T(8,128)(2,1)}), bf16[8,176,256]{2,1,0:T(8,128)(2,1)S(1)}, u32[]{:S(2)}, u32[]{:S(2)}) async-start(bf16[8,176,256]{2,1,0:T(8,128)(2,1)} %pair.1), calls=%async_computation.2 | async-start | bytes 1441792 | tf_op jit(solution)/shard_map/all_to_all | solution.py:569
  98.5 0.3 collective-permute-start.5
  98.8 2.2 %collective-permute-done.5 = f32[4,512]{1,0:T(4,128)S(1)} collective-permute-done((f32[4,512]{1,0:T(4,128)S(1)}, f32[4,512]{1,0:T(4,128)S(1)}, u32[]{:S(2)}, u32[]{:S(2)}) %collective-permute-start.5) | collective-permute-done | bytes 8224 | tf_op jit(solution)/shard_map/ppermute | solution.py:570
  101.0 0.8 collective-permute-start.6
  101.8 3.2 %collective-permute-done.6 = f32[4,512]{1,0:T(4,128)S(1)} collective-permute-done((f32[4,512]{1,0:T(4,128)S(1)}, f32[4,512]{1,0:T(4,128)S(1)}, u32[]{:S(2)}, u32[]{:S(2)}) %collective-permute-start.6) | collective-permute-done | bytes 8224 | tf_op jit(solution)/shard_map/ppermute | solution.py:571
  105.0 0.6 add.11
  105.6 3.6 %all-to-all-done.2.shares_ref = bf16[8,176,256]{2,1,0:T(8,128)(2,1)S(1)} async-done(((bf16[8,176,256]{2,1,0:T(8,128)(2,1)}), bf16[8,176,256]{2,1,0:T(8,128)(2,1)S(1)}, u32[]{:S(2)}, u32[]{:S(2)}) %all-to-all-start.2) | async-done | bytes 720928 | tf_op jit(solution)/shard_map/all_to_all | solution.py:569
  109.2 0.9 share.1
  110.1 3.5 %all-to-all-start.3 = ((bf16[8,144,256]{2,1,0:T(8,128)(2,1)}), bf16[8,144,256]{2,1,0:T(8,128)(2,1)S(1)}, u32[]{:S(2)}, u32[]{:S(2)}) async-start(bf16[8,144,256]{2,1,0:T(8,128)(2,1)} %share.1), calls=%async_computation.3 | async-start | bytes 1179648 | tf_op jit(solution)/shard_map/all_to_all | solution.py:573
  113.7 1.1 affine.1
  114.8 7.0 %all-to-all-done.3.value_ref = bf16[8,144,256]{2,1,0:T(8,128)(2,1)S(1)} async-done(((bf16[8,144,256]{2,1,0:T(8,128)(2,1)}), bf16[8,144,256]{2,1,0:T(8,128)(2,1)S(1)}, u32[]{:S(2)}, u32[]{:S(2)}) %all-to-all-start.3) | async-done | bytes 589856 | tf_op jit(solution)/shard_map/all_to_all | solution.py:573
  121.7 3.6 %collective-permute-start.7 = (bf16[8,144,256]{2,1,0:T(8,128)(2,1)S(1)}, bf16[8,144,256]{2,1,0:T(8,128)(2,1)S(1)}, u32[]{:S(2)}, u32[]{:S(2)}) collective-permute-start(bf16[8,144,256]{2,1,0:T(8,128)(2,1)S(1)} %all-to-all-done.3.value_ref), channel_id=1, source_target_pairs={{0,1},{1,0},{2,3},{3,2},{4,5},{5,4},{6,7},{7,6},{8,9},{9,8},{10,11... | collective-permute-start | bytes 1769480 | tf_op jit(solution)/shard_map/ppermute | solution.py:576
  125.4 1.1 own.1.refs_0_
  126.5 0.5 collective-permute-done.7.value_ref
  127.0 1.1 rest.1
  (2 shorter events, 0.0 us)
Async XLA Ops:
  3.1 40.5 %copy-start.2 = (bf16[4,16,16,256]{3,2,1,0:T(8,128)(2,1)S(1)}, bf16[4,16,16,256]{3,2,1,0:T(8,128)(2,1)}, u32[]{:S(2)}) copy-start(bf16[4,16,16,256]{3,2,1,0:T(8,128)(2,1)} %param.6) | copy-start | bytes 1572868
  37.3 6.3 %collective-permute-start = (bf16[4,1168,256]{2,1,0:T(8,128)(2,1)S(1)}, bf16[4,1168,256]{2,1,0:T(8,128)(2,1)S(1)}, u32[]{:S(2)}, u32[]{:S(2)}) collective-permute-start(bf16[4,1168,256]{2,1,0:T(8,128)(2,1)S(1)} %all_to_all.20.a_ref), channel_id=1, source_target_pairs={{0,1},{1,0},{2,3},{3,2},{4,5},{5,4},{6,7},{7,6},{8,9},{9,8},{10,11... | collective-permute-start | bytes 7176200 | tf_op jit(solution)/shard_map/ppermute | solution.py:551
  47.0 6.3 %collective-permute-start.1 = (bf16[256,256]{1,0:T(8,128)(2,1)S(1)}, bf16[256,256]{1,0:T(8,128)(2,1)S(1)}, u32[]{:S(2)}, u32[]{:S(2)}) collective-permute-start(bf16[256,256]{1,0:T(8,128)(2,1)S(1)} %get-tuple-element.30), channel_id=1, source_target_pairs={{0,64},{16,80},{32,96},{48,112},{64,0},{80,16},{96,32},{112,48},{1... | collective-permute-start | bytes 393224 | tf_op jit(solution)/shard_map/ppermute | solution.py:556
  49.8 3.5 %copy-start.3 = (bf16[4,16,16,256]{3,2,1,0:T(8,128)(2,1)S(1)}, bf16[4,16,16,256]{3,2,1,0:T(8,128)(2,1)}, u32[]{:S(2)}) copy-start(bf16[4,16,16,256]{3,2,1,0:T(8,128)(2,1)} %param.11) | copy-start | bytes 1572868
  59.0 5.4 %collective-permute-start.2 = (bf16[256,256]{1,0:T(8,128)(2,1)S(1)}, bf16[256,256]{1,0:T(8,128)(2,1)S(1)}, u32[]{:S(2)}, u32[]{:S(2)}) collective-permute-start(bf16[256,256]{1,0:T(8,128)(2,1)S(1)} %get-tuple-element.33), channel_id=1, source_target_pairs={{0,64},{16,80},{32,96},{48,112},{64,0},{80,16},{96,32},{112,48},{1... | collective-permute-start | bytes 393224 | tf_op jit(solution)/shard_map/ppermute | solution.py:558
  64.4 18.0 %copy-start.4 = (f32[4,512]{1,0:T(4,128)S(1)}, f32[4,512]{1,0:T(4,128)}, u32[]{:S(2)}) copy-start(f32[4,512]{1,0:T(4,128)} %latent_ref.1) | copy-start | bytes 24580
  67.0 15.5 %copy-start = (bf16[1,3,3,256,256]{4,3,2,1,0:T(8,128)(2,1)S(1)}, bf16[1,3,3,256,256]{4,3,2,1,0:T(8,128)(2,1)}, u32[]{:S(2)}) copy-start(bf16[1,3,3,256,256]{4,3,2,1,0:T(8,128)(2,1)} %param.8) | copy-start | bytes 3538948
  67.0 15.4 %copy-start.1 = (f32[1,512,256]{2,1,0:T(8,128)S(1)}, f32[1,512,256]{2,1,0:T(8,128)}, u32[]{:S(2)}) copy-start(f32[1,512,256]{2,1,0:T(8,128)} %param.9) | copy-start | bytes 1572868
  84.8 7.6 %collective-permute-start.3 = (bf16[1168,256]{1,0:T(8,128)(2,1)S(1)}, bf16[1168,256]{1,0:T(8,128)(2,1)S(1)}, u32[]{:S(2)}, u32[]{:S(2)}) collective-permute-start(bf16[1168,256]{1,0:T(8,128)(2,1)S(1)} %get-tuple-element.43), channel_id=1, source_target_pairs={{0,1},{1,0},{2,3},{3,2},{4,5},{5,4},{6,7},{7,6},{8,9},{9,8},{10,11... | collective-permute-start | bytes 1794056 | tf_op jit(solution)/shard_map/ppermute | solution.py:565
  88.3 4.0 %collective-permute-start.4 = (f32[4,512]{1,0:T(4,128)S(1)}, f32[4,512]{1,0:T(4,128)S(1)}, u32[]{:S(2)}, u32[]{:S(2)}) collective-permute-start(f32[4,512]{1,0:T(4,128)S(1)} %get-tuple-element.44), channel_id=1, source_target_pairs={{0,64},{16,80},{32,96},{48,112},{64,0},{80,16},{96,32},{112,48},{1... | collective-permute-start | bytes 24584 | tf_op jit(solution)/shard_map/ppermute | solution.py:566
  93.4 15.9 %all-to-all-start.2 = ((bf16[8,176,256]{2,1,0:T(8,128)(2,1)}), bf16[8,176,256]{2,1,0:T(8,128)(2,1)S(1)}, u32[]{:S(2)}, u32[]{:S(2)}) async-start(bf16[8,176,256]{2,1,0:T(8,128)(2,1)} %pair.1), calls=%async_computation.2 | async-start | bytes 1441792 | tf_op jit(solution)/shard_map/all_to_all | solution.py:569
  98.5 2.5 %collective-permute-start.5 = (f32[4,512]{1,0:T(4,128)S(1)}, f32[4,512]{1,0:T(4,128)S(1)}, u32[]{:S(2)}, u32[]{:S(2)}) collective-permute-start(f32[4,512]{1,0:T(4,128)S(1)} %add.9), channel_id=1, source_target_pairs={{0,16},{16,0},{32,48},{48,32},{64,80},{80,64},{96,112},{112,96},{1... | collective-permute-start | bytes 24584 | tf_op jit(solution)/shard_map/ppermute | solution.py:570
  101.0 4.0 %collective-permute-start.6 = (f32[4,512]{1,0:T(4,128)S(1)}, f32[4,512]{1,0:T(4,128)S(1)}, u32[]{:S(2)}, u32[]{:S(2)}) collective-permute-start(f32[4,512]{1,0:T(4,128)S(1)} %add.10), channel_id=1, source_target_pairs={{0,32},{16,48},{32,0},{48,16},{64,96},{80,112},{96,64},{112,80},{1... | collective-permute-start | bytes 24584 | tf_op jit(solution)/shard_map/ppermute | solution.py:571
  110.1 11.6 %all-to-all-start.3 = ((bf16[8,144,256]{2,1,0:T(8,128)(2,1)}), bf16[8,144,256]{2,1,0:T(8,128)(2,1)S(1)}, u32[]{:S(2)}, u32[]{:S(2)}) async-start(bf16[8,144,256]{2,1,0:T(8,128)(2,1)} %share.1), calls=%async_computation.3 | async-start | bytes 1179648 | tf_op jit(solution)/shard_map/all_to_all | solution.py:573
  121.7 5.3 %collective-permute-start.7 = (bf16[8,144,256]{2,1,0:T(8,128)(2,1)S(1)}, bf16[8,144,256]{2,1,0:T(8,128)(2,1)S(1)}, u32[]{:S(2)}, u32[]{:S(2)}) collective-permute-start(bf16[8,144,256]{2,1,0:T(8,128)(2,1)S(1)} %all-to-all-done.3.value_ref), channel_id=1, source_target_pairs={{0,1},{1,0},{2,3},{3,2},{4,5},{5,4},{6,7},{7,6},{8,9},{9,8},{10,11... | collective-permute-start | bytes 1769480 | tf_op jit(solution)/shard_map/ppermute | solution.py:576

commit v5 on v4

--- a/solution.py
+++ b/solution.py
@@ -23,6 +23,7 @@
 SHARE = HALF // PEERS
 ROW = 16
 BLOCK = 128
+LANES = 128
 PAD = PX + 2 * ROW
 HI = lax.Precision.HIGHEST
 
@@ -84,7 +85,7 @@
     rows_ref, affine_ref, w_ref, bias_ref, sem,
 ):
     _, _, core = place()
-    mine = pl.ds(pl.multiple_of(core * HALF, HALF), HALF)
+    mine = pl.ds(pl.multiple_of(core * LANES, LANES), LANES)
     rows_ref[...] = jnp.zeros_like(rows_ref)
     third = ROWS // 3
     loads = [
@@ -96,7 +97,7 @@
         for k in range(3)
     ]
     sends = [
-        pltpu.make_async_copy(w_hbm.at[mine], send_ref.at[k, pl.ds(0, HALF)], sem.at[6 + k]) for k in range(DEPTH)
+        pltpu.make_async_copy(w_hbm.at[:, mine], send_ref.at[k, pl.ds(0, ROWS)], sem.at[6 + k]) for k in range(DEPTH)
     ]
     for copy in loads + sends:
         copy.start()
@@ -114,7 +115,9 @@
     styles_ref[...] = styles
     demod_ref[...] = demod
     for k in range(DEPTH):
-        send_ref[k, HALF : HALF + STAT, :] = pack_rows([styles[k : k + 1], demod[k : k + 1], bias_ref[...]])
+        tile = pack_rows([styles[k : k + 1], demod[k : k + 1], bias_ref[...]])
+        send_ref[k, ROWS : ROWS + STAT, :] = tile[:, :LANES]
+        send_ref[k, ROWS + STAT : ROWS + 2 * STAT, :] = tile[:, LANES:]
     for copy in sends:
         copy.wait()
 
@@ -124,7 +127,7 @@
     return pl.pallas_call(
         prepare_kernel,
         out_shape=(
-            jax.ShapeDtypeStruct((DEPTH, HALF + STAT, C), BF),
+            jax.ShapeDtypeStruct((DEPTH, ROWS + 2 * STAT, LANES), BF),
             jax.ShapeDtypeStruct((8, C), F32),
             jax.ShapeDtypeStruct((8, C), F32),
             jax.ShapeDtypeStruct((C, C), F32),
@@ -143,18 +146,12 @@
     )(*far)
 
 
-def weight_copies(a_any, b_any, w_buf, stat_buf, sem):
-    _, _, core = place()
-    mine = pl.ds(pl.multiple_of(core * HALF, HALF), HALF)
-    other = pl.ds(pl.multiple_of((1 - core) * HALF, HALF), HALF)
-    return [
-        (
-            pltpu.make_async_copy(a_any.at[l, pl.ds(HALF, STAT)], stat_buf.at[l], sem.at[0, l]),
-            pltpu.make_async_copy(a_any.at[l, pl.ds(0, HALF)], w_buf.at[l, mine], sem.at[1, l]),
-            pltpu.make_async_copy(b_any.at[l, pl.ds(0, HALF)], w_buf.at[l, other], sem.at[2, l]),
+def read_stats(a_ref, l):
+    return unpack_rows(
+        jnp.concatenate(
+            [a_ref[l, ROWS : ROWS + STAT, :], a_ref[l, ROWS + STAT : ROWS + 2 * STAT, :]], axis=1
         )
-        for l in range(DEPTH)
-    ]
+    )
 
 
 def clear_pads(pad_ref):
@@ -183,10 +180,13 @@
     return jnp.concatenate(out, axis=0)
 
 
-def forward_layer(x, l, w_ref, stat, pad_ref):
+def forward_layer(x, l, a_ref, b_ref, stat, pad_ref):
     styles, demod, bias = stat
     spread(pad_ref, (x.astype(F32) * styles).astype(BF).astype(F32))
-    return taps_matmul(pad_ref, w_ref[l], False)
+    _, _, core = place()
+    w = jnp.concatenate([a_ref[l, 0:ROWS, :], b_ref[l, 0:ROWS, :]], axis=1)
+    conv = taps_matmul(pad_ref, w, False)
+    return jnp.where(core == 0, conv, jnp.concatenate([conv[:, LANES:], conv[:, :LANES]], axis=1))
 
 
 def activate(conv, stat):
@@ -214,36 +214,30 @@
     return (grad_scaled * styles).astype(BF)
 
 
-def first_kernel(images_any, a_ref, b_ref, out_ref, w_ref, stat_ref, x_buf, pad_ref, sem, x_sem):
+def first_kernel(images_any, a_ref, b_ref, out_ref, x_buf, pad_ref, x_sem):
     _, z, _ = place()
     x_copy = pltpu.make_async_copy(images_any.at[z], x_buf, x_sem)
     x_copy.start()
-    copies = weight_copies(a_ref, b_ref, w_ref, stat_ref, sem)
-    for copy in copies[0]:
-        copy.start()
     clear_pads(pad_ref)
     x_copy.wait()
     x = x_buf[...]
     for l in range(DEPTH):
-        for copy in copies[l]:
-            copy.wait()
-        if l < DEPTH - 1:
-            for copy in copies[l + 1]:
-                copy.start()
-        stat = unpack_rows(stat_ref[l])
-        x = activate(forward_layer(x, l, w_ref, stat, pad_ref), stat)
+        stat = read_stats(a_ref, l)
+        x = activate(forward_layer(x, l, a_ref, b_ref, stat, pad_ref), stat)
     out_ref[...] = x
 
 
-def flip_kernel(w_ref, flip_ref):
-    for l in range(DEPTH):
-        for tap in range(TAPS):
-            at = slice(tap * C, (tap + 1) * C)
-            flip_ref[l, at, :] = w_ref[l, at, :].T
+def flip_kernel(a_ref, b_ref, flip_ref):
+    _, _, core = place()
+    for source, half in ((a_ref, core), (b_ref, 1 - core)):
+        for l in range(DEPTH):
+            for tap in range(TAPS):
+                at = pl.ds(pl.multiple_of(tap * C + half * LANES, LANES), LANES)
+                flip_ref[l, at, :] = source[l, tap * C : (tap + 1) * C, :].T
 
 
 def middle_kernel(
-    images_any, cot_any, recv_ref, w_ref, flip_ref, stat_ref, dx_ref, xs_ref, conv_ref, send_ref,
+    images_any, cot_any, recv_ref, a_ref, b_ref, flip_ref, dx_ref, xs_ref, conv_ref, send_ref,
     x_buf, u_buf, pad_ref, x_sem,
 ):
     half, z, _ = place()
@@ -256,9 +250,9 @@
     x = jnp.where(half == 1, recv_ref[...], x_buf[...])
     stats = []
     for l in range(DEPTH):
-        stats.append(unpack_rows(stat_ref[l]))
+        stats.append(read_stats(a_ref, l))
         xs_ref[l] = x
-        conv = forward_layer(x, l, w_ref, stats[l], pad_ref)
+        conv = forward_layer(x, l, a_ref, b_ref, stats[l], pad_ref)
         conv_ref[l] = conv
         if l < DEPTH - 1:
             x = activate(conv, stats[l])
@@ -269,7 +263,7 @@
     dx_ref[...] = upstream
 
 
-def last_kernel(cot_any, recv_ref, xs_ref, conv_ref, flip_ref, stat_ref, send_ref, u_buf, pad_ref, u_sem):
+def last_kernel(cot_any, recv_ref, xs_ref, conv_ref, flip_ref, a_ref, send_ref, u_buf, pad_ref, u_sem):
     half, z, _ = place()
     u_copy = pltpu.make_async_copy(cot_any.at[z], u_buf, u_sem)
     u_copy.start()
@@ -277,7 +271,7 @@
     u_copy.wait()
     upstream = jnp.where(half == 1, u_buf[...], recv_ref[...])
     for l in reversed(range(DEPTH)):
-        stat = unpack_rows(stat_ref[l])
+        stat = read_stats(a_ref, l)
         upstream = backward_layer(upstream, xs_ref[l], conv_ref[l], l, flip_ref, stat, pad_ref, send_ref)
 
 
@@ -289,13 +283,12 @@
 def first(images, a, b):
     return pl.pallas_call(
         first_kernel,
-        out_shape=(MAP, KERNELS, jax.ShapeDtypeStruct((DEPTH, STAT, C), BF)),
+        out_shape=MAP,
         in_specs=[any_spec(), vmem_spec(), vmem_spec()],
-        out_specs=(vmem_spec(),) * 3,
+        out_specs=vmem_spec(),
         scratch_shapes=[
             pltpu.VMEM((PX, C), BF),
             pltpu.VMEM((3, PAD, C), BF),
-            pltpu.SemaphoreType.DMA((3, DEPTH)),
             pltpu.SemaphoreType.DMA,
         ],
         compiler_params=params(),
@@ -303,18 +296,18 @@
     )(images, a, b)
 
 
-def flip(w):
+def flip(a, b):
     return pl.pallas_call(
         flip_kernel,
         out_shape=KERNELS,
-        in_specs=[vmem_spec()],
+        in_specs=[vmem_spec()] * 2,
         out_specs=vmem_spec(),
         compiler_params=params(),
         name="flip",
-    )(w)
-
-
-def middle(images, cot, recv, w, flipped, stat):
+    )(a, b)
+
+
+def middle(images, cot, recv, a, b, flipped):
     return pl.pallas_call(
         middle_kernel,
         out_shape=(
@@ -333,10 +326,10 @@
         ],
         compiler_params=params(),
         name="middle",
-    )(images, cot, recv, w, flipped, stat)
-
-
-def last(cot, recv, xs, conv, flipped, stat):
+    )(images, cot, recv, a, b, flipped)
+
+
+def last(cot, recv, xs, conv, flipped, a):
     return pl.pallas_call(
         last_kernel,
         out_shape=SENT,
@@ -349,7 +342,7 @@
         ],
         compiler_params=params(),
         name="last",
-    )(cot, recv, xs, conv, flipped, stat)
+    )(cot, recv, xs, conv, flipped, a)
 
 
 def half_gradient(flip_ref, pad_ref, w_ref, grad_energy_ref, half, out_ref):
@@ -512,10 +505,16 @@
     out_any, wide_ref, sem = refs[-3:]
     _, _, core = place()
     half = core if own else 1 - core
-    wide_ref[...] = value_ref[...].reshape(TAPS, BLOCK, C).astype(F32)
-    copy = pltpu.make_async_copy(wide_ref, out_any.at[:, pl.ds(pl.multiple_of(half * BLOCK, BLOCK), BLOCK)], sem)
-    copy.start()
-    copy.wait()
+    value = value_ref[...].reshape(TAPS, BLOCK, C)
+    rows = pl.ds(pl.multiple_of(half * BLOCK, BLOCK), BLOCK)
+    copies = []
+    for k in range(3):
+        taps = slice(3 * k, 3 * k + 3)
+        wide_ref[taps] = value[taps].astype(F32)
+        copies.append(pltpu.make_async_copy(wide_ref.at[taps], out_any.at[taps, rows], sem.at[k]))
+        copies[k].start()
+    for copy in copies:
+        copy.wait()
 
 
 def widen(value, target=None):
@@ -527,7 +526,7 @@
         in_specs=[vmem_spec(), hbm][: len(args)],
         out_specs=hbm,
         input_output_aliases={1: 0} if len(args) == 2 else {},
-        scratch_shapes=[pltpu.VMEM((TAPS, BLOCK, C), F32), pltpu.SemaphoreType.DMA],
+        scratch_shapes=[pltpu.VMEM((TAPS, BLOCK, C), F32), pltpu.SemaphoreType.DMA((3,))],
         compiler_params=params(),
         name="own" if target is None else "rest",
     )(*args)
@@ -551,12 +550,12 @@
     b = near(lax.ppermute(a, "dp", sibling))
     a = near(a)
 
-    act, kernels, stat = first(images, a, b)
-    flipped = flip(kernels)
+    act = first(images, a, b)
+    flipped = flip(a, b)
     arrived = near(lax.ppermute(act, "segment", across))
-    dx, xs, conv, _ = middle(images, cotangent, arrived, kernels, flipped, stat)
+    dx, xs, conv, _ = middle(images, cotangent, arrived, a, b, flipped)
     returned = near(lax.ppermute(dx, "segment", across))
-    sent = last(cotangent, returned, xs, conv, flipped, stat)
+    sent = last(cotangent, returned, xs, conv, flipped, a)
 
     r = near(lax.all_to_all(sent, "segment", 0, 0, axis_index_groups=planes))
     give, extra, part, flipped_maps, padded, grad_energy = give_half(
@@ -571,9 +570,9 @@
     grad_latent = part + lax.ppermute(part, "segment", [(i, i ^ 2) for i in range(segments)])
     spread_share, grad_latent = lax.optimization_barrier((share(shares), grad_latent))
     mine = lax.all_to_all(near(spread_share), "dp", 0, 0, axis_index_groups=cores)
+    other = near(lax.ppermute(mine, "dp", sibling))
+    mine, shares = lax.optimization_barrier((mine, shares))
     grad_affine, grad_bias = affine_gradient(shares, width)
-    mine, grad_affine, grad_bias = lax.optimization_barrier((mine, grad_affine, grad_bias))
-    other = near(lax.ppermute(mine, "dp", sibling))
     grad_weight = widen(other, widen(near(mine))).reshape(weight.shape)
     return (grad_weight, grad_affine[None], grad_bias, grad_latent)
 

time: 129 us -> 127 us (0.984)
  blocking collectives: 49.6 us -> 60.1 us
  waiting for transfers between devices: 26.1 us -> 18.4 us
  starting transfers between devices: 27.3 us -> 24.6 us
  Pallas kernels: 23.7 us -> 21.6 us
    all_to_all x0 -> x1, blocking collectives: none -> 10.5 us  [body(): lax.all_to_all(near(spread_share), 'dp', 0, 0, axis_index_groups=cores)]
    all_to_all x1 -> x0, waiting for transfers between devices: 6.97 us -> none  [body(): lax.all_to_all(near(spread_share), 'dp', 0, 0, axis_index_groups=cores)]
    all_to_all x1 -> x0, starting transfers between devices: 3.54 us -> none  [body(): lax.all_to_all(near(spread_share), 'dp', 0, 0, axis_index_groups=cores)]
  transfers between devices with their start and end apart: 10 -> 9, of which waited for: 9 -> 7; matrix products, arithmetic and copies ran while one was open for 0% -> 0% of each run, Pallas kernels for 3% -> 3%
where the time goes in v5:
time: 127 us; the launch traced here: 126 us
  blocking collectives  60.1 us (47%)
  starting transfers between devices  24.6 us (19%)
  Pallas kernels  21.6 us (17%)
  waiting for transfers between devices  18.4 us (14%)
    all_to_all x1, blocking collectives, body(): a = lax.all_to_all(send, 'segment', 0, 0, axis_index_groups=planes)  34.2 us
    all_to_all x1, blocking collectives, body(): r = near(lax.all_to_all(sent, 'segment', 0, 0, axis_index_groups=planes))  15.4 us
    all_to_all x1, blocking collectives, body(): lax.all_to_all(near(spread_share), 'dp', 0, 0, axis_index_groups=cores)  10.5 us
    pallas_call x1, Pallas kernels, middle(): pl.pallas_call(middle_kernel, out_shape=(MAP, jax.ShapeDtypeStruct((DEPTH...  5.77 us
    all_to_all x1, starting transfers between devices, body(): lax.all_to_all(near(shared), 'dp', 0, 0, axis_index_groups=cores)  5.12 us
    ppermute x1, starting transfers between devices, body(): other = near(lax.ppermute(mine, 'dp', sibling))  4.37 us
    ppermute x1, waiting for transfers between devices, body(): b = near(lax.ppermute(a, 'dp', sibling))  4.21 us
    all_to_all x1, waiting for transfers between devices, body(): lax.all_to_all(near(shared), 'dp', 0, 0, axis_index_groups=cores)  3.62 us
  transfers between devices with their start and end apart: 9, of which 7 were waited for; matrix products, arithmetic and copies ran while one was open for 0% of the time, Pallas kernels for 3%

profile of v5, /device:TPU:1, one launch (start us, length us, event | category | flops | bytes accessed | tf_op | source)
XLA Modules:
  0.0 126.3 jit_solution(13534427928740103812)
XLA Ops:
  0.6 2.5 %prepare.1 = (bf16[4,2336,128]{2,1,0:T(8,128)(2,1)S(1)}, f32[8,256]{1,0:T(8,128)S(1)}, f32[8,256]{1,0:T(8,128)S(1)}, f32[256,256]{1,0:T(8,128)S(1)}) custom-call(f32[4,512]{1,0:T(4,128)} %latent_ref.1, f32[512,256]{1,0:T(8,128)} %bitcast.9, bf16[2304,256]{1,0:T(8,128)(2,1)} %bitcast.6, f32[1,256]{1,0:T(1,128)} %bias_hbm.1), custom_call_target="tpu_custom_call" | custom-call | tf_op jit(solution)/shard_map/prepare/pallas_call | solution.py:127
  3.1 0.0 copy-start.3
  3.1 34.2 %all_to_all.20.a_ref = bf16[4,2336,128]{2,1,0:T(8,128)(2,1)S(1)} all-to-all(bf16[4,2336,128]{2,1,0:T(8,128)(2,1)S(1)} %get-tuple-element.25), channel_id=1, replica_groups={{0,16,32,48},{64,80,96,112},{1,17,33,49},{65,81,97,113},{2,18,34,50},{6..., dimensions={0} | all-to-all | bytes 4784128 | tf_op jit(solution)/shard_map/all_to_all | solution.py:549
  37.3 2.1 %collective-permute-start = (bf16[4,2336,128]{2,1,0:T(8,128)(2,1)S(1)}, bf16[4,2336,128]{2,1,0:T(8,128)(2,1)S(1)}, u32[]{:S(2)}, u32[]{:S(2)}) collective-permute-start(bf16[4,2336,128]{2,1,0:T(8,128)(2,1)S(1)} %all_to_all.20.a_ref), channel_id=1, source_target_pairs={{0,1},{1,0},{2,3},{3,2},{4,5},{5,4},{6,7},{7,6},{8,9},{9,8},{10,11... | collective-permute-start | bytes 7176200 | tf_op jit(solution)/shard_map/ppermute | solution.py:550
  39.3 4.2 %collective-permute-done.b_ref = bf16[4,2336,128]{2,1,0:T(8,128)(2,1)S(1)} collective-permute-done((bf16[4,2336,128]{2,1,0:T(8,128)(2,1)S(1)}, bf16[4,2336,128]{2,1,0:T(8,128)(2,1)S(1)}, u32[]{:S(2)}, u32[]{:S(2)}) %collective-permute-start) | collective-permute-done | bytes 2392096 | tf_op jit(solution)/shard_map/ppermute | solution.py:550
  43.5 0.0 copy-done.3
  43.6 2.2 %first.1 = bf16[256,256]{1,0:T(8,128)(2,1)S(1)} custom-call(bf16[4,256,256]{2,1,0:T(8,128)(2,1)S(1)} %bitcast.13, bf16[4,2336,128]{2,1,0:T(8,128)(2,1)S(1)} %all_to_all.20.a_ref, bf16[4,2336,128]{2,1,0:T(8,128)(2,1)S(1)} %collective-permute-done.b_ref), custom_call_target="tpu_custom_call" | custom-call | tf_op jit(solution)/shard_map/first/pallas_call | solution.py:284
  45.8 0.0 copy-start.2
  45.8 2.8 %collective-permute-start.1 = (bf16[256,256]{1,0:T(8,128)(2,1)S(1)}, bf16[256,256]{1,0:T(8,128)(2,1)S(1)}, u32[]{:S(2)}, u32[]{:S(2)}) collective-permute-start(bf16[256,256]{1,0:T(8,128)(2,1)S(1)} %first.1), channel_id=1, source_target_pairs={{0,64},{16,80},{32,96},{48,112},{64,0},{80,16},{96,32},{112,48},{1... | collective-permute-start | bytes 393224 | tf_op jit(solution)/shard_map/ppermute | solution.py:555
  48.6 1.3 flip.1.flip_ref
  49.9 2.2 %collective-permute-done.1.recv_ref = bf16[256,256]{1,0:T(8,128)(2,1)S(1)} collective-permute-done((bf16[256,256]{1,0:T(8,128)(2,1)S(1)}, bf16[256,256]{1,0:T(8,128)(2,1)S(1)}, u32[]{:S(2)}, u32[]{:S(2)}) %collective-permute-start.1) | collective-permute-done | bytes 131104 | tf_op jit(solution)/shard_map/ppermute | solution.py:555
  52.1 0.0 copy-done.2
  52.1 5.8 %middle.1 = (bf16[256,256]{1,0:T(8,128)(2,1)S(1)}, bf16[4,256,256]{2,1,0:T(8,128)(2,1)S(1)}, f32[4,256,256]{2,1,0:T(8,128)S(1)}, bf16[4,528,256]{2,1,0:T(8,128)(2,1)}) custom-call(bf16[4,256,256]{2,1,0:T(8,128)(2,1)S(1)} %bitcast.14, bf16[4,256,256]{2,1,0:T(8,128)(2,1)S(1)} %bitcast.11, bf16[256,256]{1,0:T(8,128)(2,1)S(1)} %collective-permute-done.1.recv_ref, ...), custom_call_target="tpu_custom_call" | custom-call | tf_op jit(solution)/shard_map/middle/pallas_call | solution.py:311
  57.9 2.8 %collective-permute-start.2 = (bf16[256,256]{1,0:T(8,128)(2,1)S(1)}, bf16[256,256]{1,0:T(8,128)(2,1)S(1)}, u32[]{:S(2)}, u32[]{:S(2)}) collective-permute-start(bf16[256,256]{1,0:T(8,128)(2,1)S(1)} %get-tuple-element.26), channel_id=1, source_target_pairs={{0,64},{16,80},{32,96},{48,112},{64,0},{80,16},{96,32},{112,48},{1... | collective-permute-start | bytes 393224 | tf_op jit(solution)/shard_map/ppermute | solution.py:557
  60.7 2.6 %collective-permute-done.2.recv_ref = bf16[256,256]{1,0:T(8,128)(2,1)S(1)} collective-permute-done((bf16[256,256]{1,0:T(8,128)(2,1)S(1)}, bf16[256,256]{1,0:T(8,128)(2,1)S(1)}, u32[]{:S(2)}, u32[]{:S(2)}) %collective-permute-start.2) | collective-permute-done | bytes 131104 | tf_op jit(solution)/shard_map/ppermute | solution.py:557
  63.3 0.0 copy-start.4
  63.3 2.6 %last.1 = bf16[4,528,256]{2,1,0:T(8,128)(2,1)S(1)} custom-call(bf16[4,256,256]{2,1,0:T(8,128)(2,1)S(1)} %bitcast.12, bf16[256,256]{1,0:T(8,128)(2,1)S(1)} %collective-permute-done.2.recv_ref, bf16[4,256,256]{2,1,0:T(8,128)(2,1)S(1)} %get-tuple-element.27.xs_ref, f32[4,256,256]{2,1,0:T(8,128)S(1)} %get-tuple-element.28.conv_ref, ...), custom_call_target="tpu_custom_call" | custom-call | tf_op jit(solution)/shard_map/last/pallas_call | solution.py:333
  65.9 0.0 copy-start
  65.9 0.0 copy-start.1
  65.9 15.4 %all_to_all.21.r_ref = bf16[4,528,256]{2,1,0:T(8,128)(2,1)S(1)} all-to-all(bf16[4,528,256]{2,1,0:T(8,128)(2,1)S(1)} %last.1), channel_id=1, replica_groups={{0,16,32,48},{64,80,96,112},{1,17,33,49},{65,81,97,113},{2,18,34,50},{6..., dimensions={0} | all-to-all | bytes 2162688 | tf_op jit(solution)/shard_map/all_to_all | solution.py:560
  81.3 0.0 copy-done.4
  81.3 0.0 copy-done
  81.3 0.0 copy-done.1
  81.3 2.3 %give.1 = (bf16[1168,256]{1,0:T(8,128)(2,1)S(1)}, bf16[16,256]{1,0:T(8,128)(2,1)S(1)}, f32[4,512]{1,0:T(4,128)S(1)}, bf16[256,1024]{1,0:T(8,128)(2,1)S(1)}, bf16...) custom-call(bf16[4,528,256]{2,1,0:T(8,128)(2,1)S(1)} %all_to_all.21.r_ref, bf16[2304,256]{1,0:T(8,128)(2,1)S(1)} %bitcast.7, ...), custom_call_target="tpu_custom_call" | custom-call | tf_op jit(solution)/shard_map/give/pallas_call | solution.py:401
  83.6 3.6 %collective-permute-start.3 = (bf16[1168,256]{1,0:T(8,128)(2,1)S(1)}, bf16[1168,256]{1,0:T(8,128)(2,1)S(1)}, u32[]{:S(2)}, u32[]{:S(2)}) collective-permute-start(bf16[1168,256]{1,0:T(8,128)(2,1)S(1)} %get-tuple-element.36), channel_id=1, source_target_pairs={{0,1},{1,0},{2,3},{3,2},{4,5},{5,4},{6,7},{7,6},{8,9},{9,8},{10,11... | collective-permute-start | bytes 1794056 | tf_op jit(solution)/shard_map/ppermute | solution.py:564
  87.2 2.8 %collective-permute-start.4 = (f32[4,512]{1,0:T(4,128)S(1)}, f32[4,512]{1,0:T(4,128)S(1)}, u32[]{:S(2)}, u32[]{:S(2)}) collective-permute-start(f32[4,512]{1,0:T(4,128)S(1)} %get-tuple-element.37), channel_id=1, source_target_pairs={{0,64},{16,80},{32,96},{48,112},{64,0},{80,16},{96,32},{112,48},{1... | collective-permute-start | bytes 24584 | tf_op jit(solution)/shard_map/ppermute | solution.py:565
  89.9 0.8 keep.1.keep_ref
  90.7 0.4 collective-permute-done.4
  91.2 0.0 collective-permute-done.3.got_ref
  91.2 1.0 pair.1
  92.2 5.1 %all-to-all-start.2 = ((bf16[8,176,256]{2,1,0:T(8,128)(2,1)}), bf16[8,176,256]{2,1,0:T(8,128)(2,1)S(1)}, u32[]{:S(2)}, u32[]{:S(2)}) async-start(bf16[8,176,256]{2,1,0:T(8,128)(2,1)} %pair.1), calls=%async_computation.2 | async-start | bytes 1441792 | tf_op jit(solution)/shard_map/all_to_all | solution.py:568
  97.3 0.3 collective-permute-start.5
  97.6 2.2 %collective-permute-done.5 = f32[4,512]{1,0:T(4,128)S(1)} collective-permute-done((f32[4,512]{1,0:T(4,128)S(1)}, f32[4,512]{1,0:T(4,128)S(1)}, u32[]{:S(2)}, u32[]{:S(2)}) %collective-permute-start.5) | collective-permute-done | bytes 8224 | tf_op jit(solution)/shard_map/ppermute | solution.py:569
  99.8 0.8 collective-permute-start.6
  100.6 3.2 %collective-permute-done.6 = f32[4,512]{1,0:T(4,128)S(1)} collective-permute-done((f32[4,512]{1,0:T(4,128)S(1)}, f32[4,512]{1,0:T(4,128)S(1)}, u32[]{:S(2)}, u32[]{:S(2)}) %collective-permute-start.6) | collective-permute-done | bytes 8224 | tf_op jit(solution)/shard_map/ppermute | solution.py:570
  103.8 0.6 add.11
  104.4 3.6 %all-to-all-done.2.shares_ref = bf16[8,176,256]{2,1,0:T(8,128)(2,1)S(1)} async-done(((bf16[8,176,256]{2,1,0:T(8,128)(2,1)}), bf16[8,176,256]{2,1,0:T(8,128)(2,1)S(1)}, u32[]{:S(2)}, u32[]{:S(2)}) %all-to-all-start.2) | async-done | bytes 720928 | tf_op jit(solution)/shard_map/all_to_all | solution.py:568
  108.1 0.1 share.1
  108.1 10.5 %all_to_all.22.value_ref = bf16[8,144,256]{2,1,0:T(8,128)(2,1)S(1)} all-to-all(bf16[8,144,256]{2,1,0:T(8,128)(2,1)S(1)} %share.1), channel_id=1, replica_groups={{0,2,4,6,8,10,12,14},{1,3,5,7,9,11,13,15},{16,18,20,22,24,26,28,30},{17..., dimensions={0} | all-to-all | bytes 1179648 | tf_op jit(solution)/shard_map/all_to_all | solution.py:572
  118.6 4.4 %collective-permute-start.7 = (bf16[8,144,256]{2,1,0:T(8,128)(2,1)S(1)}, bf16[8,144,256]{2,1,0:T(8,128)(2,1)S(1)}, u32[]{:S(2)}, u32[]{:S(2)}) collective-permute-start(bf16[8,144,256]{2,1,0:T(8,128)(2,1)S(1)} %all_to_all.22.value_ref), channel_id=1, source_target_pairs={{0,1},{1,0},{2,3},{3,2},{4,5},{5,4},{6,7},{7,6},{8,9},{9,8},{10,11... | collective-permute-start | bytes 1769480 | tf_op jit(solution)/shard_map/ppermute | solution.py:573
  123.0 1.1 affine.1
  124.0 1.1 own.1.refs_0_
  125.1 0.0 collective-permute-done.7.value_ref
  125.1 1.1 rest.1
  (2 shorter events, 0.0 us)
Async XLA Ops:
  3.1 40.5 %copy-start.3 = (bf16[4,16,16,256]{3,2,1,0:T(8,128)(2,1)S(1)}, bf16[4,16,16,256]{3,2,1,0:T(8,128)(2,1)}, u32[]{:S(2)}) copy-start(bf16[4,16,16,256]{3,2,1,0:T(8,128)(2,1)} %param.6) | copy-start | bytes 1572868
  37.3 6.3 %collective-permute-start = (bf16[4,2336,128]{2,1,0:T(8,128)(2,1)S(1)}, bf16[4,2336,128]{2,1,0:T(8,128)(2,1)S(1)}, u32[]{:S(2)}, u32[]{:S(2)}) collective-permute-start(bf16[4,2336,128]{2,1,0:T(8,128)(2,1)S(1)} %all_to_all.20.a_ref), channel_id=1, source_target_pairs={{0,1},{1,0},{2,3},{3,2},{4,5},{5,4},{6,7},{7,6},{8,9},{9,8},{10,11... | collective-permute-start | bytes 7176200 | tf_op jit(solution)/shard_map/ppermute | solution.py:550
  45.8 6.3 %copy-start.2 = (bf16[4,16,16,256]{3,2,1,0:T(8,128)(2,1)S(1)}, bf16[4,16,16,256]{3,2,1,0:T(8,128)(2,1)}, u32[]{:S(2)}) copy-start(bf16[4,16,16,256]{3,2,1,0:T(8,128)(2,1)} %param.11) | copy-start | bytes 1572868
  45.8 6.3 %collective-permute-start.1 = (bf16[256,256]{1,0:T(8,128)(2,1)S(1)}, bf16[256,256]{1,0:T(8,128)(2,1)S(1)}, u32[]{:S(2)}, u32[]{:S(2)}) collective-permute-start(bf16[256,256]{1,0:T(8,128)(2,1)S(1)} %first.1), channel_id=1, source_target_pairs={{0,64},{16,80},{32,96},{48,112},{64,0},{80,16},{96,32},{112,48},{1... | collective-permute-start | bytes 393224 | tf_op jit(solution)/shard_map/ppermute | solution.py:555
  57.9 5.4 %collective-permute-start.2 = (bf16[256,256]{1,0:T(8,128)(2,1)S(1)}, bf16[256,256]{1,0:T(8,128)(2,1)S(1)}, u32[]{:S(2)}, u32[]{:S(2)}) collective-permute-start(bf16[256,256]{1,0:T(8,128)(2,1)S(1)} %get-tuple-element.26), channel_id=1, source_target_pairs={{0,64},{16,80},{32,96},{48,112},{64,0},{80,16},{96,32},{112,48},{1... | collective-permute-start | bytes 393224 | tf_op jit(solution)/shard_map/ppermute | solution.py:557
  63.3 18.1 %copy-start.4 = (f32[4,512]{1,0:T(4,128)S(1)}, f32[4,512]{1,0:T(4,128)}, u32[]{:S(2)}) copy-start(f32[4,512]{1,0:T(4,128)} %latent_ref.1) | copy-start | bytes 24580
  65.9 15.5 %copy-start = (bf16[1,3,3,256,256]{4,3,2,1,0:T(8,128)(2,1)S(1)}, bf16[1,3,3,256,256]{4,3,2,1,0:T(8,128)(2,1)}, u32[]{:S(2)}) copy-start(bf16[1,3,3,256,256]{4,3,2,1,0:T(8,128)(2,1)} %param.8) | copy-start | bytes 3538948
  65.9 15.5 %copy-start.1 = (f32[1,512,256]{2,1,0:T(8,128)S(1)}, f32[1,512,256]{2,1,0:T(8,128)}, u32[]{:S(2)}) copy-start(f32[1,512,256]{2,1,0:T(8,128)} %param.9) | copy-start | bytes 1572868
  83.6 7.6 %collective-permute-start.3 = (bf16[1168,256]{1,0:T(8,128)(2,1)S(1)}, bf16[1168,256]{1,0:T(8,128)(2,1)S(1)}, u32[]{:S(2)}, u32[]{:S(2)}) collective-permute-start(bf16[1168,256]{1,0:T(8,128)(2,1)S(1)} %get-tuple-element.36), channel_id=1, source_target_pairs={{0,1},{1,0},{2,3},{3,2},{4,5},{5,4},{6,7},{7,6},{8,9},{9,8},{10,11... | collective-permute-start | bytes 1794056 | tf_op jit(solution)/shard_map/ppermute | solution.py:564
  87.2 4.0 %collective-permute-start.4 = (f32[4,512]{1,0:T(4,128)S(1)}, f32[4,512]{1,0:T(4,128)S(1)}, u32[]{:S(2)}, u32[]{:S(2)}) collective-permute-start(f32[4,512]{1,0:T(4,128)S(1)} %get-tuple-element.37), channel_id=1, source_target_pairs={{0,64},{16,80},{32,96},{48,112},{64,0},{80,16},{96,32},{112,48},{1... | collective-permute-start | bytes 24584 | tf_op jit(solution)/shard_map/ppermute | solution.py:565
  92.2 15.9 %all-to-all-start.2 = ((bf16[8,176,256]{2,1,0:T(8,128)(2,1)}), bf16[8,176,256]{2,1,0:T(8,128)(2,1)S(1)}, u32[]{:S(2)}, u32[]{:S(2)}) async-start(bf16[8,176,256]{2,1,0:T(8,128)(2,1)} %pair.1), calls=%async_computation.2 | async-start | bytes 1441792 | tf_op jit(solution)/shard_map/all_to_all | solution.py:568
  97.3 2.5 %collective-permute-start.5 = (f32[4,512]{1,0:T(4,128)S(1)}, f32[4,512]{1,0:T(4,128)S(1)}, u32[]{:S(2)}, u32[]{:S(2)}) collective-permute-start(f32[4,512]{1,0:T(4,128)S(1)} %add.9), channel_id=1, source_target_pairs={{0,16},{16,0},{32,48},{48,32},{64,80},{80,64},{96,112},{112,96},{1... | collective-permute-start | bytes 24584 | tf_op jit(solution)/shard_map/ppermute | solution.py:569
  99.8 4.0 %collective-permute-start.6 = (f32[4,512]{1,0:T(4,128)S(1)}, f32[4,512]{1,0:T(4,128)S(1)}, u32[]{:S(2)}, u32[]{:S(2)}) collective-permute-start(f32[4,512]{1,0:T(4,128)S(1)} %add.10), channel_id=1, source_target_pairs={{0,32},{16,48},{32,0},{48,16},{64,96},{80,112},{96,64},{112,80},{1... | collective-permute-start | bytes 24584 | tf_op jit(solution)/shard_map/ppermute | solution.py:570
  118.6 6.5 %collective-permute-start.7 = (bf16[8,144,256]{2,1,0:T(8,128)(2,1)S(1)}, bf16[8,144,256]{2,1,0:T(8,128)(2,1)S(1)}, u32[]{:S(2)}, u32[]{:S(2)}) collective-permute-start(bf16[8,144,256]{2,1,0:T(8,128)(2,1)S(1)} %all_to_all.22.value_ref), channel_id=1, source_target_pairs={{0,1},{1,0},{2,3},{3,2},{4,5},{5,4},{6,7},{7,6},{8,9},{9,8},{10,11... | collective-permute-start | bytes 1769480 | tf_op jit(solution)/shard_map/ppermute | solution.py:573

commit v6 on v5

--- a/solution.py
+++ b/solution.py
@@ -195,22 +195,19 @@
     return (GAIN * hidden * (0.6 + 0.4 * jnp.tanh(hidden))).astype(BF)
 
 
-def backward_layer(upstream, x, conv, l, flip_ref, stat, pad_ref, send_ref):
+def backward_layer(upstream, x, conv, l, flip_ref, stat, pad_ref, send_ref=None):
     styles, demod, bias = stat
     hidden = conv * demod + bias
     t = jnp.tanh(hidden)
     dh = upstream.astype(F32) * (GAIN * (0.6 + 0.4 * t + 0.4 * hidden * (1.0 - t * t)))
-    grad_bias = jnp.sum(dh, axis=0, keepdims=True)
-    grad_demod = jnp.sum(dh * conv, axis=0, keepdims=True)
-    grad_conv = (dh * demod).astype(BF).astype(F32)
-    spread(pad_ref, grad_conv)
-    send_ref[l, PX : 2 * PX, :] = pad_ref[1, ROW : ROW + PX, :]
-    total = taps_matmul(pad_ref, flip_ref[l], True)
-    grad_scaled = total.astype(BF).astype(F32)
-    xf = x.astype(F32)
-    grad_styles = jnp.sum(grad_scaled * xf, axis=0, keepdims=True)
-    send_ref[l, 0:PX, :] = (xf * styles).astype(BF)
-    send_ref[l, 2 * PX : 2 * PX + STAT, :] = pack_rows([grad_styles, grad_demod, grad_bias])
+    spread(pad_ref, (dh * demod).astype(BF).astype(F32))
+    grad_scaled = taps_matmul(pad_ref, flip_ref[l], True).astype(BF).astype(F32)
+    if send_ref is not None:
+        grad_bias = jnp.sum(dh, axis=0, keepdims=True)
+        grad_demod = jnp.sum(dh * conv, axis=0, keepdims=True)
+        grad_styles = jnp.sum(grad_scaled * x.astype(F32), axis=0, keepdims=True)
+        send_ref[l, 0:PX, :] = pad_ref[1, ROW : ROW + PX, :]
+        send_ref[l, PX : PX + STAT, :] = pack_rows([grad_styles, grad_demod, grad_bias])
     return (grad_scaled * styles).astype(BF)
 
 
@@ -237,7 +234,7 @@
 
 
 def middle_kernel(
-    images_any, cot_any, recv_ref, a_ref, b_ref, flip_ref, dx_ref, xs_ref, conv_ref, send_ref,
+    images_any, cot_any, recv_ref, a_ref, b_ref, flip_ref, dx_ref, xs_ref, conv_ref, scaled_ref,
     x_buf, u_buf, pad_ref, x_sem,
 ):
     half, z, _ = place()
@@ -254,12 +251,13 @@
         xs_ref[l] = x
         conv = forward_layer(x, l, a_ref, b_ref, stats[l], pad_ref)
         conv_ref[l] = conv
+        scaled_ref[lax.rem(l - z + DEPTH, DEPTH)] = pad_ref[1, ROW : ROW + PX, :]
         if l < DEPTH - 1:
             x = activate(conv, stats[l])
     u_copy.wait()
     upstream = u_buf[...]
     for l in reversed(range(DEPTH)):
-        upstream = backward_layer(upstream, xs_ref[l], conv_ref[l], l, flip_ref, stats[l], pad_ref, send_ref)
+        upstream = backward_layer(upstream, xs_ref[l], conv_ref[l], l, flip_ref, stats[l], pad_ref)
     dx_ref[...] = upstream
 
 
@@ -277,7 +275,7 @@
 
 MAP = jax.ShapeDtypeStruct((PX, C), BF)
 KERNELS = jax.ShapeDtypeStruct((DEPTH, ROWS, C), BF)
-SENT = jax.ShapeDtypeStruct((DEPTH, 2 * PX + STAT, C), BF)
+SENT = jax.ShapeDtypeStruct((DEPTH, PX + STAT, C), BF)
 
 
 def first(images, a, b):
@@ -314,7 +312,7 @@
             MAP,
             jax.ShapeDtypeStruct((DEPTH, PX, C), BF),
             jax.ShapeDtypeStruct((DEPTH, PX, C), F32),
-            SENT,
+            jax.ShapeDtypeStruct((DEPTH, PX, C), BF),
         ),
         in_specs=[any_spec(), any_spec()] + [vmem_spec()] * 4,
         out_specs=(vmem_spec(),) * 4,
@@ -360,12 +358,28 @@
             out_ref[tap * BLOCK : (tap + 1) * BLOCK, :] = (part + w * grad_energy).astype(BF)
 
 
+def turn_kernel(s0_ref, s1_ref, s2_ref, s3_ref, flip_ref):
+    for k, ref in enumerate((s0_ref, s1_ref, s2_ref, s3_ref)):
+        flip_ref[:, k * PX : (k + 1) * PX] = ref[...].T
+
+
+def turn(*maps):
+    return pl.pallas_call(
+        turn_kernel,
+        out_shape=jax.ShapeDtypeStruct((C, DEPTH * PX), BF),
+        in_specs=[vmem_spec()] * DEPTH,
+        out_specs=vmem_spec(),
+        compiler_params=params(),
+        name="turn",
+    )(*maps)
+
+
 def give_kernel(
-    r_ref, w_ref, styles_ref, demod_ref, energy_ref, affine_ref, latent_ref,
-    give_ref, extra_ref, grad_latent_ref, flip_ref, pad_ref, grad_energy_ref, rows_ref,
+    r_ref, flip_ref, w_ref, styles_ref, demod_ref, energy_ref, affine_ref, latent_ref,
+    give_ref, extra_ref, grad_latent_ref, pad_ref, grad_energy_ref, rows_ref,
 ):
-    _, _, core = place()
-    parts = [unpack_rows(r_ref[n, 2 * PX : 2 * PX + STAT, :]) for n in range(DEPTH)]
+    _, z, core = place()
+    parts = [unpack_rows(r_ref[n, PX : PX + STAT, :]) for n in range(DEPTH)]
     styles = styles_ref[...]
     demod = demod_ref[...]
     grad_sum = stack_rows([p[1] for p in parts]) * (-0.5) * demod * demod * demod
@@ -390,30 +404,28 @@
     grad_energy_ref[...] = 2.0 * lax.dot_general(
         squares, grad_sum, (((0,), (0,)), ((), ())), precision=HI, preferred_element_type=F32
     )
-    for n in range(DEPTH):
-        clear_pads(pad_ref.at[n])
-        spread(pad_ref.at[n], r_ref[n, PX : 2 * PX, :].astype(F32))
-        flip_ref[:, n * PX : (n + 1) * PX] = r_ref[n, 0:PX, :].astype(F32).T.astype(BF)
+    for k in range(DEPTH):
+        clear_pads(pad_ref.at[k])
+        spread(pad_ref.at[k], r_ref[lax.rem(z - k + DEPTH, DEPTH), 0:PX, :].astype(F32))
     half_gradient(flip_ref, pad_ref, w_ref, grad_energy_ref, 1 - core, give_ref)
 
 
-def give_half(r, w, styles, demod, energy, affine, latent):
+def give_half(r, turned, w, styles, demod, energy, affine, latent):
     return pl.pallas_call(
         give_kernel,
         out_shape=(
             jax.ShapeDtypeStruct((HALF + STAT, C), BF),
             jax.ShapeDtypeStruct((STAT, C), BF),
             jax.ShapeDtypeStruct((DEPTH, affine.shape[0]), F32),
-            jax.ShapeDtypeStruct((C, DEPTH * PX), BF),
             jax.ShapeDtypeStruct((DEPTH, 3, PAD, C), BF),
             jax.ShapeDtypeStruct((C, C), F32),
         ),
-        in_specs=[vmem_spec()] * 7,
-        out_specs=(vmem_spec(),) * 6,
+        in_specs=[vmem_spec()] * 8,
+        out_specs=(vmem_spec(),) * 5,
         scratch_shapes=[pltpu.VMEM((STAT, C), F32)],
         compiler_params=params(),
         name="give",
-    )(r, w, styles, demod, energy, affine, latent)
+    )(r, turned, w, styles, demod, energy, affine, latent)
 
 
 def keep_kernel(flip_ref, pad_ref, w_ref, grad_energy_ref, keep_ref):
@@ -553,17 +565,24 @@
     act = first(images, a, b)
     flipped = flip(a, b)
     arrived = near(lax.ppermute(act, "segment", across))
-    dx, xs, conv, _ = middle(images, cotangent, arrived, a, b, flipped)
+    dx, xs, conv, scaled = middle(images, cotangent, arrived, a, b, flipped)
     returned = near(lax.ppermute(dx, "segment", across))
-    sent = last(cotangent, returned, xs, conv, flipped, a)
+    maps = [scaled[0]] + [
+        lax.ppermute(
+            scaled[k], "segment", [(i, i - i % DEPTH + (i + k) % DEPTH) for i in range(segments)]
+        )
+        for k in range(1, DEPTH)
+    ]
+    sent, *maps = lax.optimization_barrier((last(cotangent, returned, xs, conv, flipped, a), *maps))
+    turned = turn(*[near(value) for value in maps])
 
     r = near(lax.all_to_all(sent, "segment", 0, 0, axis_index_groups=planes))
-    give, extra, part, flipped_maps, padded, grad_energy = give_half(
-        r, w, styles, demod, energy, affine[0], latent
+    give, extra, part, padded, grad_energy = give_half(
+        r, turned, w, styles, demod, energy, affine[0], latent
     )
     got = near(lax.ppermute(give, "dp", sibling))
     part = part + lax.ppermute(part, "segment", across)
-    keep = keep_half(flipped_maps, padded, w, grad_energy)
+    keep = keep_half(turned, padded, w, grad_energy)
     shared, part = lax.optimization_barrier((pair(keep, extra, got), part))
     shares = near(lax.all_to_all(near(shared), "dp", 0, 0, axis_index_groups=cores))
     part = part + lax.ppermute(part, "segment", [(i, i ^ 1) for i in range(segments)])

time: 127 us -> 124 us (0.976)
  blocking collectives: 60.1 us -> 44.6 us
  waiting for transfers between devices: 18.4 us -> 27.4 us
  starting transfers between devices: 24.6 us -> 27.1 us
  local copies, waits for them, and re-layouts: 0.03 us -> 1.62 us
    all_to_all x1 -> x0, blocking collectives: 15.4 us -> none  [body(): r = near(lax.all_to_all(sent, 'segment', 0, 0, axis_index_groups=planes))]
    all_to_all x0 -> x1, waiting for transfers between devices: none -> 5.87 us  [body(): r = near(lax.all_to_all(sent, 'segment', 0, 0, axis_index_groups=planes))]
    all_to_all x0 -> x1, starting transfers between devices: none -> 3.65 us  [body(): r = near(lax.all_to_all(sent, 'segment', 0, 0, axis_index_groups=planes))]
    ppermute x0 -> x3, waiting for transfers between devices: none -> 2.63 us  [body(): lax.ppermute(scaled[k], 'segment', [(i, i - i % DEPTH + (i + k) % DEPTH)...]
    ppermute x1, starting transfers between devices: 2.77 us -> 0.24 us  [body(): part = part + lax.ppermute(part, 'segment', across)]
    ppermute x1, waiting for transfers between devices: 0.44 us -> 2.96 us  [body(): part = part + lax.ppermute(part, 'segment', across)]
    ppermute x1, waiting for transfers between devices: 2.57 us -> 0.36 us  [body(): returned = near(lax.ppermute(dx, 'segment', across))]
    ppermute x0 -> x3, starting transfers between devices: none -> 2.15 us  [body(): lax.ppermute(scaled[k], 'segment', [(i, i - i % DEPTH + (i + k) % DEPTH)...]
  transfers between devices with their start and end apart: 9 -> 13, of which waited for: 7 -> 10; matrix products, arithmetic and copies ran while one was open for 0% -> 1% of each run, Pallas kernels for 3% -> 6%
where the time goes in v6:
time: 124 us
  blocking collectives  44.6 us (36%)
  waiting for transfers between devices  27.4 us (22%)
  starting transfers between devices  27.1 us (22%)
  Pallas kernels  21.3 us (17%)
  local copies, waits for them, and re-layouts  1.62 us (1%)
    all_to_all x1, blocking collectives, body(): a = lax.all_to_all(send, 'segment', 0, 0, axis_index_groups=planes)  34.2 us
    all_to_all x1, blocking collectives, body(): lax.all_to_all(near(spread_share), 'dp', 0, 0, axis_index_groups=cores)  10.5 us
    all_to_all x1, waiting for transfers between devices, body(): r = near(lax.all_to_all(sent, 'segment', 0, 0, axis_index_groups=planes))  5.87 us
    pallas_call x1, Pallas kernels, middle(): pl.pallas_call(middle_kernel, out_shape=(MAP, jax.ShapeDtypeStruct((DEPTH...  4.46 us
    ppermute x1, starting transfers between devices, body(): other = near(lax.ppermute(mine, 'dp', sibling))  4.37 us
    ppermute x1, waiting for transfers between devices, body(): b = near(lax.ppermute(a, 'dp', sibling))  4.21 us
    all_to_all x1, starting transfers between devices, body(): lax.all_to_all(near(shared), 'dp', 0, 0, axis_index_groups=cores)  4.2 us
    ppermute x1, starting transfers between devices, body(): got = near(lax.ppermute(give, 'dp', sibling))  3.83 us
  transfers between devices with their start and end apart: 13, of which 10 were waited for; matrix products, arithmetic and copies ran while one was open for 1% of the time, Pallas kernels for 6%

profile of v6, /device:TPU:1, one launch (start us, length us, event | category | flops | bytes accessed | tf_op | source)
XLA Modules:
  0.0 123.7 jit_solution(13890803912888426098)
XLA Ops:
  0.6 2.5 %prepare.1 = (bf16[4,2336,128]{2,1,0:T(8,128)(2,1)S(1)}, f32[8,256]{1,0:T(8,128)S(1)}, f32[8,256]{1,0:T(8,128)S(1)}, f32[256,256]{1,0:T(8,128)S(1)}) custom-call(f32[4,512]{1,0:T(4,128)} %latent_ref.1, f32[512,256]{1,0:T(8,128)} %bitcast.17, bf16[2304,256]{1,0:T(8,128)(2,1)} %bitcast.14, f32[1,256]{1,0:T(1,128)} %bias_hbm.1), custom_call_target="tpu_custom_call" | custom-call | tf_op jit(solution)/shard_map/prepare/pallas_call | solution.py:127
  3.1 0.0 copy-start.3
  3.1 34.2 %all_to_all.20.a_ref = bf16[4,2336,128]{2,1,0:T(8,128)(2,1)S(1)} all-to-all(bf16[4,2336,128]{2,1,0:T(8,128)(2,1)S(1)} %get-tuple-element.30), channel_id=1, replica_groups={{0,16,32,48},{64,80,96,112},{1,17,33,49},{65,81,97,113},{2,18,34,50},{6..., dimensions={0} | all-to-all | bytes 4784128 | tf_op jit(solution)/shard_map/all_to_all | solution.py:561
  37.3 2.1 %collective-permute-start = (bf16[4,2336,128]{2,1,0:T(8,128)(2,1)S(1)}, bf16[4,2336,128]{2,1,0:T(8,128)(2,1)S(1)}, u32[]{:S(2)}, u32[]{:S(2)}) collective-permute-start(bf16[4,2336,128]{2,1,0:T(8,128)(2,1)S(1)} %all_to_all.20.a_ref), channel_id=1, source_target_pairs={{0,1},{1,0},{2,3},{3,2},{4,5},{5,4},{6,7},{7,6},{8,9},{9,8},{10,11... | collective-permute-start | bytes 7176200 | tf_op jit(solution)/shard_map/ppermute | solution.py:562
  39.3 4.2 %collective-permute-done.b_ref = bf16[4,2336,128]{2,1,0:T(8,128)(2,1)S(1)} collective-permute-done((bf16[4,2336,128]{2,1,0:T(8,128)(2,1)S(1)}, bf16[4,2336,128]{2,1,0:T(8,128)(2,1)S(1)}, u32[]{:S(2)}, u32[]{:S(2)}) %collective-permute-start) | collective-permute-done | bytes 2392096 | tf_op jit(solution)/shard_map/ppermute | solution.py:562
  43.5 0.0 copy-done.3
  43.6 2.2 %first.1 = bf16[256,256]{1,0:T(8,128)(2,1)S(1)} custom-call(bf16[4,256,256]{2,1,0:T(8,128)(2,1)S(1)} %bitcast.21, bf16[4,2336,128]{2,1,0:T(8,128)(2,1)S(1)} %all_to_all.20.a_ref, bf16[4,2336,128]{2,1,0:T(8,128)(2,1)S(1)} %collective-permute-done.b_ref), custom_call_target="tpu_custom_call" | custom-call | tf_op jit(solution)/shard_map/first/pallas_call | solution.py:282
  45.8 0.0 copy-start.2
  45.8 2.8 %collective-permute-start.1 = (bf16[256,256]{1,0:T(8,128)(2,1)S(1)}, bf16[256,256]{1,0:T(8,128)(2,1)S(1)}, u32[]{:S(2)}, u32[]{:S(2)}) collective-permute-start(bf16[256,256]{1,0:T(8,128)(2,1)S(1)} %first.1), channel_id=1, source_target_pairs={{0,64},{16,80},{32,96},{48,112},{64,0},{80,16},{96,32},{112,48},{1... | collective-permute-start | bytes 393224 | tf_op jit(solution)/shard_map/ppermute | solution.py:567
  48.6 1.3 %flip.1.flip_ref = bf16[4,2304,256]{2,1,0:T(8,128)(2,1)S(1)} custom-call(bf16[4,2336,128]{2,1,0:T(8,128)(2,1)S(1)} %all_to_all.20.a_ref, bf16[4,2336,128]{2,1,0:T(8,128)(2,1)S(1)} %collective-permute-done.b_ref), custom_call_target="tpu_custom_call" | custom-call | tf_op jit(solution)/shard_map/flip/pallas_call | solution.py:298
  49.9 2.2 %collective-permute-done.1.recv_ref = bf16[256,256]{1,0:T(8,128)(2,1)S(1)} collective-permute-done((bf16[256,256]{1,0:T(8,128)(2,1)S(1)}, bf16[256,256]{1,0:T(8,128)(2,1)S(1)}, u32[]{:S(2)}, u32[]{:S(2)}) %collective-permute-start.1) | collective-permute-done | bytes 131104 | tf_op jit(solution)/shard_map/ppermute | solution.py:567
  52.1 0.0 copy-done.2
  52.1 4.5 %middle.1 = (bf16[256,256]{1,0:T(8,128)(2,1)S(1)}, bf16[4,256,256]{2,1,0:T(8,128)(2,1)S(1)}, f32[4,256,256]{2,1,0:T(8,128)S(1)}, bf16[4,256,256]{2,1,0:T(8,128)(2,1)S(1)}) custom-call(bf16[4,256,256]{2,1,0:T(8,128)(2,1)S(1)} %bitcast.22, bf16[4,256,256]{2,1,0:T(8,128)(2,1)S(1)} %bitcast.19, bf16[256,256]{1,0:T(8,128)(2,1)S(1)} %collective-permute-done.1.recv_ref, ...), custom_call_target="tpu_custom_call" | custom-call | tf_op jit(solution)/shard_map/middle/pallas_call | solution.py:309
  56.6 2.8 %collective-permute-start.2 = (bf16[256,256]{1,0:T(8,128)(2,1)S(1)}, bf16[256,256]{1,0:T(8,128)(2,1)S(1)}, u32[]{:S(2)}, u32[]{:S(2)}) collective-permute-start(bf16[256,256]{1,0:T(8,128)(2,1)S(1)} %get-tuple-element.31), channel_id=1, source_target_pairs={{0,64},{16,80},{32,96},{48,112},{64,0},{80,16},{96,32},{112,48},{1... | collective-permute-start | bytes 393224 | tf_op jit(solution)/shard_map/ppermute | solution.py:569
  59.4 1.0 collective-permute-start.5
  60.4 1.2 collective-permute-start.4
  61.6 0.0 collective-permute-start.3
  61.6 0.4 collective-permute-done.2.recv_ref
  62.0 0.0 copy-start.6
  62.0 3.3 %last.1 = bf16[4,272,256]{2,1,0:T(8,128)(2,1)} custom-call(bf16[4,256,256]{2,1,0:T(8,128)(2,1)S(1)} %bitcast.20, bf16[256,256]{1,0:T(8,128)(2,1)S(1)} %collective-permute-done.2.recv_ref, bf16[4,256,256]{2,1,0:T(8,128)(2,1)S(1)} %get-tuple-element.32.xs_ref, f32[4,256,256]{2,1,0:T(8,128)S(1)} %get-tuple-element.33.conv_ref, ...), custom_call_target="tpu_custom_call" | custom-call | tf_op jit(solution)/shard_map/last/pallas_call | solution.py:331
  65.3 0.0 copy-start
  65.3 0.0 copy-start.1
  65.3 0.0 collective-permute-done.5.s3_ref
  65.3 0.5 collective-permute-done.4.s2_ref
  65.8 2.2 %collective-permute-done.3.s1_ref = bf16[256,256]{1,0:T(8,128)(2,1)S(1)} collective-permute-done((bf16[256,256]{1,0:T(8,128)(2,1)S(1)}, bf16[256,256]{1,0:T(8,128)(2,1)S(1)}, u32[]{:S(2)}, u32[]{:S(2)}) %collective-permute-start.3) | collective-permute-done | bytes 131104 | tf_op jit(solution)/shard_map/ppermute | solution.py:571
  68.0 0.0 copy-start.4
  68.0 0.7 copy-done.4
  68.6 3.7 %all-to-all-start.1 = ((bf16[4,272,256]{2,1,0:T(8,128)(2,1)}), bf16[4,272,256]{2,1,0:T(8,128)(2,1)S(1)}, u32[]{:S(2)}, u32[]{:S(2)}) async-start(bf16[4,272,256]{2,1,0:T(8,128)(2,1)} %last.1), calls=%async_computation.1 | async-start | bytes 1114112 | tf_op jit(solution)/shard_map/all_to_all | solution.py:579
  72.3 0.0 copy-start.5
  72.3 0.9 copy-done.5
  73.2 0.2 turn.1.flip_ref
  73.4 5.9 %all-to-all-done.1.r_ref = bf16[4,272,256]{2,1,0:T(8,128)(2,1)S(1)} async-done(((bf16[4,272,256]{2,1,0:T(8,128)(2,1)}), bf16[4,272,256]{2,1,0:T(8,128)(2,1)S(1)}, u32[]{:S(2)}, u32[]{:S(2)}) %all-to-all-start.1) | async-done | bytes 557088 | tf_op jit(solution)/shard_map/all_to_all | solution.py:579
  79.3 0.0 copy-done.6
  79.3 0.0 copy-done
  79.3 0.0 copy-done.1
  79.3 2.3 %give.1 = (bf16[1168,256]{1,0:T(8,128)(2,1)S(1)}, bf16[16,256]{1,0:T(8,128)(2,1)S(1)}, f32[4,512]{1,0:T(4,128)S(1)}, bf16[4,3,288,256]{3,2,1,0:T(8,128)(2,1)S(1)}, f32[256,256]{1,0:T(8,128)S(1)}) custom-call(bf16[4,272,256]{2,1,0:T(8,128)(2,1)S(1)} %all-to-all-done.1.r_ref, bf16[256,1024]{1,0:T(8,128)(2,1)S(1)} %turn.1.flip_ref, ...), custom_call_target="tpu_custom_call" | custom-call | tf_op jit(solution)/shard_map/give/pallas_call | solution.py:414
  81.6 3.8 %collective-permute-start.6 = (bf16[1168,256]{1,0:T(8,128)(2,1)S(1)}, bf16[1168,256]{1,0:T(8,128)(2,1)S(1)}, u32[]{:S(2)}, u32[]{:S(2)}) collective-permute-start(bf16[1168,256]{1,0:T(8,128)(2,1)S(1)} %get-tuple-element.46), channel_id=1, source_target_pairs={{0,1},{1,0},{2,3},{3,2},{4,5},{5,4},{6,7},{7,6},{8,9},{9,8},{10,11... | collective-permute-start | bytes 1794056 | tf_op jit(solution)/shard_map/ppermute | solution.py:583
  85.4 0.2 collective-permute-start.7
  85.7 0.8 keep.1.keep_ref
  86.5 3.0 %collective-permute-done.7 = f32[4,512]{1,0:T(4,128)S(1)} collective-permute-done((f32[4,512]{1,0:T(4,128)S(1)}, f32[4,512]{1,0:T(4,128)S(1)}, u32[]{:S(2)}, u32[]{:S(2)}) %collective-permute-start.7) | collective-permute-done | bytes 8224 | tf_op jit(solution)/shard_map/ppermute | solution.py:584
  89.4 0.0 collective-permute-done.6.got_ref
  89.5 1.0 pair.1
  90.5 4.2 %all-to-all-start.2 = ((bf16[8,176,256]{2,1,0:T(8,128)(2,1)}), bf16[8,176,256]{2,1,0:T(8,128)(2,1)S(1)}, u32[]{:S(2)}, u32[]{:S(2)}) async-start(bf16[8,176,256]{2,1,0:T(8,128)(2,1)} %pair.1), calls=%async_computation.2 | async-start | bytes 1441792 | tf_op jit(solution)/shard_map/all_to_all | solution.py:587
  94.7 0.3 collective-permute-start.8
  94.9 2.2 %collective-permute-done.8 = f32[4,512]{1,0:T(4,128)S(1)} collective-permute-done((f32[4,512]{1,0:T(4,128)S(1)}, f32[4,512]{1,0:T(4,128)S(1)}, u32[]{:S(2)}, u32[]{:S(2)}) %collective-permute-start.8) | collective-permute-done | bytes 8224 | tf_op jit(solution)/shard_map/ppermute | solution.py:588
  97.2 0.6 collective-permute-start.9
  97.8 3.4 %collective-permute-done.9 = f32[4,512]{1,0:T(4,128)S(1)} collective-permute-done((f32[4,512]{1,0:T(4,128)S(1)}, f32[4,512]{1,0:T(4,128)S(1)}, u32[]{:S(2)}, u32[]{:S(2)}) %collective-permute-start.9) | collective-permute-done | bytes 8224 | tf_op jit(solution)/shard_map/ppermute | solution.py:589
  101.2 0.6 add.11
  101.8 3.6 %all-to-all-done.2.shares_ref = bf16[8,176,256]{2,1,0:T(8,128)(2,1)S(1)} async-done(((bf16[8,176,256]{2,1,0:T(8,128)(2,1)}), bf16[8,176,256]{2,1,0:T(8,128)(2,1)S(1)}, u32[]{:S(2)}, u32[]{:S(2)}) %all-to-all-start.2) | async-done | bytes 720928 | tf_op jit(solution)/shard_map/all_to_all | solution.py:587
  105.4 0.1 share.1
  105.5 10.5 %all_to_all.21.value_ref = bf16[8,144,256]{2,1,0:T(8,128)(2,1)S(1)} all-to-all(bf16[8,144,256]{2,1,0:T(8,128)(2,1)S(1)} %share.1), channel_id=1, replica_groups={{0,2,4,6,8,10,12,14},{1,3,5,7,9,11,13,15},{16,18,20,22,24,26,28,30},{17..., dimensions={0} | all-to-all | bytes 1179648 | tf_op jit(solution)/shard_map/all_to_all | solution.py:591
  116.0 4.4 %collective-permute-start.10 = (bf16[8,144,256]{2,1,0:T(8,128)(2,1)S(1)}, bf16[8,144,256]{2,1,0:T(8,128)(2,1)S(1)}, u32[]{:S(2)}, u32[]{:S(2)}) collective-permute-start(bf16[8,144,256]{2,1,0:T(8,128)(2,1)S(1)} %all_to_all.21.value_ref), channel_id=1, source_target_pairs={{0,1},{1,0},{2,3},{3,2},{4,5},{5,4},{6,7},{7,6},{8,9},{9,8},{10,11... | collective-permute-start | bytes 1769480 | tf_op jit(solution)/shard_map/ppermute | solution.py:592
  120.3 1.1 affine.1
  121.4 1.1 own.1.refs_0_
  122.5 0.0 collective-permute-done.10.value_ref
  122.5 1.1 rest.1
  (3 shorter events, 0.0 us)
Async XLA Ops:
  3.1 40.5 %copy-start.3 = (bf16[4,16,16,256]{3,2,1,0:T(8,128)(2,1)S(1)}, bf16[4,16,16,256]{3,2,1,0:T(8,128)(2,1)}, u32[]{:S(2)}) copy-start(bf16[4,16,16,256]{3,2,1,0:T(8,128)(2,1)} %param.6) | copy-start | bytes 1572868
  37.3 6.3 %collective-permute-start = (bf16[4,2336,128]{2,1,0:T(8,128)(2,1)S(1)}, bf16[4,2336,128]{2,1,0:T(8,128)(2,1)S(1)}, u32[]{:S(2)}, u32[]{:S(2)}) collective-permute-start(bf16[4,2336,128]{2,1,0:T(8,128)(2,1)S(1)} %all_to_all.20.a_ref), channel_id=1, source_target_pairs={{0,1},{1,0},{2,3},{3,2},{4,5},{5,4},{6,7},{7,6},{8,9},{9,8},{10,11... | collective-permute-start | bytes 7176200 | tf_op jit(solution)/shard_map/ppermute | solution.py:562
  45.8 6.3 %copy-start.2 = (bf16[4,16,16,256]{3,2,1,0:T(8,128)(2,1)S(1)}, bf16[4,16,16,256]{3,2,1,0:T(8,128)(2,1)}, u32[]{:S(2)}) copy-start(bf16[4,16,16,256]{3,2,1,0:T(8,128)(2,1)} %param.11) | copy-start | bytes 1572868
  45.8 6.3 %collective-permute-start.1 = (bf16[256,256]{1,0:T(8,128)(2,1)S(1)}, bf16[256,256]{1,0:T(8,128)(2,1)S(1)}, u32[]{:S(2)}, u32[]{:S(2)}) collective-permute-start(bf16[256,256]{1,0:T(8,128)(2,1)S(1)} %first.1), channel_id=1, source_target_pairs={{0,64},{16,80},{32,96},{48,112},{64,0},{80,16},{96,32},{112,48},{1... | collective-permute-start | bytes 393224 | tf_op jit(solution)/shard_map/ppermute | solution.py:567
  56.6 5.4 %collective-permute-start.2 = (bf16[256,256]{1,0:T(8,128)(2,1)S(1)}, bf16[256,256]{1,0:T(8,128)(2,1)S(1)}, u32[]{:S(2)}, u32[]{:S(2)}) collective-permute-start(bf16[256,256]{1,0:T(8,128)(2,1)S(1)} %get-tuple-element.31), channel_id=1, source_target_pairs={{0,64},{16,80},{32,96},{48,112},{64,0},{80,16},{96,32},{112,48},{1... | collective-permute-start | bytes 393224 | tf_op jit(solution)/shard_map/ppermute | solution.py:569
  59.4 5.9 %collective-permute-start.5 = (bf16[256,256]{1,0:T(8,128)(2,1)S(1)}, bf16[256,256]{1,0:T(8,128)(2,1)S(1)}, u32[]{:S(2)}, u32[]{:S(2)}) collective-permute-start(bf16[256,256]{1,0:T(8,128)(2,1)S(1)} %get-tuple-element.56), channel_id=1, source_target_pairs={{0,48},{16,0},{32,16},{48,32},{64,112},{80,64},{96,80},{112,96},{1... | collective-permute-start | bytes 393224 | tf_op jit(solution)/shard_map/ppermute | solution.py:571
  60.4 5.4 %collective-permute-start.4 = (bf16[256,256]{1,0:T(8,128)(2,1)S(1)}, bf16[256,256]{1,0:T(8,128)(2,1)S(1)}, u32[]{:S(2)}, u32[]{:S(2)}) collective-permute-start(bf16[256,256]{1,0:T(8,128)(2,1)S(1)} %get-tuple-element.57), channel_id=1, source_target_pairs={{0,32},{16,48},{32,0},{48,16},{64,96},{80,112},{96,64},{112,80},{1... | collective-permute-start | bytes 393224 | tf_op jit(solution)/shard_map/ppermute | solution.py:571
  61.6 6.4 %collective-permute-start.3 = (bf16[256,256]{1,0:T(8,128)(2,1)S(1)}, bf16[256,256]{1,0:T(8,128)(2,1)S(1)}, u32[]{:S(2)}, u32[]{:S(2)}) collective-permute-start(bf16[256,256]{1,0:T(8,128)(2,1)S(1)} %get-tuple-element.58), channel_id=1, source_target_pairs={{0,16},{16,32},{32,48},{48,0},{64,80},{80,96},{96,112},{112,64},{1... | collective-permute-start | bytes 393224 | tf_op jit(solution)/shard_map/ppermute | solution.py:571
  62.0 17.3 %copy-start.6 = (f32[4,512]{1,0:T(4,128)S(1)}, f32[4,512]{1,0:T(4,128)}, u32[]{:S(2)}) copy-start(f32[4,512]{1,0:T(4,128)} %latent_ref.1) | copy-start | bytes 24580
  65.3 14.0 %copy-start = (bf16[1,3,3,256,256]{4,3,2,1,0:T(8,128)(2,1)S(1)}, bf16[1,3,3,256,256]{4,3,2,1,0:T(8,128)(2,1)}, u32[]{:S(2)}) copy-start(bf16[1,3,3,256,256]{4,3,2,1,0:T(8,128)(2,1)} %param.8) | copy-start | bytes 3538948
  65.3 14.0 %copy-start.1 = (f32[1,512,256]{2,1,0:T(8,128)S(1)}, f32[1,512,256]{2,1,0:T(8,128)}, u32[]{:S(2)}) copy-start(f32[1,512,256]{2,1,0:T(8,128)} %param.9) | copy-start | bytes 1572868
  68.0 0.7 copy-start.4
  68.6 10.6 %all-to-all-start.1 = ((bf16[4,272,256]{2,1,0:T(8,128)(2,1)}), bf16[4,272,256]{2,1,0:T(8,128)(2,1)S(1)}, u32[]{:S(2)}, u32[]{:S(2)}) async-start(bf16[4,272,256]{2,1,0:T(8,128)(2,1)} %last.1), calls=%async_computation.1 | async-start | bytes 1114112 | tf_op jit(solution)/shard_map/all_to_all | solution.py:579
  72.3 0.9 copy-start.5
  81.6 7.9 %collective-permute-start.6 = (bf16[1168,256]{1,0:T(8,128)(2,1)S(1)}, bf16[1168,256]{1,0:T(8,128)(2,1)S(1)}, u32[]{:S(2)}, u32[]{:S(2)}) collective-permute-start(bf16[1168,256]{1,0:T(8,128)(2,1)S(1)} %get-tuple-element.46), channel_id=1, source_target_pairs={{0,1},{1,0},{2,3},{3,2},{4,5},{5,4},{6,7},{7,6},{8,9},{9,8},{10,11... | collective-permute-start | bytes 1794056 | tf_op jit(solution)/shard_map/ppermute | solution.py:583
  85.4 4.0 %collective-permute-start.7 = (f32[4,512]{1,0:T(4,128)S(1)}, f32[4,512]{1,0:T(4,128)S(1)}, u32[]{:S(2)}, u32[]{:S(2)}) collective-permute-start(f32[4,512]{1,0:T(4,128)S(1)} %get-tuple-element.47), channel_id=1, source_target_pairs={{0,64},{16,80},{32,96},{48,112},{64,0},{80,16},{96,32},{112,48},{1... | collective-permute-start | bytes 24584 | tf_op jit(solution)/shard_map/ppermute | solution.py:584
  90.5 14.9 %all-to-all-start.2 = ((bf16[8,176,256]{2,1,0:T(8,128)(2,1)}), bf16[8,176,256]{2,1,0:T(8,128)(2,1)S(1)}, u32[]{:S(2)}, u32[]{:S(2)}) async-start(bf16[8,176,256]{2,1,0:T(8,128)(2,1)} %pair.1), calls=%async_computation.2 | async-start | bytes 1441792 | tf_op jit(solution)/shard_map/all_to_all | solution.py:587
  94.7 2.5 %collective-permute-start.8 = (f32[4,512]{1,0:T(4,128)S(1)}, f32[4,512]{1,0:T(4,128)S(1)}, u32[]{:S(2)}, u32[]{:S(2)}) collective-permute-start(f32[4,512]{1,0:T(4,128)S(1)} %add.9), channel_id=1, source_target_pairs={{0,16},{16,0},{32,48},{48,32},{64,80},{80,64},{96,112},{112,96},{1... | collective-permute-start | bytes 24584 | tf_op jit(solution)/shard_map/ppermute | solution.py:588
  97.2 4.0 %collective-permute-start.9 = (f32[4,512]{1,0:T(4,128)S(1)}, f32[4,512]{1,0:T(4,128)S(1)}, u32[]{:S(2)}, u32[]{:S(2)}) collective-permute-start(f32[4,512]{1,0:T(4,128)S(1)} %add.10), channel_id=1, source_target_pairs={{0,32},{16,48},{32,0},{48,16},{64,96},{80,112},{96,64},{112,80},{1... | collective-permute-start | bytes 24584 | tf_op jit(solution)/shard_map/ppermute | solution.py:589
  116.0 6.5 %collective-permute-start.10 = (bf16[8,144,256]{2,1,0:T(8,128)(2,1)S(1)}, bf16[8,144,256]{2,1,0:T(8,128)(2,1)S(1)}, u32[]{:S(2)}, u32[]{:S(2)}) collective-permute-start(bf16[8,144,256]{2,1,0:T(8,128)(2,1)S(1)} %all_to_all.21.value_ref), channel_id=1, source_target_pairs={{0,1},{1,0},{2,3},{3,2},{4,5},{5,4},{6,7},{7,6},{8,9},{9,8},{10,11... | collective-permute-start | bytes 1769480 | tf_op jit(solution)/shard_map/ppermute | solution.py:592

commit v7 on v6

--- a/solution.py
+++ b/solution.py
@@ -1,4 +1,3 @@
-import functools
 import math
 
 import jax
@@ -513,10 +512,7 @@
     )(shares)
 
 
-def widen_kernel(own, value_ref, *refs):
-    out_any, wide_ref, sem = refs[-3:]
-    _, _, core = place()
-    half = core if own else 1 - core
+def widen_half(half, value_ref, out_any, wide_ref, sem):
     value = value_ref[...].reshape(TAPS, BLOCK, C)
     rows = pl.ds(pl.multiple_of(half * BLOCK, BLOCK), BLOCK)
     copies = []
@@ -529,19 +525,47 @@
         copy.wait()
 
 
-def widen(value, target=None):
-    hbm = pl.BlockSpec(memory_space=pltpu.HBM)
-    args = (value,) if target is None else (value, target)
-    return pl.pallas_call(
-        functools.partial(widen_kernel, target is None),
-        out_shape=jax.ShapeDtypeStruct((TAPS, C, C), F32),
-        in_specs=[vmem_spec(), hbm][: len(args)],
-        out_specs=hbm,
-        input_output_aliases={1: 0} if len(args) == 2 else {},
-        scratch_shapes=[pltpu.VMEM((TAPS, BLOCK, C), F32), pltpu.SemaphoreType.DMA((3,))],
-        compiler_params=params(),
-        name="own" if target is None else "rest",
-    )(*args)
+def own_kernel(value_ref, out_any, wide_ref, sem):
+    _, _, core = place()
+    widen_half(core, value_ref, out_any, wide_ref, sem)
+
+
+def rest_kernel(value_ref, target_any, part_ref, moved_ref, out_any, sum_ref, wide_ref, sem):
+    _, _, core = place()
+    sum_ref[...] = part_ref[...] + moved_ref[...]
+    widen_half(1 - core, value_ref, out_any, wide_ref, sem)
+
+
+WIDE = jax.ShapeDtypeStruct((TAPS, C, C), F32)
+
+
+def wide_scratch():
+    return [pltpu.VMEM((TAPS, BLOCK, C), F32), pltpu.SemaphoreType.DMA((3,))]
+
+
+def own_half(value):
+    return pl.pallas_call(
+        own_kernel,
+        out_shape=WIDE,
+        in_specs=[vmem_spec()],
+        out_specs=pl.BlockSpec(memory_space=pltpu.HBM),
+        scratch_shapes=wide_scratch(),
+        compiler_params=params(),
+        name="own",
+    )(value)
+
+
+def rest_half(value, target, part, moved):
+    return pl.pallas_call(
+        rest_kernel,
+        out_shape=(WIDE, jax.ShapeDtypeStruct(part.shape, F32)),
+        in_specs=[vmem_spec(), pl.BlockSpec(memory_space=pltpu.HBM), vmem_spec(), vmem_spec()],
+        out_specs=(pl.BlockSpec(memory_space=pltpu.HBM), vmem_spec()),
+        input_output_aliases={1: 0},
+        scratch_shapes=wide_scratch(),
+        compiler_params=params(),
+        name="rest",
+    )(value, target, part, moved)
 
 
 def body(images, latent, weight, affine, biases, cotangent):
@@ -568,31 +592,34 @@
     dx, xs, conv, scaled = middle(images, cotangent, arrived, a, b, flipped)
     returned = near(lax.ppermute(dx, "segment", across))
     maps = [scaled[0]] + [
-        lax.ppermute(
-            scaled[k], "segment", [(i, i - i % DEPTH + (i + k) % DEPTH) for i in range(segments)]
+        near(
+            lax.ppermute(
+                scaled[k], "segment", [(i, i - i % DEPTH + (i + k) % DEPTH) for i in range(segments)]
+            )
         )
         for k in range(1, DEPTH)
     ]
-    sent, *maps = lax.optimization_barrier((last(cotangent, returned, xs, conv, flipped, a), *maps))
-    turned = turn(*[near(value) for value in maps])
+    turned = turn(*maps)
+    sent, turned = lax.optimization_barrier((last(cotangent, returned, xs, conv, flipped, a), turned))
 
     r = near(lax.all_to_all(sent, "segment", 0, 0, axis_index_groups=planes))
     give, extra, part, padded, grad_energy = give_half(
         r, turned, w, styles, demod, energy, affine[0], latent
     )
     got = near(lax.ppermute(give, "dp", sibling))
-    part = part + lax.ppermute(part, "segment", across)
     keep = keep_half(turned, padded, w, grad_energy)
     shared, part = lax.optimization_barrier((pair(keep, extra, got), part))
     shares = near(lax.all_to_all(near(shared), "dp", 0, 0, axis_index_groups=cores))
     part = part + lax.ppermute(part, "segment", [(i, i ^ 1) for i in range(segments)])
-    grad_latent = part + lax.ppermute(part, "segment", [(i, i ^ 2) for i in range(segments)])
-    spread_share, grad_latent = lax.optimization_barrier((share(shares), grad_latent))
+    part = part + lax.ppermute(part, "segment", [(i, i ^ 2) for i in range(segments)])
+    spread_share, part = lax.optimization_barrier((share(shares), part))
     mine = lax.all_to_all(near(spread_share), "dp", 0, 0, axis_index_groups=cores)
     other = near(lax.ppermute(mine, "dp", sibling))
-    mine, shares = lax.optimization_barrier((mine, shares))
+    mine, shares, part = lax.optimization_barrier((mine, shares, part))
+    moved = lax.ppermute(part, "segment", across)
     grad_affine, grad_bias = affine_gradient(shares, width)
-    grad_weight = widen(other, widen(near(mine))).reshape(weight.shape)
+    grad_weight, grad_latent = rest_half(other, own_half(near(mine)), part, moved)
+    grad_weight = grad_weight.reshape(weight.shape)
     return (grad_weight, grad_affine[None], grad_bias, grad_latent)
 
 

time: 124 us -> 124 us (level)
  blocking collectives: 44.6 us -> 58.8 us
  waiting for transfers between devices: 27.4 us -> 21.4 us
  starting transfers between devices: 27.1 us -> 21.9 us
  local copies, waits for them, and re-layouts: 1.62 us -> 0.06 us
    all_to_all x0 -> x1, blocking collectives: none -> 11.3 us  [body(): r = near(lax.all_to_all(sent, 'segment', 0, 0, axis_index_groups=planes))]
    all_to_all x1 -> x0, waiting for transfers between devices: 5.87 us -> none  [body(): r = near(lax.all_to_all(sent, 'segment', 0, 0, axis_index_groups=planes))]
    all_to_all x1 -> x0, starting transfers between devices: 3.65 us -> none  [body(): r = near(lax.all_to_all(sent, 'segment', 0, 0, axis_index_groups=planes))]
    all_to_all x1, blocking collectives: 10.5 us -> 13.3 us  [body(): lax.all_to_all(near(spread_share), 'dp', 0, 0, axis_index_groups=cores)]
    ppermute x1, waiting for transfers between devices: 2.96 us -> 0.14 us  [body(): moved = lax.ppermute(part, 'segment', across)]
    ppermute x1, starting transfers between devices: 4.37 us -> 2.1 us  [body(): other = near(lax.ppermute(mine, 'dp', sibling))]
    unnamed x14 -> x10, local copies, waits for them, and re-layouts: 1.58 us -> 0.03 us
    ppermute x1, starting transfers between devices: 0.24 us -> 1.72 us  [body(): moved = lax.ppermute(part, 'segment', across)]
  transfers between devices with their start and end apart: 13 -> 12, of which waited for: 10 -> 10; matrix products, arithmetic and copies ran while one was open for 1% -> 0% of each run, Pallas kernels for 6% -> 5%
where the time goes in v7:
time: 124 us
  blocking collectives  58.8 us (47%)
  starting transfers between devices  21.9 us (18%)
  waiting for transfers between devices  21.4 us (17%)
  Pallas kernels  21.1 us (17%)
    all_to_all x1, blocking collectives, body(): a = lax.all_to_all(send, 'segment', 0, 0, axis_index_groups=planes)  34.2 us
    all_to_all x1, blocking collectives, body(): lax.all_to_all(near(spread_share), 'dp', 0, 0, axis_index_groups=cores)  13.3 us
    all_to_all x1, blocking collectives, body(): r = near(lax.all_to_all(sent, 'segment', 0, 0, axis_index_groups=planes))  11.3 us
    all_to_all x1, waiting for transfers between devices, body(): lax.all_to_all(near(shared), 'dp', 0, 0, axis_index_groups=cores)  4.8 us
    pallas_call x1, Pallas kernels, middle(): pl.pallas_call(middle_kernel, out_shape=(MAP, jax.ShapeDtypeStruct((DEPTH...  4.46 us
    ppermute x1, waiting for transfers between devices, body(): b = near(lax.ppermute(a, 'dp', sibling))  4.21 us
    all_to_all x1, starting transfers between devices, body(): lax.all_to_all(near(shared), 'dp', 0, 0, axis_index_groups=cores)  4.17 us
    ppermute x3, waiting for transfers between devices, body(): lax.ppermute(scaled[k], 'segment', [(i, i - i % DEPTH + (i + k) % DEPTH)...  3.44 us
  transfers between devices with their start and end apart: 12, of which 10 were waited for; matrix products, arithmetic and copies ran while one was open for 0% of the time, Pallas kernels for 5%

profile of v7, /device:TPU:1, one launch (start us, length us, event | category | flops | bytes accessed | tf_op | source)
XLA Modules:
  0.0 124.1 jit_solution(1679155687298876186)
XLA Ops:
  0.6 2.5 %prepare.1 = (bf16[4,2336,128]{2,1,0:T(8,128)(2,1)S(1)}, f32[8,256]{1,0:T(8,128)S(1)}, f32[8,256]{1,0:T(8,128)S(1)}, f32[256,256]{1,0:T(8,128)S(1)}) custom-call(f32[4,512]{1,0:T(4,128)} %latent_ref.1, f32[512,256]{1,0:T(8,128)} %bitcast.17, bf16[2304,256]{1,0:T(8,128)(2,1)} %bitcast.14, f32[1,256]{1,0:T(1,128)} %bias_hbm.1), custom_call_target="tpu_custom_call" | custom-call | tf_op jit(solution)/shard_map/prepare/pallas_call | solution.py:126
  3.1 0.0 copy-start.3
  3.1 34.2 %all_to_all.20.a_ref = bf16[4,2336,128]{2,1,0:T(8,128)(2,1)S(1)} all-to-all(bf16[4,2336,128]{2,1,0:T(8,128)(2,1)S(1)} %get-tuple-element.30), channel_id=1, replica_groups={{0,16,32,48},{64,80,96,112},{1,17,33,49},{65,81,97,113},{2,18,34,50},{6..., dimensions={0} | all-to-all | bytes 4784128 | tf_op jit(solution)/shard_map/all_to_all | solution.py:585
  37.3 2.1 %collective-permute-start = (bf16[4,2336,128]{2,1,0:T(8,128)(2,1)S(1)}, bf16[4,2336,128]{2,1,0:T(8,128)(2,1)S(1)}, u32[]{:S(2)}, u32[]{:S(2)}) collective-permute-start(bf16[4,2336,128]{2,1,0:T(8,128)(2,1)S(1)} %all_to_all.20.a_ref), channel_id=1, source_target_pairs={{0,1},{1,0},{2,3},{3,2},{4,5},{5,4},{6,7},{7,6},{8,9},{9,8},{10,11... | collective-permute-start | bytes 7176200 | tf_op jit(solution)/shard_map/ppermute | solution.py:586
  39.3 4.2 %collective-permute-done.b_ref = bf16[4,2336,128]{2,1,0:T(8,128)(2,1)S(1)} collective-permute-done((bf16[4,2336,128]{2,1,0:T(8,128)(2,1)S(1)}, bf16[4,2336,128]{2,1,0:T(8,128)(2,1)S(1)}, u32[]{:S(2)}, u32[]{:S(2)}) %collective-permute-start) | collective-permute-done | bytes 2392096 | tf_op jit(solution)/shard_map/ppermute | solution.py:586
  43.5 0.0 copy-done.3
  43.6 2.2 %first.1 = bf16[256,256]{1,0:T(8,128)(2,1)S(1)} custom-call(bf16[4,256,256]{2,1,0:T(8,128)(2,1)S(1)} %bitcast.21, bf16[4,2336,128]{2,1,0:T(8,128)(2,1)S(1)} %all_to_all.20.a_ref, bf16[4,2336,128]{2,1,0:T(8,128)(2,1)S(1)} %collective-permute-done.b_ref), custom_call_target="tpu_custom_call" | custom-call | tf_op jit(solution)/shard_map/first/pallas_call | solution.py:281
  45.8 0.0 copy-start.2
  45.8 2.8 %collective-permute-start.1 = (bf16[256,256]{1,0:T(8,128)(2,1)S(1)}, bf16[256,256]{1,0:T(8,128)(2,1)S(1)}, u32[]{:S(2)}, u32[]{:S(2)}) collective-permute-start(bf16[256,256]{1,0:T(8,128)(2,1)S(1)} %first.1), channel_id=1, source_target_pairs={{0,64},{16,80},{32,96},{48,112},{64,0},{80,16},{96,32},{112,48},{1... | collective-permute-start | bytes 393224 | tf_op jit(solution)/shard_map/ppermute | solution.py:591
  48.6 1.3 %flip.1.flip_ref = bf16[4,2304,256]{2,1,0:T(8,128)(2,1)S(1)} custom-call(bf16[4,2336,128]{2,1,0:T(8,128)(2,1)S(1)} %all_to_all.20.a_ref, bf16[4,2336,128]{2,1,0:T(8,128)(2,1)S(1)} %collective-permute-done.b_ref), custom_call_target="tpu_custom_call" | custom-call | tf_op jit(solution)/shard_map/flip/pallas_call | solution.py:297
  49.9 2.2 %collective-permute-done.1.recv_ref = bf16[256,256]{1,0:T(8,128)(2,1)S(1)} collective-permute-done((bf16[256,256]{1,0:T(8,128)(2,1)S(1)}, bf16[256,256]{1,0:T(8,128)(2,1)S(1)}, u32[]{:S(2)}, u32[]{:S(2)}) %collective-permute-start.1) | collective-permute-done | bytes 131104 | tf_op jit(solution)/shard_map/ppermute | solution.py:591
  52.1 0.0 copy-done.2
  52.1 4.5 %middle.1 = (bf16[256,256]{1,0:T(8,128)(2,1)S(1)}, bf16[4,256,256]{2,1,0:T(8,128)(2,1)S(1)}, f32[4,256,256]{2,1,0:T(8,128)S(1)}, bf16[4,256,256]{2,1,0:T(8,128)(2,1)S(1)}) custom-call(bf16[4,256,256]{2,1,0:T(8,128)(2,1)S(1)} %bitcast.22, bf16[4,256,256]{2,1,0:T(8,128)(2,1)S(1)} %bitcast.19, bf16[256,256]{1,0:T(8,128)(2,1)S(1)} %collective-permute-done.1.recv_ref, ...), custom_call_target="tpu_custom_call" | custom-call | tf_op jit(solution)/shard_map/middle/pallas_call | solution.py:308
  56.6 2.8 %collective-permute-start.2 = (bf16[256,256]{1,0:T(8,128)(2,1)S(1)}, bf16[256,256]{1,0:T(8,128)(2,1)S(1)}, u32[]{:S(2)}, u32[]{:S(2)}) collective-permute-start(bf16[256,256]{1,0:T(8,128)(2,1)S(1)} %get-tuple-element.31), channel_id=1, source_target_pairs={{0,64},{16,80},{32,96},{48,112},{64,0},{80,16},{96,32},{112,48},{1... | collective-permute-start | bytes 393224 | tf_op jit(solution)/shard_map/ppermute | solution.py:593
  59.4 1.0 collective-permute-start.5
  60.4 1.2 collective-permute-start.4
  61.6 0.0 collective-permute-start.3
  61.6 0.4 collective-permute-done.2.recv_ref
  62.0 0.0 copy-start.4
  62.0 2.5 %last.1 = bf16[4,272,256]{2,1,0:T(8,128)(2,1)S(1)} custom-call(bf16[4,256,256]{2,1,0:T(8,128)(2,1)S(1)} %bitcast.20, bf16[256,256]{1,0:T(8,128)(2,1)S(1)} %collective-permute-done.2.recv_ref, bf16[4,256,256]{2,1,0:T(8,128)(2,1)S(1)} %get-tuple-element.32.xs_ref, f32[4,256,256]{2,1,0:T(8,128)S(1)} %get-tuple-element.33.conv_ref, ...), custom_call_target="tpu_custom_call" | custom-call | tf_op jit(solution)/shard_map/last/pallas_call | solution.py:330
  64.5 0.0 copy-start
  64.5 0.0 copy-start.1
  64.5 0.0 collective-permute-done.5.s3_ref
  64.5 1.3 %collective-permute-done.4.s2_ref = bf16[256,256]{1,0:T(8,128)(2,1)S(1)} collective-permute-done((bf16[256,256]{1,0:T(8,128)(2,1)S(1)}, bf16[256,256]{1,0:T(8,128)(2,1)S(1)}, u32[]{:S(2)}, u32[]{:S(2)}) %collective-permute-start.4) | collective-permute-done | bytes 131104 | tf_op jit(solution)/shard_map/ppermute | solution.py:596
  65.8 2.2 %collective-permute-done.3.s1_ref = bf16[256,256]{1,0:T(8,128)(2,1)S(1)} collective-permute-done((bf16[256,256]{1,0:T(8,128)(2,1)S(1)}, bf16[256,256]{1,0:T(8,128)(2,1)S(1)}, u32[]{:S(2)}, u32[]{:S(2)}) %collective-permute-start.3) | collective-permute-done | bytes 131104 | tf_op jit(solution)/shard_map/ppermute | solution.py:596
  68.0 0.2 turn.1.flip_ref
  68.2 11.3 %all_to_all.21.r_ref = bf16[4,272,256]{2,1,0:T(8,128)(2,1)S(1)} all-to-all(bf16[4,272,256]{2,1,0:T(8,128)(2,1)S(1)} %last.1), channel_id=1, replica_groups={{0,16,32,48},{64,80,96,112},{1,17,33,49},{65,81,97,113},{2,18,34,50},{6..., dimensions={0} | all-to-all | bytes 1114112 | tf_op jit(solution)/shard_map/all_to_all | solution.py:605
  79.5 0.0 copy-done.4
  79.5 0.0 copy-done
  79.5 0.0 copy-done.1
  79.5 2.3 %give.1 = (bf16[1168,256]{1,0:T(8,128)(2,1)S(1)}, bf16[16,256]{1,0:T(8,128)(2,1)S(1)}, f32[4,512]{1,0:T(4,128)S(1)}, bf16[4,3,288,256]{3,2,1,0:T(8,128)(2,1)S(1)}, f32[256,256]{1,0:T(8,128)S(1)}) custom-call(bf16[4,272,256]{2,1,0:T(8,128)(2,1)S(1)} %all_to_all.21.r_ref, bf16[256,1024]{1,0:T(8,128)(2,1)S(1)} %turn.1.flip_ref, bf16[2304,256]{1,0:T(8,128)(2,1)S(1)} %bitcast.15, ...), custom_call_target="tpu_custom_call" | custom-call | tf_op jit(solution)/shard_map/give/pallas_call | solution.py:413
  81.8 2.9 %collective-permute-start.6 = (bf16[1168,256]{1,0:T(8,128)(2,1)S(1)}, bf16[1168,256]{1,0:T(8,128)(2,1)S(1)}, u32[]{:S(2)}, u32[]{:S(2)}) collective-permute-start(bf16[1168,256]{1,0:T(8,128)(2,1)S(1)} %get-tuple-element.43), channel_id=1, source_target_pairs={{0,1},{1,0},{2,3},{3,2},{4,5},{5,4},{6,7},{7,6},{8,9},{9,8},{10,11... | collective-permute-start | bytes 1794056 | tf_op jit(solution)/shard_map/ppermute | solution.py:609
  84.7 0.8 keep.1.keep_ref
  85.5 0.8 collective-permute-done.6.got_ref
  86.3 1.0 pair.1
  87.3 4.2 %all-to-all-start.2 = ((bf16[8,176,256]{2,1,0:T(8,128)(2,1)}), bf16[8,176,256]{2,1,0:T(8,128)(2,1)S(1)}, u32[]{:S(2)}, u32[]{:S(2)}) async-start(bf16[8,176,256]{2,1,0:T(8,128)(2,1)} %pair.1), calls=%async_computation.2 | async-start | bytes 1441792 | tf_op jit(solution)/shard_map/all_to_all | solution.py:612
  91.5 0.3 collective-permute-start.7
  91.8 2.2 %collective-permute-done.7 = f32[4,512]{1,0:T(4,128)S(1)} collective-permute-done((f32[4,512]{1,0:T(4,128)S(1)}, f32[4,512]{1,0:T(4,128)S(1)}, u32[]{:S(2)}, u32[]{:S(2)}) %collective-permute-start.7) | collective-permute-done | bytes 8224 | tf_op jit(solution)/shard_map/ppermute | solution.py:613
  94.0 0.8 collective-permute-start.8
  94.8 3.2 %collective-permute-done.8 = f32[4,512]{1,0:T(4,128)S(1)} collective-permute-done((f32[4,512]{1,0:T(4,128)S(1)}, f32[4,512]{1,0:T(4,128)S(1)}, u32[]{:S(2)}, u32[]{:S(2)}) %collective-permute-start.8) | collective-permute-done | bytes 8224 | tf_op jit(solution)/shard_map/ppermute | solution.py:614
  98.0 4.8 %all-to-all-done.2.shares_ref = bf16[8,176,256]{2,1,0:T(8,128)(2,1)S(1)} async-done(((bf16[8,176,256]{2,1,0:T(8,128)(2,1)}), bf16[8,176,256]{2,1,0:T(8,128)(2,1)S(1)}, u32[]{:S(2)}, u32[]{:S(2)}) %all-to-all-start.2) | async-done | bytes 720928 | tf_op jit(solution)/shard_map/all_to_all | solution.py:612
  102.8 0.1 share.1
  102.9 13.3 %all_to_all.22.value_ref = bf16[8,144,256]{2,1,0:T(8,128)(2,1)S(1)} all-to-all(bf16[8,144,256]{2,1,0:T(8,128)(2,1)S(1)} %share.1), channel_id=1, replica_groups={{0,2,4,6,8,10,12,14},{1,3,5,7,9,11,13,15},{16,18,20,22,24,26,28,30},{17..., dimensions={0} | all-to-all | bytes 1179648 | tf_op jit(solution)/shard_map/all_to_all | solution.py:616
  116.2 2.1 %collective-permute-start.9 = (bf16[8,144,256]{2,1,0:T(8,128)(2,1)S(1)}, bf16[8,144,256]{2,1,0:T(8,128)(2,1)S(1)}, u32[]{:S(2)}, u32[]{:S(2)}) collective-permute-start(bf16[8,144,256]{2,1,0:T(8,128)(2,1)S(1)} %all_to_all.22.value_ref), channel_id=1, source_target_pairs={{0,1},{1,0},{2,3},{3,2},{4,5},{5,4},{6,7},{7,6},{8,9},{9,8},{10,11... | collective-permute-start | bytes 1769480 | tf_op jit(solution)/shard_map/ppermute | solution.py:617
  118.3 1.7 %collective-permute-start.10 = (f32[4,512]{1,0:T(4,128)S(1)}, f32[4,512]{1,0:T(4,128)S(1)}, u32[]{:S(2)}, u32[]{:S(2)}) collective-permute-start(f32[4,512]{1,0:T(4,128)S(1)} %add.7.part_ref), channel_id=1, source_target_pairs={{0,64},{16,80},{32,96},{48,112},{64,0},{80,16},{96,32},{112,48},{1... | collective-permute-start | bytes 24584 | tf_op jit(solution)/shard_map/ppermute | solution.py:619
  120.0 1.1 affine.1
  121.1 1.1 own.1.target_any
  122.2 0.1 collective-permute-done.10.moved_ref
  122.3 0.0 collective-permute-done.9.value_ref
  122.3 1.7 %rest.1 = (f32[9,256,256]{2,1,0:T(8,128)}, f32[4,512]{1,0:T(4,128)}) custom-call(bf16[8,144,256]{2,1,0:T(8,128)(2,1)S(1)} %collective-permute-done.9.value_ref, f32[9,256,256]{2,1,0:T(8,128)} %own.1.target_any, f32[4,512]{1,0:T(4,128)S(1)} %add.7.part_ref, f32[4,512]{1,0:T(4,128)S(1)} %collective-permute-done.10.moved_ref), custom_call_target="tpu_custom_call", output_to_operand_aliasing={{0}: (1, {})} | custom-call | tf_op jit(solution)/shard_map/rest/pallas_call | solution.py:559
  (3 shorter events, 0.0 us)
Async XLA Ops:
  3.1 40.5 %copy-start.3 = (bf16[4,16,16,256]{3,2,1,0:T(8,128)(2,1)S(1)}, bf16[4,16,16,256]{3,2,1,0:T(8,128)(2,1)}, u32[]{:S(2)}) copy-start(bf16[4,16,16,256]{3,2,1,0:T(8,128)(2,1)} %param.6) | copy-start | bytes 1572868
  37.3 6.3 %collective-permute-start = (bf16[4,2336,128]{2,1,0:T(8,128)(2,1)S(1)}, bf16[4,2336,128]{2,1,0:T(8,128)(2,1)S(1)}, u32[]{:S(2)}, u32[]{:S(2)}) collective-permute-start(bf16[4,2336,128]{2,1,0:T(8,128)(2,1)S(1)} %all_to_all.20.a_ref), channel_id=1, source_target_pairs={{0,1},{1,0},{2,3},{3,2},{4,5},{5,4},{6,7},{7,6},{8,9},{9,8},{10,11... | collective-permute-start | bytes 7176200 | tf_op jit(solution)/shard_map/ppermute | solution.py:586
  45.8 6.3 %copy-start.2 = (bf16[4,16,16,256]{3,2,1,0:T(8,128)(2,1)S(1)}, bf16[4,16,16,256]{3,2,1,0:T(8,128)(2,1)}, u32[]{:S(2)}) copy-start(bf16[4,16,16,256]{3,2,1,0:T(8,128)(2,1)} %param.11) | copy-start | bytes 1572868
  45.8 6.3 %collective-permute-start.1 = (bf16[256,256]{1,0:T(8,128)(2,1)S(1)}, bf16[256,256]{1,0:T(8,128)(2,1)S(1)}, u32[]{:S(2)}, u32[]{:S(2)}) collective-permute-start(bf16[256,256]{1,0:T(8,128)(2,1)S(1)} %first.1), channel_id=1, source_target_pairs={{0,64},{16,80},{32,96},{48,112},{64,0},{80,16},{96,32},{112,48},{1... | collective-permute-start | bytes 393224 | tf_op jit(solution)/shard_map/ppermute | solution.py:591
  56.6 5.4 %collective-permute-start.2 = (bf16[256,256]{1,0:T(8,128)(2,1)S(1)}, bf16[256,256]{1,0:T(8,128)(2,1)S(1)}, u32[]{:S(2)}, u32[]{:S(2)}) collective-permute-start(bf16[256,256]{1,0:T(8,128)(2,1)S(1)} %get-tuple-element.31), channel_id=1, source_target_pairs={{0,64},{16,80},{32,96},{48,112},{64,0},{80,16},{96,32},{112,48},{1... | collective-permute-start | bytes 393224 | tf_op jit(solution)/shard_map/ppermute | solution.py:593
  59.4 5.1 %collective-permute-start.5 = (bf16[256,256]{1,0:T(8,128)(2,1)S(1)}, bf16[256,256]{1,0:T(8,128)(2,1)S(1)}, u32[]{:S(2)}, u32[]{:S(2)}) collective-permute-start(bf16[256,256]{1,0:T(8,128)(2,1)S(1)} %get-tuple-element.56), channel_id=1, source_target_pairs={{0,48},{16,0},{32,16},{48,32},{64,112},{80,64},{96,80},{112,96},{1... | collective-permute-start | bytes 393224 | tf_op jit(solution)/shard_map/ppermute | solution.py:596
  60.4 5.4 %collective-permute-start.4 = (bf16[256,256]{1,0:T(8,128)(2,1)S(1)}, bf16[256,256]{1,0:T(8,128)(2,1)S(1)}, u32[]{:S(2)}, u32[]{:S(2)}) collective-permute-start(bf16[256,256]{1,0:T(8,128)(2,1)S(1)} %get-tuple-element.57), channel_id=1, source_target_pairs={{0,32},{16,48},{32,0},{48,16},{64,96},{80,112},{96,64},{112,80},{1... | collective-permute-start | bytes 393224 | tf_op jit(solution)/shard_map/ppermute | solution.py:596
  61.6 6.4 %collective-permute-start.3 = (bf16[256,256]{1,0:T(8,128)(2,1)S(1)}, bf16[256,256]{1,0:T(8,128)(2,1)S(1)}, u32[]{:S(2)}, u32[]{:S(2)}) collective-permute-start(bf16[256,256]{1,0:T(8,128)(2,1)S(1)} %get-tuple-element.58), channel_id=1, source_target_pairs={{0,16},{16,32},{32,48},{48,0},{64,80},{80,96},{96,112},{112,64},{1... | collective-permute-start | bytes 393224 | tf_op jit(solution)/shard_map/ppermute | solution.py:596
  62.0 17.5 %copy-start.4 = (f32[4,512]{1,0:T(4,128)S(1)}, f32[4,512]{1,0:T(4,128)}, u32[]{:S(2)}) copy-start(f32[4,512]{1,0:T(4,128)} %latent_ref.1) | copy-start | bytes 24580
  64.5 15.0 %copy-start = (bf16[1,3,3,256,256]{4,3,2,1,0:T(8,128)(2,1)S(1)}, bf16[1,3,3,256,256]{4,3,2,1,0:T(8,128)(2,1)}, u32[]{:S(2)}) copy-start(bf16[1,3,3,256,256]{4,3,2,1,0:T(8,128)(2,1)} %param.8) | copy-start | bytes 3538948
  64.5 15.0 %copy-start.1 = (f32[1,512,256]{2,1,0:T(8,128)S(1)}, f32[1,512,256]{2,1,0:T(8,128)}, u32[]{:S(2)}) copy-start(f32[1,512,256]{2,1,0:T(8,128)} %param.9) | copy-start | bytes 1572868
  81.8 4.5 %collective-permute-start.6 = (bf16[1168,256]{1,0:T(8,128)(2,1)S(1)}, bf16[1168,256]{1,0:T(8,128)(2,1)S(1)}, u32[]{:S(2)}, u32[]{:S(2)}) collective-permute-start(bf16[1168,256]{1,0:T(8,128)(2,1)S(1)} %get-tuple-element.43), channel_id=1, source_target_pairs={{0,1},{1,0},{2,3},{3,2},{4,5},{5,4},{6,7},{7,6},{8,9},{9,8},{10,11... | collective-permute-start | bytes 1794056 | tf_op jit(solution)/shard_map/ppermute | solution.py:609
  87.3 15.5 %all-to-all-start.2 = ((bf16[8,176,256]{2,1,0:T(8,128)(2,1)}), bf16[8,176,256]{2,1,0:T(8,128)(2,1)S(1)}, u32[]{:S(2)}, u32[]{:S(2)}) async-start(bf16[8,176,256]{2,1,0:T(8,128)(2,1)} %pair.1), calls=%async_computation.2 | async-start | bytes 1441792 | tf_op jit(solution)/shard_map/all_to_all | solution.py:612
  91.5 2.5 %collective-permute-start.7 = (f32[4,512]{1,0:T(4,128)S(1)}, f32[4,512]{1,0:T(4,128)S(1)}, u32[]{:S(2)}, u32[]{:S(2)}) collective-permute-start(f32[4,512]{1,0:T(4,128)S(1)} %get-tuple-element.46), channel_id=1, source_target_pairs={{0,16},{16,0},{32,48},{48,32},{64,80},{80,64},{96,112},{112,96},{1... | collective-permute-start | bytes 24584 | tf_op jit(solution)/shard_map/ppermute | solution.py:613
  94.0 4.0 %collective-permute-start.8 = (f32[4,512]{1,0:T(4,128)S(1)}, f32[4,512]{1,0:T(4,128)S(1)}, u32[]{:S(2)}, u32[]{:S(2)}) collective-permute-start(f32[4,512]{1,0:T(4,128)S(1)} %add.6), channel_id=1, source_target_pairs={{0,32},{16,48},{32,0},{48,16},{64,96},{80,112},{96,64},{112,80},{1... | collective-permute-start | bytes 24584 | tf_op jit(solution)/shard_map/ppermute | solution.py:614
  116.2 6.1 %collective-permute-start.9 = (bf16[8,144,256]{2,1,0:T(8,128)(2,1)S(1)}, bf16[8,144,256]{2,1,0:T(8,128)(2,1)S(1)}, u32[]{:S(2)}, u32[]{:S(2)}) collective-permute-start(bf16[8,144,256]{2,1,0:T(8,128)(2,1)S(1)} %all_to_all.22.value_ref), channel_id=1, source_target_pairs={{0,1},{1,0},{2,3},{3,2},{4,5},{5,4},{6,7},{7,6},{8,9},{9,8},{10,11... | collective-permute-start | bytes 1769480 | tf_op jit(solution)/shard_map/ppermute | solution.py:617
  118.3 4.0 %collective-permute-start.10 = (f32[4,512]{1,0:T(4,128)S(1)}, f32[4,512]{1,0:T(4,128)S(1)}, u32[]{:S(2)}, u32[]{:S(2)}) collective-permute-start(f32[4,512]{1,0:T(4,128)S(1)} %add.7.part_ref), channel_id=1, source_target_pairs={{0,64},{16,80},{32,96},{48,112},{64,0},{80,16},{96,32},{112,48},{1... | collective-permute-start | bytes 24584 | tf_op jit(solution)/shard_map/ppermute | solution.py:619

commit v8 on v7

--- a/solution.py
+++ b/solution.py
@@ -20,9 +20,9 @@
 DEPTH = 4
 PEERS = 8
 SHARE = HALF // PEERS
+PART = HALF // 2
 ROW = 16
 BLOCK = 128
-LANES = 128
 PAD = PX + 2 * ROW
 HI = lax.Precision.HIGHEST
 
@@ -46,6 +46,10 @@
 def place():
     seg = lax.axis_index("segment")
     return seg // DEPTH, seg % DEPTH, lax.axis_index("dp") % 2
+
+
+def part_start(core, side):
+    return pl.multiple_of(core * HALF + side * PART, PART)
 
 
 def split3(value):
@@ -80,11 +84,12 @@
 
 
 def prepare_kernel(
-    latent_hbm, affine_hbm, w_hbm, bias_hbm, send_ref, styles_ref, demod_ref, energy_ref,
-    rows_ref, affine_ref, w_ref, bias_ref, sem,
+    latent_hbm, affine_hbm, w_hbm, bias_hbm, down_ref, up_ref, far_ref, tile_ref, styles_ref, demod_ref, energy_ref,
+    rows_ref, affine_ref, w_ref, bias_ref, tiles_ref, sem,
 ):
-    _, _, core = place()
-    mine = pl.ds(pl.multiple_of(core * LANES, LANES), LANES)
+    _, z, core = place()
+    side = (lax.axis_index("dp") // 2) % 2
+    mine = pl.ds(pl.multiple_of(core * HALF, HALF), HALF)
     rows_ref[...] = jnp.zeros_like(rows_ref)
     third = ROWS // 3
     loads = [
@@ -96,7 +101,9 @@
         for k in range(3)
     ]
     sends = [
-        pltpu.make_async_copy(w_hbm.at[:, mine], send_ref.at[k, pl.ds(0, ROWS)], sem.at[6 + k]) for k in range(DEPTH)
+        pltpu.make_async_copy(w_hbm.at[pl.ds(part_start(core, side), PART)], far_ref.at[pl.ds(0, PART)], sem.at[6]),
+        pltpu.make_async_copy(w_hbm.at[mine], down_ref.at[pl.ds(0, HALF)], sem.at[7]),
+        pltpu.make_async_copy(w_hbm.at[mine], up_ref.at[pl.ds(0, HALF)], sem.at[8]),
     ]
     for copy in loads + sends:
         copy.start()
@@ -114,9 +121,11 @@
     styles_ref[...] = styles
     demod_ref[...] = demod
     for k in range(DEPTH):
-        tile = pack_rows([styles[k : k + 1], demod[k : k + 1], bias_ref[...]])
-        send_ref[k, ROWS : ROWS + STAT, :] = tile[:, :LANES]
-        send_ref[k, ROWS + STAT : ROWS + 2 * STAT, :] = tile[:, LANES:]
+        tiles_ref[k] = pack_rows([styles[k : k + 1], demod[k : k + 1], bias_ref[...]])
+    tile_ref[...] = tiles_ref[z]
+    down_ref[HALF : HALF + STAT, :] = tiles_ref[lax.rem(z + DEPTH - 1, DEPTH)]
+    up_ref[HALF : HALF + STAT, :] = tiles_ref[lax.rem(z + 1, DEPTH)]
+    far_ref[PART : PART + STAT, :] = tiles_ref[lax.rem(z + 2, DEPTH)]
     for copy in sends:
         copy.wait()
 
@@ -126,31 +135,27 @@
     return pl.pallas_call(
         prepare_kernel,
         out_shape=(
-            jax.ShapeDtypeStruct((DEPTH, ROWS + 2 * STAT, LANES), BF),
+            jax.ShapeDtypeStruct((HALF + STAT, C), BF),
+            jax.ShapeDtypeStruct((HALF + STAT, C), BF),
+            jax.ShapeDtypeStruct((PART + STAT, C), BF),
+            jax.ShapeDtypeStruct((STAT, C), BF),
             jax.ShapeDtypeStruct((8, C), F32),
             jax.ShapeDtypeStruct((8, C), F32),
             jax.ShapeDtypeStruct((C, C), F32),
         ),
         in_specs=[pl.BlockSpec(memory_space=pltpu.HBM)] * 4,
-        out_specs=(vmem_spec(),) * 4,
+        out_specs=(vmem_spec(),) * 7,
         scratch_shapes=[
             pltpu.VMEM((8, latent.shape[1]), F32),
             pltpu.VMEM(affine.shape, F32),
             pltpu.VMEM((ROWS, C), BF),
             pltpu.VMEM((1, C), F32),
-            pltpu.SemaphoreType.DMA((6 + DEPTH,)),
+            pltpu.VMEM((DEPTH, STAT, C), BF),
+            pltpu.SemaphoreType.DMA((9,)),
         ],
         compiler_params=params(),
         name="prepare",
     )(*far)
-
-
-def read_stats(a_ref, l):
-    return unpack_rows(
-        jnp.concatenate(
-            [a_ref[l, ROWS : ROWS + STAT, :], a_ref[l, ROWS + STAT : ROWS + 2 * STAT, :]], axis=1
-        )
-    )
 
 
 def clear_pads(pad_ref):
@@ -179,13 +184,10 @@
     return jnp.concatenate(out, axis=0)
 
 
-def forward_layer(x, l, a_ref, b_ref, stat, pad_ref):
+def forward_layer(x, l, w_ref, stat, pad_ref):
     styles, demod, bias = stat
     spread(pad_ref, (x.astype(F32) * styles).astype(BF).astype(F32))
-    _, _, core = place()
-    w = jnp.concatenate([a_ref[l, 0:ROWS, :], b_ref[l, 0:ROWS, :]], axis=1)
-    conv = taps_matmul(pad_ref, w, False)
-    return jnp.where(core == 0, conv, jnp.concatenate([conv[:, LANES:], conv[:, :LANES]], axis=1))
+    return taps_matmul(pad_ref, w_ref[l], False)
 
 
 def activate(conv, stat):
@@ -210,30 +212,63 @@
     return (grad_scaled * styles).astype(BF)
 
 
-def first_kernel(images_any, a_ref, b_ref, out_ref, x_buf, pad_ref, x_sem):
+def layer_copies(tile_ref, w_any, near_refs, far_refs, w_ref, stat_ref, sem):
+    _, z, core = place()
+    side = (lax.axis_index("dp") // 2) % 2
+    layer = [lax.rem(z + k, DEPTH) for k in range(DEPTH)]
+    copies = [
+        pltpu.make_async_copy(w_any, w_ref.at[layer[0]], sem.at[0]),
+        pltpu.make_async_copy(tile_ref, stat_ref.at[layer[0]], sem.at[1]),
+    ]
+
+    def add(source, target):
+        copies.append(pltpu.make_async_copy(source, target, sem.at[len(copies)]))
+
+    for k, (a_ref, b_ref) in near_refs:
+        for ref, half in ((a_ref, core), (b_ref, 1 - core)):
+            add(ref.at[pl.ds(0, HALF)], w_ref.at[layer[k], pl.ds(pl.multiple_of(half * HALF, HALF), HALF)])
+        add(a_ref.at[pl.ds(HALF, STAT)], stat_ref.at[layer[k]])
+    for index, ref in enumerate(far_refs):
+        half = core if index < 2 else 1 - core
+        which = side if index % 2 == 0 else 1 - side
+        add(ref.at[pl.ds(0, PART)], w_ref.at[layer[2], pl.ds(part_start(half, which), PART)])
+    add(far_refs[0].at[pl.ds(PART, STAT)], stat_ref.at[layer[2]])
+    return copies
+
+
+def first_kernel(
+    images_any, w_any, tile_ref, a1_ref, b1_ref, a3_ref, b3_ref, f0_ref, f1_ref, f2_ref, f3_ref,
+    out_ref, w_ref, stat_ref, x_buf, pad_ref, sem, x_sem,
+):
     _, z, _ = place()
+    copies = layer_copies(
+        tile_ref, w_any, ((1, (a1_ref, b1_ref)), (3, (a3_ref, b3_ref))), (f0_ref, f1_ref, f2_ref, f3_ref),
+        w_ref, stat_ref, sem,
+    )
     x_copy = pltpu.make_async_copy(images_any.at[z], x_buf, x_sem)
     x_copy.start()
+    for copy in copies:
+        copy.start()
     clear_pads(pad_ref)
     x_copy.wait()
     x = x_buf[...]
+    for copy in copies:
+        copy.wait()
     for l in range(DEPTH):
-        stat = read_stats(a_ref, l)
-        x = activate(forward_layer(x, l, a_ref, b_ref, stat, pad_ref), stat)
+        stat = unpack_rows(stat_ref[l])
+        x = activate(forward_layer(x, l, w_ref, stat, pad_ref), stat)
     out_ref[...] = x
 
 
-def flip_kernel(a_ref, b_ref, flip_ref):
-    _, _, core = place()
-    for source, half in ((a_ref, core), (b_ref, 1 - core)):
-        for l in range(DEPTH):
-            for tap in range(TAPS):
-                at = pl.ds(pl.multiple_of(tap * C + half * LANES, LANES), LANES)
-                flip_ref[l, at, :] = source[l, tap * C : (tap + 1) * C, :].T
+def flip_kernel(w_ref, flip_ref):
+    for l in range(DEPTH):
+        for tap in range(TAPS):
+            at = slice(tap * C, (tap + 1) * C)
+            flip_ref[l, at, :] = w_ref[l, at, :].T
 
 
 def middle_kernel(
-    images_any, cot_any, recv_ref, a_ref, b_ref, flip_ref, dx_ref, xs_ref, conv_ref, scaled_ref,
+    images_any, cot_any, recv_ref, w_ref, flip_ref, stat_ref, dx_ref, xs_ref, conv_ref, scaled_ref,
     x_buf, u_buf, pad_ref, x_sem,
 ):
     half, z, _ = place()
@@ -246,9 +281,9 @@
     x = jnp.where(half == 1, recv_ref[...], x_buf[...])
     stats = []
     for l in range(DEPTH):
-        stats.append(read_stats(a_ref, l))
+        stats.append(unpack_rows(stat_ref[l]))
         xs_ref[l] = x
-        conv = forward_layer(x, l, a_ref, b_ref, stats[l], pad_ref)
+        conv = forward_layer(x, l, w_ref, stats[l], pad_ref)
         conv_ref[l] = conv
         scaled_ref[lax.rem(l - z + DEPTH, DEPTH)] = pad_ref[1, ROW : ROW + PX, :]
         if l < DEPTH - 1:
@@ -260,7 +295,7 @@
     dx_ref[...] = upstream
 
 
-def last_kernel(cot_any, recv_ref, xs_ref, conv_ref, flip_ref, a_ref, send_ref, u_buf, pad_ref, u_sem):
+def last_kernel(cot_any, recv_ref, xs_ref, conv_ref, flip_ref, stat_ref, send_ref, u_buf, pad_ref, u_sem):
     half, z, _ = place()
     u_copy = pltpu.make_async_copy(cot_any.at[z], u_buf, u_sem)
     u_copy.start()
@@ -268,7 +303,7 @@
     u_copy.wait()
     upstream = jnp.where(half == 1, u_buf[...], recv_ref[...])
     for l in reversed(range(DEPTH)):
-        stat = read_stats(a_ref, l)
+        stat = unpack_rows(stat_ref[l])
         upstream = backward_layer(upstream, xs_ref[l], conv_ref[l], l, flip_ref, stat, pad_ref, send_ref)
 
 
@@ -277,34 +312,35 @@
 SENT = jax.ShapeDtypeStruct((DEPTH, PX + STAT, C), BF)
 
 
-def first(images, a, b):
+def first(images, w, tile, *parts):
     return pl.pallas_call(
         first_kernel,
-        out_shape=MAP,
-        in_specs=[any_spec(), vmem_spec(), vmem_spec()],
-        out_specs=vmem_spec(),
+        out_shape=(MAP, KERNELS, jax.ShapeDtypeStruct((DEPTH, STAT, C), BF)),
+        in_specs=[pl.BlockSpec(memory_space=pltpu.HBM), any_spec()] + [vmem_spec()] * 9,
+        out_specs=(vmem_spec(),) * 3,
         scratch_shapes=[
             pltpu.VMEM((PX, C), BF),
             pltpu.VMEM((3, PAD, C), BF),
+            pltpu.SemaphoreType.DMA((13,)),
             pltpu.SemaphoreType.DMA,
         ],
         compiler_params=params(),
         name="first",
-    )(images, a, b)
-
-
-def flip(a, b):
+    )(pltpu.with_memory_space_constraint(images, pltpu.HBM), w, tile, *parts)
+
+
+def flip(w):
     return pl.pallas_call(
         flip_kernel,
         out_shape=KERNELS,
-        in_specs=[vmem_spec()] * 2,
+        in_specs=[vmem_spec()],
         out_specs=vmem_spec(),
         compiler_params=params(),
         name="flip",
-    )(a, b)
-
-
-def middle(images, cot, recv, a, b, flipped):
+    )(w)
+
+
+def middle(images, cot, recv, w, flipped, stat):
     return pl.pallas_call(
         middle_kernel,
         out_shape=(
@@ -323,10 +359,10 @@
         ],
         compiler_params=params(),
         name="middle",
-    )(images, cot, recv, a, b, flipped)
-
-
-def last(cot, recv, xs, conv, flipped, a):
+    )(images, cot, recv, w, flipped, stat)
+
+
+def last(cot, recv, xs, conv, flipped, stat):
     return pl.pallas_call(
         last_kernel,
         out_shape=SENT,
@@ -339,7 +375,7 @@
         ],
         compiler_params=params(),
         name="last",
-    )(cot, recv, xs, conv, flipped, a)
+    )(cot, recv, xs, conv, flipped, stat)
 
 
 def half_gradient(flip_ref, pad_ref, w_ref, grad_energy_ref, half, out_ref):
@@ -581,15 +617,24 @@
     images = images.reshape(DEPTH, PX, C)
     cotangent = cotangent.reshape(DEPTH, PX, C)
 
-    send, styles, demod, energy = prepare(latent, affine[0], w, biases)
-    a = lax.all_to_all(send, "segment", 0, 0, axis_index_groups=planes)
-    b = near(lax.ppermute(a, "dp", sibling))
-    a = near(a)
-
-    act = first(images, a, b)
-    flipped = flip(a, b)
+    def along(value, shift):
+        pairs = [(i, i - i % DEPTH + (i + shift) % DEPTH) for i in range(segments)]
+        return near(lax.ppermute(value, "segment", pairs))
+
+    def swap(value):
+        return near(lax.ppermute(value, "dp", sibling))
+
+    beside = [(i, i ^ 2) for i in range(replicas)]
+    down, up, far, tile, styles, demod, energy = prepare(latent, affine[0], w, biases)
+    f0 = along(far, 2)
+    f0, down, up = lax.optimization_barrier((f0, down, up))
+    f1 = near(lax.ppermute(f0, "dp", beside))
+    a1 = along(down, DEPTH - 1)
+    a3 = along(up, 1)
+    act, kernels, stat = first(images, w, tile, a1, swap(a1), a3, swap(a3), f0, f1, swap(f0), swap(f1))
+    flipped = flip(kernels)
     arrived = near(lax.ppermute(act, "segment", across))
-    dx, xs, conv, scaled = middle(images, cotangent, arrived, a, b, flipped)
+    dx, xs, conv, scaled = middle(images, cotangent, arrived, kernels, flipped, stat)
     returned = near(lax.ppermute(dx, "segment", across))
     maps = [scaled[0]] + [
         near(
@@ -600,7 +645,7 @@
         for k in range(1, DEPTH)
     ]
     turned = turn(*maps)
-    sent, turned = lax.optimization_barrier((last(cotangent, returned, xs, conv, flipped, a), turned))
+    sent, turned = lax.optimization_barrier((last(cotangent, returned, xs, conv, flipped, stat), turned))
 
     r = near(lax.all_to_all(sent, "segment", 0, 0, axis_index_groups=planes))
     give, extra, part, padded, grad_energy = give_half(

time: 124 us -> 119 us (0.960)
  blocking collectives: 58.8 us -> 24.2 us
  waiting for transfers between devices: 21.4 us -> 38.7 us
  starting transfers between devices: 21.9 us -> 32.9 us
    all_to_all x1 -> x0, blocking collectives: 34.2 us -> none  [body(): a = lax.all_to_all(send, 'segment', 0, 0, axis_index_groups=planes)]
    ppermute x1 -> x8, waiting for transfers between devices: 4.21 us -> 19.6 us  [the longest x3 17.6 us: along(): return near(lax.ppermute(value, 'segment', pairs))]
    ppermute x1 -> x8, starting transfers between devices: 2.06 us -> 14.3 us  [the longest x3 7.32 us: along(): return near(lax.ppermute(value, 'segment', pairs))]
    ppermute x3, waiting for transfers between devices: 3.44 us -> 4.73 us  [body(): lax.ppermute(scaled[k], 'segment', [(i, i - i % DEPTH + (i + k) % DEPTH)...]
  transfers between devices with their start and end apart: 12 -> 19, of which waited for: 10 -> 14; matrix products, arithmetic and copies ran while one was open for 0% -> 0% of each run, Pallas kernels for 5% -> 6%
where the time goes in v8:
time: 119 us
  waiting for transfers between devices  38.7 us (33%)
  starting transfers between devices  32.9 us (28%)
  blocking collectives  24.2 us (20%)
  Pallas kernels  22 us (18%)
    ppermute x3, waiting for transfers between devices, along(): return near(lax.ppermute(value, 'segment', pairs))  17.6 us
    all_to_all x1, blocking collectives, body(): lax.all_to_all(near(spread_share), 'dp', 0, 0, axis_index_groups=cores)  13.3 us
    all_to_all x1, blocking collectives, body(): r = near(lax.all_to_all(sent, 'segment', 0, 0, axis_index_groups=planes))  10.9 us
    ppermute x3, starting transfers between devices, along(): return near(lax.ppermute(value, 'segment', pairs))  7.32 us
    ppermute x4, starting transfers between devices, swap(): return near(lax.ppermute(value, 'dp', sibling))  5.73 us
    all_to_all x1, waiting for transfers between devices, body(): lax.all_to_all(near(shared), 'dp', 0, 0, axis_index_groups=cores)  4.8 us
    ppermute x3, waiting for transfers between devices, body(): lax.ppermute(scaled[k], 'segment', [(i, i - i % DEPTH + (i + k) % DEPTH)...  4.73 us
    pallas_call x1, Pallas kernels, middle(): pl.pallas_call(middle_kernel, out_shape=(MAP, jax.ShapeDtypeStruct((DEPTH...  4.44 us
  transfers between devices with their start and end apart: 19, of which 14 were waited for; matrix products, arithmetic and copies ran while one was open for 0% of the time, Pallas kernels for 6%

profile of v8, /device:TPU:1, one launch (start us, length us, event | category | flops | bytes accessed | tf_op | source)
XLA Modules:
  0.0 118.8 jit_solution(8623388629922378028)
XLA Ops:
  0.6 0.0 copy-start
  0.6 2.2 %prepare.1 = (bf16[1168,256]{1,0:T(8,128)(2,1)S(1)}, bf16[1168,256]{1,0:T(8,128)(2,1)S(1)}, bf16[592,256]{1,0:T(8,128)(2,1)S(1)}, bf16[16,256]{1,0:T(8,128)(2,1)...) custom-call(f32[4,512]{1,0:T(4,128)} %latent_ref.1, f32[512,256]{1,0:T(8,128)} %bitcast.20, ...), custom_call_target="tpu_custom_call" | custom-call | tf_op jit(solution)/shard_map/prepare/pallas_call | solution.py:135
  2.9 4.5 %collective-permute-start = (bf16[592,256]{1,0:T(8,128)(2,1)S(1)}, bf16[592,256]{1,0:T(8,128)(2,1)S(1)}, u32[]{:S(2)}, u32[]{:S(2)}) collective-permute-start(bf16[592,256]{1,0:T(8,128)(2,1)S(1)} %get-tuple-element.40), channel_id=1, source_target_pairs={{0,32},{16,48},{32,0},{48,16},{64,96},{80,112},{96,64},{112,80},{1... | collective-permute-start | bytes 909320 | tf_op jit(solution)/shard_map/ppermute | solution.py:622
  7.4 6.9 %collective-permute-done.f0_ref = bf16[592,256]{1,0:T(8,128)(2,1)S(1)} collective-permute-done((bf16[592,256]{1,0:T(8,128)(2,1)S(1)}, bf16[592,256]{1,0:T(8,128)(2,1)S(1)}, u32[]{:S(2)}, u32[]{:S(2)}) %collective-permute-start) | collective-permute-done | bytes 303136 | tf_op jit(solution)/shard_map/ppermute | solution.py:622
  14.3 2.8 %collective-permute-start.1 = (bf16[1168,256]{1,0:T(8,128)(2,1)S(1)}, bf16[1168,256]{1,0:T(8,128)(2,1)S(1)}, u32[]{:S(2)}, u32[]{:S(2)}) collective-permute-start(bf16[1168,256]{1,0:T(8,128)(2,1)S(1)} %get-tuple-element.43), channel_id=1, source_target_pairs={{0,48},{16,0},{32,16},{48,32},{64,112},{80,64},{96,80},{112,96},{1... | collective-permute-start | bytes 1794056 | tf_op jit(solution)/shard_map/ppermute | solution.py:622
  17.1 0.0 collective-permute-start.3
  17.1 1.2 %collective-permute-start.5 = (bf16[592,256]{1,0:T(8,128)(2,1)S(1)}, bf16[592,256]{1,0:T(8,128)(2,1)S(1)}, u32[]{:S(2)}, u32[]{:S(2)}) collective-permute-start(bf16[592,256]{1,0:T(8,128)(2,1)S(1)} %collective-permute-done.f0_ref), channel_id=1, source_target_pairs={{0,2},{1,3},{2,0},{3,1},{4,6},{5,7},{6,4},{7,5},{8,10},{9,11},{10,... | collective-permute-start | bytes 909320 | tf_op jit(solution)/shard_map/ppermute | solution.py:631
  18.3 10.0 %collective-permute-done.1.a1_ref = bf16[1168,256]{1,0:T(8,128)(2,1)S(1)} collective-permute-done((bf16[1168,256]{1,0:T(8,128)(2,1)S(1)}, bf16[1168,256]{1,0:T(8,128)(2,1)S(1)}, u32[]{:S(2)}, u32[]{:S(2)}) %collective-permute-start.1) | collective-permute-done | bytes 598048 | tf_op jit(solution)/shard_map/ppermute | solution.py:622
  28.4 2.5 %collective-permute-start.2 = (bf16[1168,256]{1,0:T(8,128)(2,1)S(1)}, bf16[1168,256]{1,0:T(8,128)(2,1)S(1)}, u32[]{:S(2)}, u32[]{:S(2)}) collective-permute-start(bf16[1168,256]{1,0:T(8,128)(2,1)S(1)} %collective-permute-done.1.a1_ref), channel_id=1, source_target_pairs={{0,1},{1,0},{2,3},{3,2},{4,5},{5,4},{6,7},{7,6},{8,9},{9,8},{10,11... | collective-permute-start | bytes 1794056 | tf_op jit(solution)/shard_map/ppermute | solution.py:625
  30.8 0.7 collective-permute-done.3.a3_ref
  31.5 2.7 %collective-permute-start.4 = (bf16[1168,256]{1,0:T(8,128)(2,1)S(1)}, bf16[1168,256]{1,0:T(8,128)(2,1)S(1)}, u32[]{:S(2)}, u32[]{:S(2)}) collective-permute-start(bf16[1168,256]{1,0:T(8,128)(2,1)S(1)} %collective-permute-done.3.a3_ref), channel_id=1, source_target_pairs={{0,1},{1,0},{2,3},{3,2},{4,5},{5,4},{6,7},{7,6},{8,9},{9,8},{10,11... | collective-permute-start | bytes 1794056 | tf_op jit(solution)/shard_map/ppermute | solution.py:625
  34.2 0.0 collective-permute-start.6
  34.2 0.0 collective-permute-done.5.f1_ref
  34.2 0.5 collective-permute-start.7
  34.8 1.6 %collective-permute-done.6.f2_ref = bf16[592,256]{1,0:T(8,128)(2,1)S(1)} collective-permute-done((bf16[592,256]{1,0:T(8,128)(2,1)S(1)}, bf16[592,256]{1,0:T(8,128)(2,1)S(1)}, u32[]{:S(2)}, u32[]{:S(2)}) %collective-permute-start.6) | collective-permute-done | bytes 303136 | tf_op jit(solution)/shard_map/ppermute | solution.py:625
  36.3 0.4 collective-permute-done.7.f3_ref
  36.8 0.0 collective-permute-done.2.b1_ref
  36.8 0.0 collective-permute-done.4.b3_ref
  36.8 0.0 copy-done
  36.8 3.3 %first.1 = (bf16[256,256]{1,0:T(8,128)(2,1)S(1)}, bf16[4,2304,256]{2,1,0:T(8,128)(2,1)S(1)}, bf16[4,16,256]{2,1,0:T(8,128)(2,1)S(1)}) custom-call(bf16[4,256,256]{2,1,0:T(8,128)(2,1)} %bitcast.22, bf16[2304,256]{1,0:T(8,128)(2,1)S(1)} %bitcast.15, bf16[16,256]{1,0:T(8,128)(2,1)S(1)} %get-tuple-element.39.tile_ref, ...), custom_call_target="tpu_custom_call" | custom-call | tf_op jit(solution)/shard_map/first/pallas_call | solution.py:316
  40.1 2.8 %collective-permute-start.8 = (bf16[256,256]{1,0:T(8,128)(2,1)S(1)}, bf16[256,256]{1,0:T(8,128)(2,1)S(1)}, u32[]{:S(2)}, u32[]{:S(2)}) collective-permute-start(bf16[256,256]{1,0:T(8,128)(2,1)S(1)} %get-tuple-element.46), channel_id=1, source_target_pairs={{0,64},{16,80},{32,96},{48,112},{64,0},{80,16},{96,32},{112,48},{1... | collective-permute-start | bytes 393224 | tf_op jit(solution)/shard_map/ppermute | solution.py:636
  42.9 0.0 copy-start.1
  42.9 0.0 copy-start.3
  42.9 1.3 %flip.1.flip_ref = bf16[4,2304,256]{2,1,0:T(8,128)(2,1)S(1)} custom-call(bf16[4,2304,256]{2,1,0:T(8,128)(2,1)S(1)} %get-tuple-element.47.w_ref), custom_call_target="tpu_custom_call" | custom-call | tf_op jit(solution)/shard_map/flip/pallas_call | solution.py:333
  44.2 2.2 %collective-permute-done.8.recv_ref = bf16[256,256]{1,0:T(8,128)(2,1)S(1)} collective-permute-done((bf16[256,256]{1,0:T(8,128)(2,1)S(1)}, bf16[256,256]{1,0:T(8,128)(2,1)S(1)}, u32[]{:S(2)}, u32[]{:S(2)}) %collective-permute-start.8) | collective-permute-done | bytes 131104 | tf_op jit(solution)/shard_map/ppermute | solution.py:636
  46.4 0.0 copy-done.1
  46.4 0.0 copy-done.3
  46.4 4.4 %middle.1 = (bf16[256,256]{1,0:T(8,128)(2,1)S(1)}, bf16[4,256,256]{2,1,0:T(8,128)(2,1)S(1)}, f32[4,256,256]{2,1,0:T(8,128)S(1)}, bf16[4,256,256]{2,1,0:T(8,128)(2,1)S(1)}) custom-call(bf16[4,256,256]{2,1,0:T(8,128)(2,1)S(1)} %bitcast.23, bf16[4,256,256]{2,1,0:T(8,128)(2,1)S(1)} %bitcast.18, bf16[256,256]{1,0:T(8,128)(2,1)S(1)} %collective-permute-done.8.recv_ref, ...), custom_call_target="tpu_custom_call" | custom-call | tf_op jit(solution)/shard_map/middle/pallas_call | solution.py:344
  50.9 2.8 %collective-permute-start.9 = (bf16[256,256]{1,0:T(8,128)(2,1)S(1)}, bf16[256,256]{1,0:T(8,128)(2,1)S(1)}, u32[]{:S(2)}, u32[]{:S(2)}) collective-permute-start(bf16[256,256]{1,0:T(8,128)(2,1)S(1)} %get-tuple-element.49), channel_id=1, source_target_pairs={{0,64},{16,80},{32,96},{48,112},{64,0},{80,16},{96,32},{112,48},{1... | collective-permute-start | bytes 393224 | tf_op jit(solution)/shard_map/ppermute | solution.py:638
  53.7 0.9 collective-permute-start.12
  54.6 0.0 collective-permute-start.11
  54.7 0.7 collective-permute-start.10
  55.3 0.9 collective-permute-done.9.recv_ref
  56.3 0.0 copy-start.4
  56.3 2.6 %last.1 = bf16[4,272,256]{2,1,0:T(8,128)(2,1)S(1)} custom-call(bf16[4,256,256]{2,1,0:T(8,128)(2,1)S(1)} %bitcast.19, bf16[256,256]{1,0:T(8,128)(2,1)S(1)} %collective-permute-done.9.recv_ref, bf16[4,256,256]{2,1,0:T(8,128)(2,1)S(1)} %get-tuple-element.50.xs_ref, f32[4,256,256]{2,1,0:T(8,128)S(1)} %get-tuple-element.51.conv_ref, ...), custom_call_target="tpu_custom_call" | custom-call | tf_op jit(solution)/shard_map/last/pallas_call | solution.py:366
  58.8 0.0 copy-start.2
  58.8 0.0 collective-permute-done.12.s3_ref
  58.8 1.2 %collective-permute-done.11.s2_ref = bf16[256,256]{1,0:T(8,128)(2,1)S(1)} collective-permute-done((bf16[256,256]{1,0:T(8,128)(2,1)S(1)}, bf16[256,256]{1,0:T(8,128)(2,1)S(1)}, u32[]{:S(2)}, u32[]{:S(2)}) %collective-permute-start.11) | collective-permute-done | bytes 131104 | tf_op jit(solution)/shard_map/ppermute | solution.py:641
  60.1 3.5 %collective-permute-done.10.s1_ref = bf16[256,256]{1,0:T(8,128)(2,1)S(1)} collective-permute-done((bf16[256,256]{1,0:T(8,128)(2,1)S(1)}, bf16[256,256]{1,0:T(8,128)(2,1)S(1)}, u32[]{:S(2)}, u32[]{:S(2)}) %collective-permute-start.10) | collective-permute-done | bytes 131104 | tf_op jit(solution)/shard_map/ppermute | solution.py:641
  63.6 0.2 turn.1.flip_ref
  63.8 10.9 %all_to_all.15.r_ref = bf16[4,272,256]{2,1,0:T(8,128)(2,1)S(1)} all-to-all(bf16[4,272,256]{2,1,0:T(8,128)(2,1)S(1)} %last.1), channel_id=1, replica_groups={{0,16,32,48},{64,80,96,112},{1,17,33,49},{65,81,97,113},{2,18,34,50},{6..., dimensions={0} | all-to-all | bytes 1114112 | tf_op jit(solution)/shard_map/all_to_all | solution.py:650
  74.7 0.0 copy-done.4
  74.7 0.0 copy-done.2
  74.7 2.3 %give.1 = (bf16[1168,256]{1,0:T(8,128)(2,1)S(1)}, bf16[16,256]{1,0:T(8,128)(2,1)S(1)}, f32[4,512]{1,0:T(4,128)S(1)}, bf16[4,3,288,256]{3,2,1,0:T(8,128)(2,1)S(1)}, f32[256,256]{1,0:T(8,128)S(1)}) custom-call(bf16[4,272,256]{2,1,0:T(8,128)(2,1)S(1)} %all_to_all.15.r_ref, bf16[256,1024]{1,0:T(8,128)(2,1)S(1)} %turn.1.flip_ref, bf16[2304,256]{1,0:T(8,128)(2,1)S(1)} %bitcast.16, ...), custom_call_target="tpu_custom_call" | custom-call | tf_op jit(solution)/shard_map/give/pallas_call | solution.py:449
  77.0 2.3 %collective-permute-start.13 = (bf16[1168,256]{1,0:T(8,128)(2,1)S(1)}, bf16[1168,256]{1,0:T(8,128)(2,1)S(1)}, u32[]{:S(2)}, u32[]{:S(2)}) collective-permute-start(bf16[1168,256]{1,0:T(8,128)(2,1)S(1)} %get-tuple-element.61), channel_id=1, source_target_pairs={{0,1},{1,0},{2,3},{3,2},{4,5},{5,4},{6,7},{7,6},{8,9},{9,8},{10,11... | collective-permute-start | bytes 1794056 | tf_op jit(solution)/shard_map/ppermute | solution.py:654
  79.3 0.8 keep.1.keep_ref
  80.2 0.8 collective-permute-done.13.got_ref
  81.0 1.0 pair.1
  82.0 4.2 %all-to-all-start.1 = ((bf16[8,176,256]{2,1,0:T(8,128)(2,1)}), bf16[8,176,256]{2,1,0:T(8,128)(2,1)S(1)}, u32[]{:S(2)}, u32[]{:S(2)}) async-start(bf16[8,176,256]{2,1,0:T(8,128)(2,1)} %pair.1), calls=%async_computation.1 | async-start | bytes 1441792 | tf_op jit(solution)/shard_map/all_to_all | solution.py:657
  86.2 0.3 collective-permute-start.14
  86.4 2.2 %collective-permute-done.14 = f32[4,512]{1,0:T(4,128)S(1)} collective-permute-done((f32[4,512]{1,0:T(4,128)S(1)}, f32[4,512]{1,0:T(4,128)S(1)}, u32[]{:S(2)}, u32[]{:S(2)}) %collective-permute-start.14) | collective-permute-done | bytes 8224 | tf_op jit(solution)/shard_map/ppermute | solution.py:658
  88.7 0.8 collective-permute-start.15
  89.5 3.2 %collective-permute-done.15 = f32[4,512]{1,0:T(4,128)S(1)} collective-permute-done((f32[4,512]{1,0:T(4,128)S(1)}, f32[4,512]{1,0:T(4,128)S(1)}, u32[]{:S(2)}, u32[]{:S(2)}) %collective-permute-start.15) | collective-permute-done | bytes 8224 | tf_op jit(solution)/shard_map/ppermute | solution.py:659
  92.7 4.8 %all-to-all-done.1.shares_ref = bf16[8,176,256]{2,1,0:T(8,128)(2,1)S(1)} async-done(((bf16[8,176,256]{2,1,0:T(8,128)(2,1)}), bf16[8,176,256]{2,1,0:T(8,128)(2,1)S(1)}, u32[]{:S(2)}, u32[]{:S(2)}) %all-to-all-start.1) | async-done | bytes 720928 | tf_op jit(solution)/shard_map/all_to_all | solution.py:657
  97.5 0.1 share.1
  97.6 13.3 %all_to_all.16.value_ref = bf16[8,144,256]{2,1,0:T(8,128)(2,1)S(1)} all-to-all(bf16[8,144,256]{2,1,0:T(8,128)(2,1)S(1)} %share.1), channel_id=1, replica_groups={{0,2,4,6,8,10,12,14},{1,3,5,7,9,11,13,15},{16,18,20,22,24,26,28,30},{17..., dimensions={0} | all-to-all | bytes 1179648 | tf_op jit(solution)/shard_map/all_to_all | solution.py:661
  110.9 2.1 %collective-permute-start.16 = (bf16[8,144,256]{2,1,0:T(8,128)(2,1)S(1)}, bf16[8,144,256]{2,1,0:T(8,128)(2,1)S(1)}, u32[]{:S(2)}, u32[]{:S(2)}) collective-permute-start(bf16[8,144,256]{2,1,0:T(8,128)(2,1)S(1)} %all_to_all.16.value_ref), channel_id=1, source_target_pairs={{0,1},{1,0},{2,3},{3,2},{4,5},{5,4},{6,7},{7,6},{8,9},{9,8},{10,11... | collective-permute-start | bytes 1769480 | tf_op jit(solution)/shard_map/ppermute | solution.py:662
  113.0 1.7 %collective-permute-start.17 = (f32[4,512]{1,0:T(4,128)S(1)}, f32[4,512]{1,0:T(4,128)S(1)}, u32[]{:S(2)}, u32[]{:S(2)}) collective-permute-start(f32[4,512]{1,0:T(4,128)S(1)} %add.7.part_ref), channel_id=1, source_target_pairs={{0,64},{16,80},{32,96},{48,112},{64,0},{80,16},{96,32},{112,48},{1... | collective-permute-start | bytes 24584 | tf_op jit(solution)/shard_map/ppermute | solution.py:664
  114.7 1.1 affine.1
  115.8 1.1 own.1.target_any
  116.8 0.1 collective-permute-done.17.moved_ref
  117.0 0.0 collective-permute-done.16.value_ref
  117.0 1.7 %rest.1 = (f32[9,256,256]{2,1,0:T(8,128)}, f32[4,512]{1,0:T(4,128)}) custom-call(bf16[8,144,256]{2,1,0:T(8,128)(2,1)S(1)} %collective-permute-done.16.value_ref, f32[9,256,256]{2,1,0:T(8,128)} %own.1.target_any, f32[4,512]{1,0:T(4,128)S(1)} %add.7.part_ref, f32[4,512]{1,0:T(4,128)S(1)} %collective-permute-done.17.moved_ref), custom_call_target="tpu_custom_call", output_to_operand_aliasing={{0}: (1, {})} | custom-call | tf_op jit(solution)/shard_map/rest/pallas_call | solution.py:595
  (3 shorter events, 0.0 us)
Async XLA Ops:
  0.6 36.1 %copy-start = (bf16[1,3,3,256,256]{4,3,2,1,0:T(8,128)(2,1)S(1)}, bf16[1,3,3,256,256]{4,3,2,1,0:T(8,128)(2,1)}, u32[]{:S(2)}) copy-start(bf16[1,3,3,256,256]{4,3,2,1,0:T(8,128)(2,1)} %param.8) | copy-start | bytes 3538948
  2.9 11.4 %collective-permute-start = (bf16[592,256]{1,0:T(8,128)(2,1)S(1)}, bf16[592,256]{1,0:T(8,128)(2,1)S(1)}, u32[]{:S(2)}, u32[]{:S(2)}) collective-permute-start(bf16[592,256]{1,0:T(8,128)(2,1)S(1)} %get-tuple-element.40), channel_id=1, source_target_pairs={{0,32},{16,48},{32,0},{48,16},{64,96},{80,112},{96,64},{112,80},{1... | collective-permute-start | bytes 909320 | tf_op jit(solution)/shard_map/ppermute | solution.py:622
  14.3 14.1 %collective-permute-start.1 = (bf16[1168,256]{1,0:T(8,128)(2,1)S(1)}, bf16[1168,256]{1,0:T(8,128)(2,1)S(1)}, u32[]{:S(2)}, u32[]{:S(2)}) collective-permute-start(bf16[1168,256]{1,0:T(8,128)(2,1)S(1)} %get-tuple-element.43), channel_id=1, source_target_pairs={{0,48},{16,0},{32,16},{48,32},{64,112},{80,64},{96,80},{112,96},{1... | collective-permute-start | bytes 1794056 | tf_op jit(solution)/shard_map/ppermute | solution.py:622
  17.1 14.4 %collective-permute-start.3 = (bf16[1168,256]{1,0:T(8,128)(2,1)S(1)}, bf16[1168,256]{1,0:T(8,128)(2,1)S(1)}, u32[]{:S(2)}, u32[]{:S(2)}) collective-permute-start(bf16[1168,256]{1,0:T(8,128)(2,1)S(1)} %get-tuple-element.44), channel_id=1, source_target_pairs={{0,16},{16,32},{32,48},{48,0},{64,80},{80,96},{96,112},{112,64},{1... | collective-permute-start | bytes 1794056 | tf_op jit(solution)/shard_map/ppermute | solution.py:622
  17.1 17.1 %collective-permute-start.5 = (bf16[592,256]{1,0:T(8,128)(2,1)S(1)}, bf16[592,256]{1,0:T(8,128)(2,1)S(1)}, u32[]{:S(2)}, u32[]{:S(2)}) collective-permute-start(bf16[592,256]{1,0:T(8,128)(2,1)S(1)} %collective-permute-done.f0_ref), channel_id=1, source_target_pairs={{0,2},{1,3},{2,0},{3,1},{4,6},{5,7},{6,4},{7,5},{8,10},{9,11},{10,... | collective-permute-start | bytes 909320 | tf_op jit(solution)/shard_map/ppermute | solution.py:631
  28.4 8.4 %collective-permute-start.2 = (bf16[1168,256]{1,0:T(8,128)(2,1)S(1)}, bf16[1168,256]{1,0:T(8,128)(2,1)S(1)}, u32[]{:S(2)}, u32[]{:S(2)}) collective-permute-start(bf16[1168,256]{1,0:T(8,128)(2,1)S(1)} %collective-permute-done.1.a1_ref), channel_id=1, source_target_pairs={{0,1},{1,0},{2,3},{3,2},{4,5},{5,4},{6,7},{7,6},{8,9},{9,8},{10,11... | collective-permute-start | bytes 1794056 | tf_op jit(solution)/shard_map/ppermute | solution.py:625
  31.5 5.3 %collective-permute-start.4 = (bf16[1168,256]{1,0:T(8,128)(2,1)S(1)}, bf16[1168,256]{1,0:T(8,128)(2,1)S(1)}, u32[]{:S(2)}, u32[]{:S(2)}) collective-permute-start(bf16[1168,256]{1,0:T(8,128)(2,1)S(1)} %collective-permute-done.3.a3_ref), channel_id=1, source_target_pairs={{0,1},{1,0},{2,3},{3,2},{4,5},{5,4},{6,7},{7,6},{8,9},{9,8},{10,11... | collective-permute-start | bytes 1794056 | tf_op jit(solution)/shard_map/ppermute | solution.py:625
  34.2 2.1 %collective-permute-start.6 = (bf16[592,256]{1,0:T(8,128)(2,1)S(1)}, bf16[592,256]{1,0:T(8,128)(2,1)S(1)}, u32[]{:S(2)}, u32[]{:S(2)}) collective-permute-start(bf16[592,256]{1,0:T(8,128)(2,1)S(1)} %collective-permute-done.f0_ref), channel_id=1, source_target_pairs={{0,1},{1,0},{2,3},{3,2},{4,5},{5,4},{6,7},{7,6},{8,9},{9,8},{10,11... | collective-permute-start | bytes 909320 | tf_op jit(solution)/shard_map/ppermute | solution.py:625
  34.2 2.5 %collective-permute-start.7 = (bf16[592,256]{1,0:T(8,128)(2,1)S(1)}, bf16[592,256]{1,0:T(8,128)(2,1)S(1)}, u32[]{:S(2)}, u32[]{:S(2)}) collective-permute-start(bf16[592,256]{1,0:T(8,128)(2,1)S(1)} %collective-permute-done.5.f1_ref), channel_id=1, source_target_pairs={{0,1},{1,0},{2,3},{3,2},{4,5},{5,4},{6,7},{7,6},{8,9},{9,8},{10,11... | collective-permute-start | bytes 909320 | tf_op jit(solution)/shard_map/ppermute | solution.py:625
  40.1 6.3 %collective-permute-start.8 = (bf16[256,256]{1,0:T(8,128)(2,1)S(1)}, bf16[256,256]{1,0:T(8,128)(2,1)S(1)}, u32[]{:S(2)}, u32[]{:S(2)}) collective-permute-start(bf16[256,256]{1,0:T(8,128)(2,1)S(1)} %get-tuple-element.46), channel_id=1, source_target_pairs={{0,64},{16,80},{32,96},{48,112},{64,0},{80,16},{96,32},{112,48},{1... | collective-permute-start | bytes 393224 | tf_op jit(solution)/shard_map/ppermute | solution.py:636
  42.9 3.5 %copy-start.1 = (bf16[4,16,16,256]{3,2,1,0:T(8,128)(2,1)S(1)}, bf16[4,16,16,256]{3,2,1,0:T(8,128)(2,1)}, u32[]{:S(2)}) copy-start(bf16[4,16,16,256]{3,2,1,0:T(8,128)(2,1)} %param.11) | copy-start | bytes 1572868
  42.9 3.5 %copy-start.3 = (bf16[4,16,16,256]{3,2,1,0:T(8,128)(2,1)S(1)}, bf16[4,16,16,256]{3,2,1,0:T(8,128)(2,1)}, u32[]{:S(2)}) copy-start(bf16[4,16,16,256]{3,2,1,0:T(8,128)(2,1)} %param.6) | copy-start | bytes 1572868
  50.9 5.4 %collective-permute-start.9 = (bf16[256,256]{1,0:T(8,128)(2,1)S(1)}, bf16[256,256]{1,0:T(8,128)(2,1)S(1)}, u32[]{:S(2)}, u32[]{:S(2)}) collective-permute-start(bf16[256,256]{1,0:T(8,128)(2,1)S(1)} %get-tuple-element.49), channel_id=1, source_target_pairs={{0,64},{16,80},{32,96},{48,112},{64,0},{80,16},{96,32},{112,48},{1... | collective-permute-start | bytes 393224 | tf_op jit(solution)/shard_map/ppermute | solution.py:638
  53.7 5.1 %collective-permute-start.12 = (bf16[256,256]{1,0:T(8,128)(2,1)S(1)}, bf16[256,256]{1,0:T(8,128)(2,1)S(1)}, u32[]{:S(2)}, u32[]{:S(2)}) collective-permute-start(bf16[256,256]{1,0:T(8,128)(2,1)S(1)} %get-tuple-element.74), channel_id=1, source_target_pairs={{0,48},{16,0},{32,16},{48,32},{64,112},{80,64},{96,80},{112,96},{1... | collective-permute-start | bytes 393224 | tf_op jit(solution)/shard_map/ppermute | solution.py:641
  54.6 5.4 %collective-permute-start.11 = (bf16[256,256]{1,0:T(8,128)(2,1)S(1)}, bf16[256,256]{1,0:T(8,128)(2,1)S(1)}, u32[]{:S(2)}, u32[]{:S(2)}) collective-permute-start(bf16[256,256]{1,0:T(8,128)(2,1)S(1)} %get-tuple-element.75), channel_id=1, source_target_pairs={{0,32},{16,48},{32,0},{48,16},{64,96},{80,112},{96,64},{112,80},{1... | collective-permute-start | bytes 393224 | tf_op jit(solution)/shard_map/ppermute | solution.py:641
  54.7 8.9 %collective-permute-start.10 = (bf16[256,256]{1,0:T(8,128)(2,1)S(1)}, bf16[256,256]{1,0:T(8,128)(2,1)S(1)}, u32[]{:S(2)}, u32[]{:S(2)}) collective-permute-start(bf16[256,256]{1,0:T(8,128)(2,1)S(1)} %get-tuple-element.76), channel_id=1, source_target_pairs={{0,16},{16,32},{32,48},{48,0},{64,80},{80,96},{96,112},{112,64},{1... | collective-permute-start | bytes 393224 | tf_op jit(solution)/shard_map/ppermute | solution.py:641
  56.3 18.5 %copy-start.4 = (f32[4,512]{1,0:T(4,128)S(1)}, f32[4,512]{1,0:T(4,128)}, u32[]{:S(2)}) copy-start(f32[4,512]{1,0:T(4,128)} %latent_ref.1) | copy-start | bytes 24580
  58.8 15.9 %copy-start.2 = (f32[1,512,256]{2,1,0:T(8,128)S(1)}, f32[1,512,256]{2,1,0:T(8,128)}, u32[]{:S(2)}) copy-start(f32[1,512,256]{2,1,0:T(8,128)} %param.9) | copy-start | bytes 1572868
  77.0 4.0 %collective-permute-start.13 = (bf16[1168,256]{1,0:T(8,128)(2,1)S(1)}, bf16[1168,256]{1,0:T(8,128)(2,1)S(1)}, u32[]{:S(2)}, u32[]{:S(2)}) collective-permute-start(bf16[1168,256]{1,0:T(8,128)(2,1)S(1)} %get-tuple-element.61), channel_id=1, source_target_pairs={{0,1},{1,0},{2,3},{3,2},{4,5},{5,4},{6,7},{7,6},{8,9},{9,8},{10,11... | collective-permute-start | bytes 1794056 | tf_op jit(solution)/shard_map/ppermute | solution.py:654
  82.0 15.5 %all-to-all-start.1 = ((bf16[8,176,256]{2,1,0:T(8,128)(2,1)}), bf16[8,176,256]{2,1,0:T(8,128)(2,1)S(1)}, u32[]{:S(2)}, u32[]{:S(2)}) async-start(bf16[8,176,256]{2,1,0:T(8,128)(2,1)} %pair.1), calls=%async_computation.1 | async-start | bytes 1441792 | tf_op jit(solution)/shard_map/all_to_all | solution.py:657
  86.2 2.5 %collective-permute-start.14 = (f32[4,512]{1,0:T(4,128)S(1)}, f32[4,512]{1,0:T(4,128)S(1)}, u32[]{:S(2)}, u32[]{:S(2)}) collective-permute-start(f32[4,512]{1,0:T(4,128)S(1)} %get-tuple-element.64), channel_id=1, source_target_pairs={{0,16},{16,0},{32,48},{48,32},{64,80},{80,64},{96,112},{112,96},{1... | collective-permute-start | bytes 24584 | tf_op jit(solution)/shard_map/ppermute | solution.py:658
  88.7 4.0 %collective-permute-start.15 = (f32[4,512]{1,0:T(4,128)S(1)}, f32[4,512]{1,0:T(4,128)S(1)}, u32[]{:S(2)}, u32[]{:S(2)}) collective-permute-start(f32[4,512]{1,0:T(4,128)S(1)} %add.6), channel_id=1, source_target_pairs={{0,32},{16,48},{32,0},{48,16},{64,96},{80,112},{96,64},{112,80},{1... | collective-permute-start | bytes 24584 | tf_op jit(solution)/shard_map/ppermute | solution.py:659
  110.9 6.1 %collective-permute-start.16 = (bf16[8,144,256]{2,1,0:T(8,128)(2,1)S(1)}, bf16[8,144,256]{2,1,0:T(8,128)(2,1)S(1)}, u32[]{:S(2)}, u32[]{:S(2)}) collective-permute-start(bf16[8,144,256]{2,1,0:T(8,128)(2,1)S(1)} %all_to_all.16.value_ref), channel_id=1, source_target_pairs={{0,1},{1,0},{2,3},{3,2},{4,5},{5,4},{6,7},{7,6},{8,9},{9,8},{10,11... | collective-permute-start | bytes 1769480 | tf_op jit(solution)/shard_map/ppermute | solution.py:662
  113.0 4.0 %collective-permute-start.17 = (f32[4,512]{1,0:T(4,128)S(1)}, f32[4,512]{1,0:T(4,128)S(1)}, u32[]{:S(2)}, u32[]{:S(2)}) collective-permute-start(f32[4,512]{1,0:T(4,128)S(1)} %add.7.part_ref), channel_id=1, source_target_pairs={{0,64},{16,80},{32,96},{48,112},{64,0},{80,16},{96,32},{112,48},{1... | collective-permute-start | bytes 24584 | tf_op jit(solution)/shard_map/ppermute | solution.py:664

commit v9 on v8

--- a/solution.py
+++ b/solution.py
@@ -627,7 +627,7 @@
     beside = [(i, i ^ 2) for i in range(replicas)]
     down, up, far, tile, styles, demod, energy = prepare(latent, affine[0], w, biases)
     f0 = along(far, 2)
-    f0, down, up = lax.optimization_barrier((f0, down, up))
+    f0, up = lax.optimization_barrier((f0, up))
     f1 = near(lax.ppermute(f0, "dp", beside))
     a1 = along(down, DEPTH - 1)
     a3 = along(up, 1)

time: 119 us -> 117 us (0.983)
  starting transfers between devices: 32.9 us -> 30.7 us
    ppermute x3, starting transfers between devices: 7.32 us -> 5.67 us  [along(): return near(lax.ppermute(value, 'segment', pairs))]
  transfers between devices with their start and end apart: 19 -> 19, of which waited for: 14 -> 13; matrix products, arithmetic and copies ran while one was open for 0% -> 0% of each run, Pallas kernels for 6% -> 6%
where the time goes in v9:
time: 117 us
  waiting for transfers between devices  38.6 us (33%)
  starting transfers between devices  30.7 us (26%)
  blocking collectives  24.2 us (21%)
  Pallas kernels  22 us (19%)
    ppermute x3, waiting for transfers between devices, along(): return near(lax.ppermute(value, 'segment', pairs))  17.8 us
    all_to_all x1, blocking collectives, body(): lax.all_to_all(near(spread_share), 'dp', 0, 0, axis_index_groups=cores)  13.3 us
    all_to_all x1, blocking collectives, body(): r = near(lax.all_to_all(sent, 'segment', 0, 0, axis_index_groups=planes))  11 us
    ppermute x3, starting transfers between devices, along(): return near(lax.ppermute(value, 'segment', pairs))  5.67 us
    ppermute x3, waiting for transfers between devices, body(): lax.ppermute(scaled[k], 'segment', [(i, i - i % DEPTH + (i + k) % DEPTH)...  5.06 us
    all_to_all x1, waiting for transfers between devices, body(): lax.all_to_all(near(shared), 'dp', 0, 0, axis_index_groups=cores)  4.8 us
    ppermute x4, starting transfers between devices, swap(): return near(lax.ppermute(value, 'dp', sibling))  4.54 us
    pallas_call x1, Pallas kernels, middle(): pl.pallas_call(middle_kernel, out_shape=(MAP, jax.ShapeDtypeStruct((DEPTH...  4.45 us
  transfers between devices with their start and end apart: 19, of which 13 were waited for; matrix products, arithmetic and copies ran while one was open for 0% of the time, Pallas kernels for 6%

profile of v9, /device:TPU:1, one launch (start us, length us, event | category | flops | bytes accessed | tf_op | source)
XLA Modules:
  0.0 116.5 jit_solution(7532154912822749834)
XLA Ops:
  0.6 0.0 copy-start
  0.6 2.2 %prepare.1 = (bf16[1168,256]{1,0:T(8,128)(2,1)S(1)}, bf16[1168,256]{1,0:T(8,128)(2,1)S(1)}, bf16[592,256]{1,0:T(8,128)(2,1)S(1)}, bf16[16,256]{1,0:T(8,128)(2,1)...) custom-call(f32[4,512]{1,0:T(4,128)} %latent_ref.1, f32[512,256]{1,0:T(8,128)} %bitcast.20, ...), custom_call_target="tpu_custom_call" | custom-call | tf_op jit(solution)/shard_map/prepare/pallas_call | solution.py:135
  2.9 4.5 %collective-permute-start.2 = (bf16[592,256]{1,0:T(8,128)(2,1)S(1)}, bf16[592,256]{1,0:T(8,128)(2,1)S(1)}, u32[]{:S(2)}, u32[]{:S(2)}) collective-permute-start(bf16[592,256]{1,0:T(8,128)(2,1)S(1)} %get-tuple-element.40), channel_id=1, source_target_pairs={{0,32},{16,48},{32,0},{48,16},{64,96},{80,112},{96,64},{112,80},{1... | collective-permute-start | bytes 909320 | tf_op jit(solution)/shard_map/ppermute | solution.py:622
  7.4 0.4 collective-permute-start
  7.8 6.5 %collective-permute-done.2.f0_ref = bf16[592,256]{1,0:T(8,128)(2,1)S(1)} collective-permute-done((bf16[592,256]{1,0:T(8,128)(2,1)S(1)}, bf16[592,256]{1,0:T(8,128)(2,1)S(1)}, u32[]{:S(2)}, u32[]{:S(2)}) %collective-permute-start.2) | collective-permute-done | bytes 303136 | tf_op jit(solution)/shard_map/ppermute | solution.py:622
  14.3 0.7 collective-permute-start.3
  15.0 1.2 %collective-permute-start.5 = (bf16[592,256]{1,0:T(8,128)(2,1)S(1)}, bf16[592,256]{1,0:T(8,128)(2,1)S(1)}, u32[]{:S(2)}, u32[]{:S(2)}) collective-permute-start(bf16[592,256]{1,0:T(8,128)(2,1)S(1)} %collective-permute-done.2.f0_ref), channel_id=1, source_target_pairs={{0,2},{1,3},{2,0},{3,1},{4,6},{5,7},{6,4},{7,5},{8,10},{9,11},{10,... | collective-permute-start | bytes 909320 | tf_op jit(solution)/shard_map/ppermute | solution.py:631
  16.2 11.4 %collective-permute-done.a1_ref = bf16[1168,256]{1,0:T(8,128)(2,1)S(1)} collective-permute-done((bf16[1168,256]{1,0:T(8,128)(2,1)S(1)}, bf16[1168,256]{1,0:T(8,128)(2,1)S(1)}, u32[]{:S(2)}, u32[]{:S(2)}) %collective-permute-start) | collective-permute-done | bytes 598048 | tf_op jit(solution)/shard_map/ppermute | solution.py:622
  27.6 1.5 %collective-permute-start.1 = (bf16[1168,256]{1,0:T(8,128)(2,1)S(1)}, bf16[1168,256]{1,0:T(8,128)(2,1)S(1)}, u32[]{:S(2)}, u32[]{:S(2)}) collective-permute-start(bf16[1168,256]{1,0:T(8,128)(2,1)S(1)} %collective-permute-done.a1_ref), channel_id=1, source_target_pairs={{0,1},{1,0},{2,3},{3,2},{4,5},{5,4},{6,7},{7,6},{8,9},{9,8},{10,11... | collective-permute-start | bytes 1794056 | tf_op jit(solution)/shard_map/ppermute | solution.py:625
  29.1 0.0 collective-permute-done.3.a3_ref
  29.1 2.5 %collective-permute-start.4 = (bf16[1168,256]{1,0:T(8,128)(2,1)S(1)}, bf16[1168,256]{1,0:T(8,128)(2,1)S(1)}, u32[]{:S(2)}, u32[]{:S(2)}) collective-permute-start(bf16[1168,256]{1,0:T(8,128)(2,1)S(1)} %collective-permute-done.3.a3_ref), channel_id=1, source_target_pairs={{0,1},{1,0},{2,3},{3,2},{4,5},{5,4},{6,7},{7,6},{8,9},{9,8},{10,11... | collective-permute-start | bytes 1794056 | tf_op jit(solution)/shard_map/ppermute | solution.py:625
  31.6 0.0 collective-permute-start.6
  31.7 0.0 collective-permute-done.5.f1_ref
  31.7 0.5 collective-permute-start.7
  32.2 1.6 %collective-permute-done.6.f2_ref = bf16[592,256]{1,0:T(8,128)(2,1)S(1)} collective-permute-done((bf16[592,256]{1,0:T(8,128)(2,1)S(1)}, bf16[592,256]{1,0:T(8,128)(2,1)S(1)}, u32[]{:S(2)}, u32[]{:S(2)}) %collective-permute-start.6) | collective-permute-done | bytes 303136 | tf_op jit(solution)/shard_map/ppermute | solution.py:625
  33.7 0.4 collective-permute-done.7.f3_ref
  34.2 0.0 collective-permute-done.1.b1_ref
  34.2 0.0 collective-permute-done.4.b3_ref
  34.2 0.0 copy-done
  34.2 3.3 %first.1 = (bf16[256,256]{1,0:T(8,128)(2,1)S(1)}, bf16[4,2304,256]{2,1,0:T(8,128)(2,1)S(1)}, bf16[4,16,256]{2,1,0:T(8,128)(2,1)S(1)}) custom-call(bf16[4,256,256]{2,1,0:T(8,128)(2,1)} %bitcast.22, bf16[2304,256]{1,0:T(8,128)(2,1)S(1)} %bitcast.15, bf16[16,256]{1,0:T(8,128)(2,1)S(1)} %get-tuple-element.38.tile_ref, ...), custom_call_target="tpu_custom_call" | custom-call | tf_op jit(solution)/shard_map/first/pallas_call | solution.py:316
  37.5 2.8 %collective-permute-start.8 = (bf16[256,256]{1,0:T(8,128)(2,1)S(1)}, bf16[256,256]{1,0:T(8,128)(2,1)S(1)}, u32[]{:S(2)}, u32[]{:S(2)}) collective-permute-start(bf16[256,256]{1,0:T(8,128)(2,1)S(1)} %get-tuple-element.44), channel_id=1, source_target_pairs={{0,64},{16,80},{32,96},{48,112},{64,0},{80,16},{96,32},{112,48},{1... | collective-permute-start | bytes 393224 | tf_op jit(solution)/shard_map/ppermute | solution.py:636
  40.3 0.0 copy-start.1
  40.3 0.0 copy-start.3
  40.3 1.3 %flip.1.flip_ref = bf16[4,2304,256]{2,1,0:T(8,128)(2,1)S(1)} custom-call(bf16[4,2304,256]{2,1,0:T(8,128)(2,1)S(1)} %get-tuple-element.45.w_ref), custom_call_target="tpu_custom_call" | custom-call | tf_op jit(solution)/shard_map/flip/pallas_call | solution.py:333
  41.6 2.2 %collective-permute-done.8.recv_ref = bf16[256,256]{1,0:T(8,128)(2,1)S(1)} collective-permute-done((bf16[256,256]{1,0:T(8,128)(2,1)S(1)}, bf16[256,256]{1,0:T(8,128)(2,1)S(1)}, u32[]{:S(2)}, u32[]{:S(2)}) %collective-permute-start.8) | collective-permute-done | bytes 131104 | tf_op jit(solution)/shard_map/ppermute | solution.py:636
  43.8 0.0 copy-done.1
  43.8 0.0 copy-done.3
  43.8 4.5 %middle.1 = (bf16[256,256]{1,0:T(8,128)(2,1)S(1)}, bf16[4,256,256]{2,1,0:T(8,128)(2,1)S(1)}, f32[4,256,256]{2,1,0:T(8,128)S(1)}, bf16[4,256,256]{2,1,0:T(8,128)(2,1)S(1)}) custom-call(bf16[4,256,256]{2,1,0:T(8,128)(2,1)S(1)} %bitcast.23, bf16[4,256,256]{2,1,0:T(8,128)(2,1)S(1)} %bitcast.18, bf16[256,256]{1,0:T(8,128)(2,1)S(1)} %collective-permute-done.8.recv_ref, ...), custom_call_target="tpu_custom_call" | custom-call | tf_op jit(solution)/shard_map/middle/pallas_call | solution.py:344
  48.3 2.8 %collective-permute-start.9 = (bf16[256,256]{1,0:T(8,128)(2,1)S(1)}, bf16[256,256]{1,0:T(8,128)(2,1)S(1)}, u32[]{:S(2)}, u32[]{:S(2)}) collective-permute-start(bf16[256,256]{1,0:T(8,128)(2,1)S(1)} %get-tuple-element.47), channel_id=1, source_target_pairs={{0,64},{16,80},{32,96},{48,112},{64,0},{80,16},{96,32},{112,48},{1... | collective-permute-start | bytes 393224 | tf_op jit(solution)/shard_map/ppermute | solution.py:638
  51.1 1.5 %collective-permute-start.12 = (bf16[256,256]{1,0:T(8,128)(2,1)S(1)}, bf16[256,256]{1,0:T(8,128)(2,1)S(1)}, u32[]{:S(2)}, u32[]{:S(2)}) collective-permute-start(bf16[256,256]{1,0:T(8,128)(2,1)S(1)} %get-tuple-element.72), channel_id=1, source_target_pairs={{0,48},{16,0},{32,16},{48,32},{64,112},{80,64},{96,80},{112,96},{1... | collective-permute-start | bytes 393224 | tf_op jit(solution)/shard_map/ppermute | solution.py:641
  52.6 0.0 collective-permute-start.11
  52.6 0.7 collective-permute-start.10
  53.3 0.3 collective-permute-done.9.recv_ref
  53.7 0.0 copy-start.4
  53.7 2.6 %last.1 = bf16[4,272,256]{2,1,0:T(8,128)(2,1)S(1)} custom-call(bf16[4,256,256]{2,1,0:T(8,128)(2,1)S(1)} %bitcast.19, bf16[256,256]{1,0:T(8,128)(2,1)S(1)} %collective-permute-done.9.recv_ref, bf16[4,256,256]{2,1,0:T(8,128)(2,1)S(1)} %get-tuple-element.48.xs_ref, f32[4,256,256]{2,1,0:T(8,128)S(1)} %get-tuple-element.49.conv_ref, ...), custom_call_target="tpu_custom_call" | custom-call | tf_op jit(solution)/shard_map/last/pallas_call | solution.py:366
  56.2 0.0 copy-start.2
  56.2 0.0 collective-permute-done.12.s3_ref
  56.2 1.8 %collective-permute-done.11.s2_ref = bf16[256,256]{1,0:T(8,128)(2,1)S(1)} collective-permute-done((bf16[256,256]{1,0:T(8,128)(2,1)S(1)}, bf16[256,256]{1,0:T(8,128)(2,1)S(1)}, u32[]{:S(2)}, u32[]{:S(2)}) %collective-permute-start.11) | collective-permute-done | bytes 131104 | tf_op jit(solution)/shard_map/ppermute | solution.py:641
  58.1 3.2 %collective-permute-done.10.s1_ref = bf16[256,256]{1,0:T(8,128)(2,1)S(1)} collective-permute-done((bf16[256,256]{1,0:T(8,128)(2,1)S(1)}, bf16[256,256]{1,0:T(8,128)(2,1)S(1)}, u32[]{:S(2)}, u32[]{:S(2)}) %collective-permute-start.10) | collective-permute-done | bytes 131104 | tf_op jit(solution)/shard_map/ppermute | solution.py:641
  61.3 0.2 turn.1.flip_ref
  61.5 11.0 %all_to_all.15.r_ref = bf16[4,272,256]{2,1,0:T(8,128)(2,1)S(1)} all-to-all(bf16[4,272,256]{2,1,0:T(8,128)(2,1)S(1)} %last.1), channel_id=1, replica_groups={{0,16,32,48},{64,80,96,112},{1,17,33,49},{65,81,97,113},{2,18,34,50},{6..., dimensions={0} | all-to-all | bytes 1114112 | tf_op jit(solution)/shard_map/all_to_all | solution.py:650
  72.4 0.0 copy-done.4
  72.4 0.0 copy-done.2
  72.5 2.3 %give.1 = (bf16[1168,256]{1,0:T(8,128)(2,1)S(1)}, bf16[16,256]{1,0:T(8,128)(2,1)S(1)}, f32[4,512]{1,0:T(4,128)S(1)}, bf16[4,3,288,256]{3,2,1,0:T(8,128)(2,1)S(1)}, f32[256,256]{1,0:T(8,128)S(1)}) custom-call(bf16[4,272,256]{2,1,0:T(8,128)(2,1)S(1)} %all_to_all.15.r_ref, bf16[256,1024]{1,0:T(8,128)(2,1)S(1)} %turn.1.flip_ref, bf16[2304,256]{1,0:T(8,128)(2,1)S(1)} %bitcast.16, ...), custom_call_target="tpu_custom_call" | custom-call | tf_op jit(solution)/shard_map/give/pallas_call | solution.py:449
  74.8 2.3 %collective-permute-start.13 = (bf16[1168,256]{1,0:T(8,128)(2,1)S(1)}, bf16[1168,256]{1,0:T(8,128)(2,1)S(1)}, u32[]{:S(2)}, u32[]{:S(2)}) collective-permute-start(bf16[1168,256]{1,0:T(8,128)(2,1)S(1)} %get-tuple-element.59), channel_id=1, source_target_pairs={{0,1},{1,0},{2,3},{3,2},{4,5},{5,4},{6,7},{7,6},{8,9},{9,8},{10,11... | collective-permute-start | bytes 1794056 | tf_op jit(solution)/shard_map/ppermute | solution.py:654
  77.1 0.8 keep.1.keep_ref
  77.9 0.8 collective-permute-done.13.got_ref
  78.7 1.0 pair.1
  79.7 4.2 %all-to-all-start.1 = ((bf16[8,176,256]{2,1,0:T(8,128)(2,1)}), bf16[8,176,256]{2,1,0:T(8,128)(2,1)S(1)}, u32[]{:S(2)}, u32[]{:S(2)}) async-start(bf16[8,176,256]{2,1,0:T(8,128)(2,1)} %pair.1), calls=%async_computation.1 | async-start | bytes 1441792 | tf_op jit(solution)/shard_map/all_to_all | solution.py:657
  83.9 0.3 collective-permute-start.14
  84.2 2.2 %collective-permute-done.14 = f32[4,512]{1,0:T(4,128)S(1)} collective-permute-done((f32[4,512]{1,0:T(4,128)S(1)}, f32[4,512]{1,0:T(4,128)S(1)}, u32[]{:S(2)}, u32[]{:S(2)}) %collective-permute-start.14) | collective-permute-done | bytes 8224 | tf_op jit(solution)/shard_map/ppermute | solution.py:658
  86.4 0.8 collective-permute-start.15
  87.2 3.2 %collective-permute-done.15 = f32[4,512]{1,0:T(4,128)S(1)} collective-permute-done((f32[4,512]{1,0:T(4,128)S(1)}, f32[4,512]{1,0:T(4,128)S(1)}, u32[]{:S(2)}, u32[]{:S(2)}) %collective-permute-start.15) | collective-permute-done | bytes 8224 | tf_op jit(solution)/shard_map/ppermute | solution.py:659
  90.4 4.8 %all-to-all-done.1.shares_ref = bf16[8,176,256]{2,1,0:T(8,128)(2,1)S(1)} async-done(((bf16[8,176,256]{2,1,0:T(8,128)(2,1)}), bf16[8,176,256]{2,1,0:T(8,128)(2,1)S(1)}, u32[]{:S(2)}, u32[]{:S(2)}) %all-to-all-start.1) | async-done | bytes 720928 | tf_op jit(solution)/shard_map/all_to_all | solution.py:657
  95.2 0.1 share.1
  95.3 13.3 %all_to_all.16.value_ref = bf16[8,144,256]{2,1,0:T(8,128)(2,1)S(1)} all-to-all(bf16[8,144,256]{2,1,0:T(8,128)(2,1)S(1)} %share.1), channel_id=1, replica_groups={{0,2,4,6,8,10,12,14},{1,3,5,7,9,11,13,15},{16,18,20,22,24,26,28,30},{17..., dimensions={0} | all-to-all | bytes 1179648 | tf_op jit(solution)/shard_map/all_to_all | solution.py:661
  108.6 2.1 %collective-permute-start.16 = (bf16[8,144,256]{2,1,0:T(8,128)(2,1)S(1)}, bf16[8,144,256]{2,1,0:T(8,128)(2,1)S(1)}, u32[]{:S(2)}, u32[]{:S(2)}) collective-permute-start(bf16[8,144,256]{2,1,0:T(8,128)(2,1)S(1)} %all_to_all.16.value_ref), channel_id=1, source_target_pairs={{0,1},{1,0},{2,3},{3,2},{4,5},{5,4},{6,7},{7,6},{8,9},{9,8},{10,11... | collective-permute-start | bytes 1769480 | tf_op jit(solution)/shard_map/ppermute | solution.py:662
  110.7 1.8 %collective-permute-start.17 = (f32[4,512]{1,0:T(4,128)S(1)}, f32[4,512]{1,0:T(4,128)S(1)}, u32[]{:S(2)}, u32[]{:S(2)}) collective-permute-start(f32[4,512]{1,0:T(4,128)S(1)} %add.7.part_ref), channel_id=1, source_target_pairs={{0,64},{16,80},{32,96},{48,112},{64,0},{80,16},{96,32},{112,48},{1... | collective-permute-start | bytes 24584 | tf_op jit(solution)/shard_map/ppermute | solution.py:664
  112.5 1.1 affine.1
  113.6 1.1 own.1.target_any
  114.6 0.1 collective-permute-done.17.moved_ref
  114.7 0.0 collective-permute-done.16.value_ref
  114.7 1.7 %rest.1 = (f32[9,256,256]{2,1,0:T(8,128)}, f32[4,512]{1,0:T(4,128)}) custom-call(bf16[8,144,256]{2,1,0:T(8,128)(2,1)S(1)} %collective-permute-done.16.value_ref, f32[9,256,256]{2,1,0:T(8,128)} %own.1.target_any, f32[4,512]{1,0:T(4,128)S(1)} %add.7.part_ref, f32[4,512]{1,0:T(4,128)S(1)} %collective-permute-done.17.moved_ref), custom_call_target="tpu_custom_call", output_to_operand_aliasing={{0}: (1, {})} | custom-call | tf_op jit(solution)/shard_map/rest/pallas_call | solution.py:595
  (3 shorter events, 0.0 us)
Async XLA Ops:
  0.6 33.5 %copy-start = (bf16[1,3,3,256,256]{4,3,2,1,0:T(8,128)(2,1)S(1)}, bf16[1,3,3,256,256]{4,3,2,1,0:T(8,128)(2,1)}, u32[]{:S(2)}) copy-start(bf16[1,3,3,256,256]{4,3,2,1,0:T(8,128)(2,1)} %param.8) | copy-start | bytes 3538948
  2.9 11.4 %collective-permute-start.2 = (bf16[592,256]{1,0:T(8,128)(2,1)S(1)}, bf16[592,256]{1,0:T(8,128)(2,1)S(1)}, u32[]{:S(2)}, u32[]{:S(2)}) collective-permute-start(bf16[592,256]{1,0:T(8,128)(2,1)S(1)} %get-tuple-element.40), channel_id=1, source_target_pairs={{0,32},{16,48},{32,0},{48,16},{64,96},{80,112},{96,64},{112,80},{1... | collective-permute-start | bytes 909320 | tf_op jit(solution)/shard_map/ppermute | solution.py:622
  7.4 20.2 %collective-permute-start = (bf16[1168,256]{1,0:T(8,128)(2,1)S(1)}, bf16[1168,256]{1,0:T(8,128)(2,1)S(1)}, u32[]{:S(2)}, u32[]{:S(2)}) collective-permute-start(bf16[1168,256]{1,0:T(8,128)(2,1)S(1)} %get-tuple-element.39), channel_id=1, source_target_pairs={{0,48},{16,0},{32,16},{48,32},{64,112},{80,64},{96,80},{112,96},{1... | collective-permute-start | bytes 1794056 | tf_op jit(solution)/shard_map/ppermute | solution.py:622
  14.3 14.8 %collective-permute-start.3 = (bf16[1168,256]{1,0:T(8,128)(2,1)S(1)}, bf16[1168,256]{1,0:T(8,128)(2,1)S(1)}, u32[]{:S(2)}, u32[]{:S(2)}) collective-permute-start(bf16[1168,256]{1,0:T(8,128)(2,1)S(1)} %get-tuple-element.42), channel_id=1, source_target_pairs={{0,16},{16,32},{32,48},{48,0},{64,80},{80,96},{96,112},{112,64},{1... | collective-permute-start | bytes 1794056 | tf_op jit(solution)/shard_map/ppermute | solution.py:622
  15.0 16.6 %collective-permute-start.5 = (bf16[592,256]{1,0:T(8,128)(2,1)S(1)}, bf16[592,256]{1,0:T(8,128)(2,1)S(1)}, u32[]{:S(2)}, u32[]{:S(2)}) collective-permute-start(bf16[592,256]{1,0:T(8,128)(2,1)S(1)} %collective-permute-done.2.f0_ref), channel_id=1, source_target_pairs={{0,2},{1,3},{2,0},{3,1},{4,6},{5,7},{6,4},{7,5},{8,10},{9,11},{10,... | collective-permute-start | bytes 909320 | tf_op jit(solution)/shard_map/ppermute | solution.py:631
  27.6 6.5 %collective-permute-start.1 = (bf16[1168,256]{1,0:T(8,128)(2,1)S(1)}, bf16[1168,256]{1,0:T(8,128)(2,1)S(1)}, u32[]{:S(2)}, u32[]{:S(2)}) collective-permute-start(bf16[1168,256]{1,0:T(8,128)(2,1)S(1)} %collective-permute-done.a1_ref), channel_id=1, source_target_pairs={{0,1},{1,0},{2,3},{3,2},{4,5},{5,4},{6,7},{7,6},{8,9},{9,8},{10,11... | collective-permute-start | bytes 1794056 | tf_op jit(solution)/shard_map/ppermute | solution.py:625
  29.1 5.0 %collective-permute-start.4 = (bf16[1168,256]{1,0:T(8,128)(2,1)S(1)}, bf16[1168,256]{1,0:T(8,128)(2,1)S(1)}, u32[]{:S(2)}, u32[]{:S(2)}) collective-permute-start(bf16[1168,256]{1,0:T(8,128)(2,1)S(1)} %collective-permute-done.3.a3_ref), channel_id=1, source_target_pairs={{0,1},{1,0},{2,3},{3,2},{4,5},{5,4},{6,7},{7,6},{8,9},{9,8},{10,11... | collective-permute-start | bytes 1794056 | tf_op jit(solution)/shard_map/ppermute | solution.py:625
  31.6 2.1 %collective-permute-start.6 = (bf16[592,256]{1,0:T(8,128)(2,1)S(1)}, bf16[592,256]{1,0:T(8,128)(2,1)S(1)}, u32[]{:S(2)}, u32[]{:S(2)}) collective-permute-start(bf16[592,256]{1,0:T(8,128)(2,1)S(1)} %collective-permute-done.2.f0_ref), channel_id=1, source_target_pairs={{0,1},{1,0},{2,3},{3,2},{4,5},{5,4},{6,7},{7,6},{8,9},{9,8},{10,11... | collective-permute-start | bytes 909320 | tf_op jit(solution)/shard_map/ppermute | solution.py:625
  31.7 2.5 %collective-permute-start.7 = (bf16[592,256]{1,0:T(8,128)(2,1)S(1)}, bf16[592,256]{1,0:T(8,128)(2,1)S(1)}, u32[]{:S(2)}, u32[]{:S(2)}) collective-permute-start(bf16[592,256]{1,0:T(8,128)(2,1)S(1)} %collective-permute-done.5.f1_ref), channel_id=1, source_target_pairs={{0,1},{1,0},{2,3},{3,2},{4,5},{5,4},{6,7},{7,6},{8,9},{9,8},{10,11... | collective-permute-start | bytes 909320 | tf_op jit(solution)/shard_map/ppermute | solution.py:625
  37.5 6.3 %collective-permute-start.8 = (bf16[256,256]{1,0:T(8,128)(2,1)S(1)}, bf16[256,256]{1,0:T(8,128)(2,1)S(1)}, u32[]{:S(2)}, u32[]{:S(2)}) collective-permute-start(bf16[256,256]{1,0:T(8,128)(2,1)S(1)} %get-tuple-element.44), channel_id=1, source_target_pairs={{0,64},{16,80},{32,96},{48,112},{64,0},{80,16},{96,32},{112,48},{1... | collective-permute-start | bytes 393224 | tf_op jit(solution)/shard_map/ppermute | solution.py:636
  40.3 3.5 %copy-start.1 = (bf16[4,16,16,256]{3,2,1,0:T(8,128)(2,1)S(1)}, bf16[4,16,16,256]{3,2,1,0:T(8,128)(2,1)}, u32[]{:S(2)}) copy-start(bf16[4,16,16,256]{3,2,1,0:T(8,128)(2,1)} %param.11) | copy-start | bytes 1572868
  40.3 3.5 %copy-start.3 = (bf16[4,16,16,256]{3,2,1,0:T(8,128)(2,1)S(1)}, bf16[4,16,16,256]{3,2,1,0:T(8,128)(2,1)}, u32[]{:S(2)}) copy-start(bf16[4,16,16,256]{3,2,1,0:T(8,128)(2,1)} %param.6) | copy-start | bytes 1572868
  48.3 5.4 %collective-permute-start.9 = (bf16[256,256]{1,0:T(8,128)(2,1)S(1)}, bf16[256,256]{1,0:T(8,128)(2,1)S(1)}, u32[]{:S(2)}, u32[]{:S(2)}) collective-permute-start(bf16[256,256]{1,0:T(8,128)(2,1)S(1)} %get-tuple-element.47), channel_id=1, source_target_pairs={{0,64},{16,80},{32,96},{48,112},{64,0},{80,16},{96,32},{112,48},{1... | collective-permute-start | bytes 393224 | tf_op jit(solution)/shard_map/ppermute | solution.py:638
  51.1 5.1 %collective-permute-start.12 = (bf16[256,256]{1,0:T(8,128)(2,1)S(1)}, bf16[256,256]{1,0:T(8,128)(2,1)S(1)}, u32[]{:S(2)}, u32[]{:S(2)}) collective-permute-start(bf16[256,256]{1,0:T(8,128)(2,1)S(1)} %get-tuple-element.72), channel_id=1, source_target_pairs={{0,48},{16,0},{32,16},{48,32},{64,112},{80,64},{96,80},{112,96},{1... | collective-permute-start | bytes 393224 | tf_op jit(solution)/shard_map/ppermute | solution.py:641
  52.6 5.4 %collective-permute-start.11 = (bf16[256,256]{1,0:T(8,128)(2,1)S(1)}, bf16[256,256]{1,0:T(8,128)(2,1)S(1)}, u32[]{:S(2)}, u32[]{:S(2)}) collective-permute-start(bf16[256,256]{1,0:T(8,128)(2,1)S(1)} %get-tuple-element.73), channel_id=1, source_target_pairs={{0,32},{16,48},{32,0},{48,16},{64,96},{80,112},{96,64},{112,80},{1... | collective-permute-start | bytes 393224 | tf_op jit(solution)/shard_map/ppermute | solution.py:641
  52.6 8.6 %collective-permute-start.10 = (bf16[256,256]{1,0:T(8,128)(2,1)S(1)}, bf16[256,256]{1,0:T(8,128)(2,1)S(1)}, u32[]{:S(2)}, u32[]{:S(2)}) collective-permute-start(bf16[256,256]{1,0:T(8,128)(2,1)S(1)} %get-tuple-element.74), channel_id=1, source_target_pairs={{0,16},{16,32},{32,48},{48,0},{64,80},{80,96},{96,112},{112,64},{1... | collective-permute-start | bytes 393224 | tf_op jit(solution)/shard_map/ppermute | solution.py:641
  53.7 18.8 %copy-start.4 = (f32[4,512]{1,0:T(4,128)S(1)}, f32[4,512]{1,0:T(4,128)}, u32[]{:S(2)}) copy-start(f32[4,512]{1,0:T(4,128)} %latent_ref.1) | copy-start | bytes 24580
  56.2 16.2 %copy-start.2 = (f32[1,512,256]{2,1,0:T(8,128)S(1)}, f32[1,512,256]{2,1,0:T(8,128)}, u32[]{:S(2)}) copy-start(f32[1,512,256]{2,1,0:T(8,128)} %param.9) | copy-start | bytes 1572868
  74.8 3.9 %collective-permute-start.13 = (bf16[1168,256]{1,0:T(8,128)(2,1)S(1)}, bf16[1168,256]{1,0:T(8,128)(2,1)S(1)}, u32[]{:S(2)}, u32[]{:S(2)}) collective-permute-start(bf16[1168,256]{1,0:T(8,128)(2,1)S(1)} %get-tuple-element.59), channel_id=1, source_target_pairs={{0,1},{1,0},{2,3},{3,2},{4,5},{5,4},{6,7},{7,6},{8,9},{9,8},{10,11... | collective-permute-start | bytes 1794056 | tf_op jit(solution)/shard_map/ppermute | solution.py:654
  79.7 15.5 %all-to-all-start.1 = ((bf16[8,176,256]{2,1,0:T(8,128)(2,1)}), bf16[8,176,256]{2,1,0:T(8,128)(2,1)S(1)}, u32[]{:S(2)}, u32[]{:S(2)}) async-start(bf16[8,176,256]{2,1,0:T(8,128)(2,1)} %pair.1), calls=%async_computation.1 | async-start | bytes 1441792 | tf_op jit(solution)/shard_map/all_to_all | solution.py:657
  83.9 2.5 %collective-permute-start.14 = (f32[4,512]{1,0:T(4,128)S(1)}, f32[4,512]{1,0:T(4,128)S(1)}, u32[]{:S(2)}, u32[]{:S(2)}) collective-permute-start(f32[4,512]{1,0:T(4,128)S(1)} %get-tuple-element.62), channel_id=1, source_target_pairs={{0,16},{16,0},{32,48},{48,32},{64,80},{80,64},{96,112},{112,96},{1... | collective-permute-start | bytes 24584 | tf_op jit(solution)/shard_map/ppermute | solution.py:658
  86.4 4.0 %collective-permute-start.15 = (f32[4,512]{1,0:T(4,128)S(1)}, f32[4,512]{1,0:T(4,128)S(1)}, u32[]{:S(2)}, u32[]{:S(2)}) collective-permute-start(f32[4,512]{1,0:T(4,128)S(1)} %add.6), channel_id=1, source_target_pairs={{0,32},{16,48},{32,0},{48,16},{64,96},{80,112},{96,64},{112,80},{1... | collective-permute-start | bytes 24584 | tf_op jit(solution)/shard_map/ppermute | solution.py:659
  108.6 6.1 %collective-permute-start.16 = (bf16[8,144,256]{2,1,0:T(8,128)(2,1)S(1)}, bf16[8,144,256]{2,1,0:T(8,128)(2,1)S(1)}, u32[]{:S(2)}, u32[]{:S(2)}) collective-permute-start(bf16[8,144,256]{2,1,0:T(8,128)(2,1)S(1)} %all_to_all.16.value_ref), channel_id=1, source_target_pairs={{0,1},{1,0},{2,3},{3,2},{4,5},{5,4},{6,7},{7,6},{8,9},{9,8},{10,11... | collective-permute-start | bytes 1769480 | tf_op jit(solution)/shard_map/ppermute | solution.py:662
  110.7 4.0 %collective-permute-start.17 = (f32[4,512]{1,0:T(4,128)S(1)}, f32[4,512]{1,0:T(4,128)S(1)}, u32[]{:S(2)}, u32[]{:S(2)}) collective-permute-start(f32[4,512]{1,0:T(4,128)S(1)} %add.7.part_ref), channel_id=1, source_target_pairs={{0,64},{16,80},{32,96},{48,112},{64,0},{80,16},{96,32},{112,48},{1... | collective-permute-start | bytes 24584 | tf_op jit(solution)/shard_map/ppermute | solution.py:664
